TPU v7x, 32 devices: a whole 2x2x4 slice. The times are simulated.
32 devices in a mesh: wide: 8 (over z, y), narrow: 4 (over x, core).
Axes of the slice: x: 2, y: 2, z: 4, core: 2. Of those that a mesh axis runs over, the one named last changes fastest.
Arguments:
- tokens: bfloat16 [32, 680, 1024], P(('wide', 'narrow')), may hold values from -6 to 6
- labels: int32 [32], P(('wide', 'narrow')), may hold values from 0 to 1000
- stop_scale: int32 [32], P(('wide', 'narrow')), may hold values from 6 to 10
- class_table: bfloat16 [1001, 1024], P(None, ('wide', 'narrow')), may hold values from -6 to 6
- ada_weight: bfloat16 [1024, 6144], P(('wide', 'narrow')), may hold values from -0.1875 to 0.1875
- ada_bias: bfloat16 [6144], P(('wide', 'narrow')), may hold values from -3 to 3
- qkv_weight: bfloat16 [1024, 3072], P(('wide', 'narrow')), may hold values from -0.1875 to 0.1875
- head_scale: float32 [16], replicated, may hold values from 2.1 to 3.1
- out_weight: bfloat16 [1024, 1024], P(('wide', 'narrow')), may hold values from -0.75 to 0.75
- up_weight: bfloat16 [1024, 4096], P(('wide', 'narrow')), may hold values from -0.1875 to 0.1875
- up_bias: bfloat16 [4096], P(('wide', 'narrow')), may hold values from -3 to 3
- down_weight: bfloat16 [4096, 1024], P(('wide', 'narrow')), may hold values from -0.09375 to 0.09375
- cotangent: bfloat16 [32, 680, 1024], P(('wide', 'narrow')), may hold values from -6 to 6
Outputs:
- block_out: bfloat16 [32, 680, 1024], P(('wide', 'narrow'))
- input_grad: float32 [32, 680, 1024], P(('wide', 'narrow'))
- class_table_grad: float32 [1001, 1024], P(None, ('wide', 'narrow'))
- ada_weight_grad: float32 [1024, 6144], P(('wide', 'narrow'))
- ada_bias_grad: float32 [6144], P(('wide', 'narrow'))
- qkv_weight_grad: float32 [1024, 3072], P(('wide', 'narrow'))
- head_scale_grad: float32 [16], replicated
- out_weight_grad: float32 [1024, 1024], P(('wide', 'narrow'))
- up_weight_grad: float32 [1024, 4096], P(('wide', 'narrow'))
- up_bias_grad: float32 [4096], P(('wide', 'narrow'))
- down_weight_grad: float32 [4096, 1024], P(('wide', 'narrow'))
Inputs may be any that keep to these rules, and one draw needn't show every extreme that they name: `labels`: class index of each image. Each image keeps its first stop_scale scales; its later positions are padding.
All inputs are finite; a program needn't handle non-finite values.
Results may differ from a plain program's by a relative error of at most 0.023.
Values may be sent and summed in bfloat16 or wider, within the bound.
No kernel may reach another device: no remote copies, remote signals or barrier semaphores. Data moves between devices by JAX's collectives and lax.ppermute only.
A program may use at most 320 MiB of HBM per device.

v0:
```python
from functools import partial

import jax
import jax.numpy as jnp
import numpy as np
from jax import lax
from jax.sharding import PartitionSpec as P

HDIM = 64
SCALES = 10


scale_sides = (1, 2, 3, 4, 5, 6, 8, 10, 13, 16)
head_block = 4


def position_scale(scale_count):
    return np.concatenate(
        [
            np.full(side_size * side_size, level_index, dtype=np.int32)
            for level_index, side_size in enumerate(scale_sides[:scale_count])
        ]
    )


def normalized(inputs):
    centred = inputs - jnp.mean(inputs, axis=-1, keepdims=True)
    return centred * lax.rsqrt(jnp.mean(centred * centred, axis=-1, keepdims=True) + 1e-06)


def modulate(inputs, scale_vec, shift_vec):
    return normalized(inputs) * (1.0 + scale_vec[:, None, :]) + shift_vec[:, None, :]


def unit_rows(inputs):
    return inputs * lax.rsqrt(jnp.sum(inputs * inputs, axis=-1, keepdims=True) + 1e-06)


def gelu_tanh(inputs):
    return jax.nn.gelu(inputs, approximate=True)


def split_heads(matrix, image_count, seq_len):
    blocks = matrix.reshape(image_count, seq_len, -1, head_block, HDIM)
    return jnp.moveaxis(blocks, 2, 1).reshape(-1, seq_len, head_block, HDIM)


def join_heads(blocks, image_count, seq_len):
    shaped = blocks.reshape(image_count, -1, seq_len, head_block, HDIM)
    return jnp.moveaxis(shaped, 1, 2).reshape(image_count * seq_len, -1)


def masked_scores(query_block, key_block, allowed):
    scores = jnp.einsum("qhc,khc->hqk", query_block, key_block, preferred_element_type=jnp.float32)
    return jnp.where(allowed[None], scores, -1e30)


def attend_forward(pieces, allowed):
    query_block, key_block, value_block = pieces
    scores = masked_scores(query_block, key_block, allowed)
    row_peak = jnp.max(scores, axis=-1, keepdims=True)
    log_total = row_peak + jnp.log(jnp.sum(jnp.exp(scores - row_peak), axis=-1, keepdims=True))
    probs_low = jnp.exp(scores - log_total).astype(jnp.bfloat16)
    attended = jnp.einsum(
        "hqk,khc->qhc", probs_low, value_block, preferred_element_type=jnp.float32
    )
    return (attended, log_total)


def attend_backward(pieces, allowed):
    query_block, key_block, value_block, grad_block, log_total = pieces
    scores = masked_scores(query_block, key_block, allowed)
    probs = jnp.exp(scores - log_total)
    probs_low = probs.astype(jnp.bfloat16)
    grad_probs = jnp.einsum(
        "qhc,khc->hqk", grad_block, value_block, preferred_element_type=jnp.float32
    )
    row_inner = jnp.sum(probs * grad_probs, axis=-1, keepdims=True)
    grad_scores = (probs * (grad_probs - row_inner)).astype(jnp.bfloat16)
    grad_values = jnp.einsum(
        "hqk,qhc->khc", probs_low, grad_block, preferred_element_type=jnp.float32
    )
    grad_queries = jnp.einsum(
        "hqk,khc->qhc", grad_scores, key_block, preferred_element_type=jnp.float32
    )
    grad_keys = jnp.einsum(
        "hqk,qhc->khc", grad_scores, query_block, preferred_element_type=jnp.float32
    )
    return (grad_queries, grad_keys, grad_values)


def per_device(
    tokens,
    labels,
    stop_scale,
    class_table,
    ada_weight,
    ada_bias,
    qkv_weight,
    head_scale,
    out_weight,
    up_weight,
    up_bias,
    down_weight,
    cotangent,
):
    image_count, seq_len, model_width = tokens.shape
    row_count = image_count * seq_len
    levels = position_scale(SCALES)
    allowed = jnp.asarray(levels[None, :] <= levels[:, None])
    live_mask = (jnp.asarray(levels)[None, :] < stop_scale[:, None]).astype(jnp.float32)[:, :, None]
    class_count = class_table.shape[0]
    ada_full, ada_bias_full, qkv_full, out_full = (
        lax.all_gather(ada_weight, ("wide", "narrow"), axis=0, tiled=True),
        lax.all_gather(ada_bias, ("wide", "narrow"), axis=0, tiled=True),
        lax.all_gather(qkv_weight, ("wide", "narrow"), axis=0, tiled=True),
        lax.all_gather(out_weight, ("wide", "narrow"), axis=0, tiled=True),
    )
    table_full = lax.all_gather(class_table, ("wide", "narrow"), axis=1, tiled=True)
    onehot = labels[:, None] == jnp.arange(class_count, dtype=jnp.int32)[None, :]
    condition = jnp.dot(onehot.astype(jnp.bfloat16), table_full, preferred_element_type=jnp.float32)
    cond_act = jax.nn.silu(condition).astype(jnp.bfloat16)
    modulation = jnp.dot(
        cond_act, ada_full, preferred_element_type=jnp.float32
    ) + ada_bias_full.astype(jnp.float32)
    gate_one, gate_two, scale_one, scale_two, shift_one, shift_two = jnp.split(
        modulation, 6, axis=-1
    )
    inputs = tokens.astype(jnp.float32)
    attn_in = (
        modulate(inputs, scale_one, shift_one).astype(jnp.bfloat16).reshape(row_count, model_width)
    )
    qkv_rows = jnp.dot(attn_in, qkv_full, preferred_element_type=jnp.float32)
    query_raw, key_raw, value_raw = jnp.split(qkv_rows, 3, axis=-1)

    def scaled_query(query_input, log_scale):
        return unit_rows(query_input.reshape(row_count, -1, HDIM)) * jnp.exp(log_scale)[:, None]

    def key_unit_rows(key_input):
        return unit_rows(key_input.reshape(row_count, -1, HDIM))

    query_low = (
        scaled_query(query_raw, head_scale).astype(jnp.bfloat16).reshape(row_count, model_width)
    )
    key_low = key_unit_rows(key_raw).astype(jnp.bfloat16).reshape(row_count, model_width)
    value_low = value_raw.astype(jnp.bfloat16)
    head_pieces = (
        split_heads(query_low, image_count, seq_len),
        split_heads(key_low, image_count, seq_len),
        split_heads(value_low, image_count, seq_len),
    )
    attended_blocks, log_totals = lax.map(partial(attend_forward, allowed=allowed), head_pieces)
    attended = join_heads(attended_blocks, image_count, seq_len).astype(jnp.bfloat16)
    projected = jnp.dot(attended, out_full, preferred_element_type=jnp.float32).reshape(
        image_count, seq_len, model_width
    )
    residual = inputs + gate_one[:, None, :] * projected
    up_full, up_bias_full, down_full = (
        lax.all_gather(up_weight, ("wide", "narrow"), axis=0, tiled=True),
        lax.all_gather(up_bias, ("wide", "narrow"), axis=0, tiled=True),
        lax.all_gather(down_weight, ("wide", "narrow"), axis=0, tiled=True),
    )
    mlp_in = (
        modulate(residual, scale_two, shift_two)
        .astype(jnp.bfloat16)
        .reshape(row_count, model_width)
    )
    hidden = jnp.dot(mlp_in, up_full, preferred_element_type=jnp.float32) + up_bias_full.astype(
        jnp.float32
    )
    activated = gelu_tanh(hidden).astype(jnp.bfloat16)
    mlp_out = jnp.dot(activated, down_full, preferred_element_type=jnp.float32).reshape(
        image_count, seq_len, model_width
    )
    block_out = ((residual + gate_two[:, None, :] * mlp_out) * live_mask).astype(jnp.bfloat16)
    up_back, down_back = (
        lax.all_gather(up_weight, ("wide", "narrow"), axis=0, tiled=True),
        lax.all_gather(down_weight, ("wide", "narrow"), axis=0, tiled=True),
    )
    qkv_back, out_back = (
        lax.all_gather(qkv_weight, ("wide", "narrow"), axis=0, tiled=True),
        lax.all_gather(out_weight, ("wide", "narrow"), axis=0, tiled=True),
    )
    grad_out = cotangent.astype(jnp.float32) * live_mask
    gate_two_grad = jnp.sum(grad_out * mlp_out, axis=1)
    grad_mlp = (
        (gate_two[:, None, :] * grad_out).astype(jnp.bfloat16).reshape(row_count, model_width)
    )
    down_grad = jnp.einsum("rf,rd->fd", activated, grad_mlp, preferred_element_type=jnp.float32)
    grad_act = jnp.einsum("rd,fd->rf", grad_mlp, down_back, preferred_element_type=jnp.float32)
    gelu_back = jax.vjp(gelu_tanh, hidden)[1]
    grad_hidden = gelu_back(grad_act)[0].astype(jnp.bfloat16)
    up_bias_grad = jnp.sum(grad_hidden.astype(jnp.float32), axis=0)
    up_grad = jnp.einsum("rd,rf->df", mlp_in, grad_hidden, preferred_element_type=jnp.float32)
    up_grad_own, up_bias_own, down_grad_own = (
        lax.psum_scatter(up_grad, ("wide", "narrow"), scatter_dimension=0, tiled=True),
        lax.psum_scatter(up_bias_grad, ("wide", "narrow"), scatter_dimension=0, tiled=True),
        lax.psum_scatter(down_grad, ("wide", "narrow"), scatter_dimension=0, tiled=True),
    )
    grad_mlp_in = jnp.einsum(
        "rf,df->rd", grad_hidden, up_back, preferred_element_type=jnp.float32
    ).reshape(image_count, seq_len, model_width)
    second_back = jax.vjp(modulate, residual, scale_two, shift_two)[1]
    grad_resid_part, scale_two_grad, shift_two_grad = second_back(grad_mlp_in)
    grad_resid = grad_out + grad_resid_part
    gate_one_grad = jnp.sum(grad_resid * projected, axis=1)
    grad_proj = (
        (gate_one[:, None, :] * grad_resid).astype(jnp.bfloat16).reshape(row_count, model_width)
    )
    out_grad = jnp.einsum("rd,re->de", attended, grad_proj, preferred_element_type=jnp.float32)
    grad_attended = jnp.einsum(
        "re,de->rd", grad_proj, out_back, preferred_element_type=jnp.float32
    ).astype(jnp.bfloat16)
    grad_blocks = lax.map(
        partial(attend_backward, allowed=allowed),
        head_pieces + (split_heads(grad_attended, image_count, seq_len), log_totals),
    )
    grad_query_scaled = join_heads(grad_blocks[0], image_count, seq_len)
    grad_key_unit = join_heads(grad_blocks[1], image_count, seq_len)
    grad_values = join_heads(grad_blocks[2], image_count, seq_len)
    query_back = jax.vjp(scaled_query, query_raw, head_scale)[1]
    grad_query_raw, head_scale_part = query_back(grad_query_scaled.reshape(row_count, -1, HDIM))
    key_back = jax.vjp(key_unit_rows, key_raw)[1]
    grad_key_raw = key_back(grad_key_unit.reshape(row_count, -1, HDIM))[0]
    grad_qkv = jnp.concatenate([grad_query_raw, grad_key_raw, grad_values], axis=-1).astype(
        jnp.bfloat16
    )
    qkv_grad = jnp.einsum("rd,re->de", attn_in, grad_qkv, preferred_element_type=jnp.float32)
    grad_attn_in = jnp.einsum(
        "re,de->rd", grad_qkv, qkv_back, preferred_element_type=jnp.float32
    ).reshape(image_count, seq_len, model_width)
    first_back = jax.vjp(modulate, inputs, scale_one, shift_one)[1]
    grad_token_part, scale_one_grad, shift_one_grad = first_back(grad_attn_in)
    input_grad = grad_resid + grad_token_part
    grad_modul = jnp.concatenate(
        [
            gate_one_grad,
            gate_two_grad,
            scale_one_grad,
            scale_two_grad,
            shift_one_grad,
            shift_two_grad,
        ],
        axis=-1,
    ).astype(jnp.bfloat16)
    ada_bias_grad = jnp.sum(grad_modul.astype(jnp.float32), axis=0)
    ada_grad = jnp.einsum("id,ie->de", cond_act, grad_modul, preferred_element_type=jnp.float32)
    grad_cond_act = jnp.einsum(
        "ie,de->id", grad_modul, ada_full, preferred_element_type=jnp.float32
    )
    grad_condition = jax.vjp(jax.nn.silu, condition)[1](grad_cond_act)[0]
    table_grad = jnp.einsum(
        "ic,id->cd", onehot.astype(jnp.float32), grad_condition, precision=lax.Precision.HIGHEST
    )
    ada_own, ada_bias_own, qkv_own, out_own = (
        lax.psum_scatter(ada_grad, ("wide", "narrow"), scatter_dimension=0, tiled=True),
        lax.psum_scatter(ada_bias_grad, ("wide", "narrow"), scatter_dimension=0, tiled=True),
        lax.psum_scatter(qkv_grad, ("wide", "narrow"), scatter_dimension=0, tiled=True),
        lax.psum_scatter(out_grad, ("wide", "narrow"), scatter_dimension=0, tiled=True),
    )
    table_own = lax.psum_scatter(table_grad, ("wide", "narrow"), scatter_dimension=1, tiled=True)
    head_scale_grad = lax.psum(head_scale_part, ("wide", "narrow"))
    return (
        block_out,
        input_grad,
        table_own,
        ada_own,
        ada_bias_own,
        qkv_own,
        head_scale_grad,
        out_own,
        up_grad_own,
        up_bias_own,
        down_grad_own,
    )


def solution(mesh):
    in_specs = (
        P(("wide", "narrow"), None, None),
        P(("wide", "narrow")),
        P(("wide", "narrow")),
        P(None, ("wide", "narrow")),
        P(("wide", "narrow"), None),
        P(("wide", "narrow")),
        P(("wide", "narrow"), None),
        P(),
        P(("wide", "narrow"), None),
        P(("wide", "narrow"), None),
        P(("wide", "narrow")),
        P(("wide", "narrow"), None),
        P(("wide", "narrow"), None, None),
    )
    out_specs = (
        P(("wide", "narrow"), None, None),
        P(("wide", "narrow"), None, None),
        P(None, ("wide", "narrow")),
        P(("wide", "narrow"), None),
        P(("wide", "narrow")),
        P(("wide", "narrow"), None),
        P(),
        P(("wide", "narrow"), None),
        P(("wide", "narrow"), None),
        P(("wide", "narrow")),
        P(("wide", "narrow"), None),
    )
    return jax.shard_map(
        per_device, mesh=mesh, in_specs=in_specs, out_specs=out_specs, check_vma=False
    )
```

profile of v0, /device:TPU:0, one launch (start us, length us, event | category | flops | bytes accessed | tf_op | source)
XLA Modules:
  0.0 1722.3 jit_solution(7312376964460585602)
XLA Ops:
  17.4 43.1 %all-gather = bf16[32,1,128]{2,1,0:T(2,128)(2,1)S(1)} all-gather(bf16[1,1,128]{2,1,0:T(2,128)(2,1)S(1)} %bitcast.321), channel_id=1, replica_groups=mesh['wide'=8,'narrow'=4] {'wide','narrow'}, dimensions={0}, use_global_device_ids=true | all-gather | bytes 8448 | tf_op jit(solution)/shard_map/all_gather | solution.py:160
  62.0 37.8 %all-reduce = bf16[6144]{0:T(1024)(128)(2,1)S(1)} all-reduce(bf16[6144]{0:T(1024)(128)(2,1)S(1)} %dynamic-update-slice), channel_id=1, replica_groups=mesh['wide'=8,'narrow'=4] {'wide','narrow'}, use_global_device_ids=true, to_apply=%add | all-reduce | flops 6144 | bytes 24576
  104.7 63.1 %all-gather.10.cloned.1.call-done = bf16[1024,6144]{1,0:T(8,128)(2,1)} async-done(((bf16[32,6144]{1,0:T(8,128)(2,1)}), bf16[1024,6144]{1,0:T(8,128)(2,1)}) %all-gather.10.cloned.1.call-update) | async-done | bytes 12582928 | tf_op jit(solution)/shard_map/all_gather | solution.py:114
  167.8 6.3 fusion.122
  174.3 64.3 %all-gather.12.cloned.1.call-done = bf16[1024,3072]{1,0:T(8,128)(2,1)} async-done(((bf16[32,3072]{1,0:T(8,128)(2,1)}), bf16[1024,3072]{1,0:T(8,128)(2,1)}) %all-gather.12.cloned.1.call-update) | async-done | bytes 6291472 | tf_op jit(solution)/shard_map/all_gather | solution.py:116
  238.5 7.3 fusion.107
  263.9 4.9 fusion.84
  268.9 34.2 %while.30 = (s32[]{:T(128)}, bf16[4,680,4,64]{1,3,2,0:T(8,128)(2,1)}, f32[4,4,680,1]{2,1,3,0:T(4,128)S(1)}, bf16[4,680,4,64]{1,3,2,0:T(8,128)(2,1)}, bf16[4,680,...) while((s32[]{:T(128)}, ...), condition=%wide.region_7.8_spmd.clone.clone, body=%wide.region_4.7_spmd.sunk.clone.sunk.clone | while | flops 488291680 | bytes 37862984 | solution.py:152
  303.1 5.4 fusion.117
  310.5 64.8 %all-gather.16.cloned.1.call-done = bf16[1024,4096]{1,0:T(8,128)(2,1)} async-done(((bf16[32,4096]{1,0:T(8,128)(2,1)}), bf16[1024,4096]{1,0:T(8,128)(2,1)}) %all-gather.16.cloned.1.call-update) | async-done | bytes 8388624 | tf_op jit(solution)/shard_map/all_gather | solution.py:159
  375.3 12.3 fusion.112
  387.5 66.5 %all-gather.18.cloned.1.call-done = bf16[4096,1024]{1,0:T(8,128)(2,1)} async-done(((bf16[128,1024]{1,0:T(8,128)(2,1)}), bf16[4096,1024]{1,0:T(8,128)(2,1)}) %all-gather.18.cloned.1.call-update) | async-done | bytes 8388624 | tf_op jit(solution)/shard_map/all_gather | solution.py:161
  454.0 19.8 %convert_reduce_fusion = (f32[4096]{0:T(1024)}, bf16[680,4096]{1,0:T(8,128)(2,1)}) fusion(f32[680,4096]{1,0:T(8,128)} %fusion.112, f32[4096]{0:T(1024)S(1)} %bitcast.305, bf16[4096,1024]{1,0:T(8,128)(2,1)} %all-gather.18.cloned.1.call-done, bf16[1,680,1024]{2,1,0:T(8,128)(2,1)} %param.31, f32[1024]{0:T(1024)S(1)} %bitcast.313, f32[680]{0:T(1024)S(1)} %copy-done.57), kind=kOutput, calls=%fused_computation.68 | convolution fusion | flops 5771096064 | bytes 26532512 | tf_op jit(solution)/shard_map/rd,fd->rf/dot_general | solution.py:190
  473.9 11.1 fusion.76
  492.6 64.8 %while.31 = (s32[]{:T(128)}, f32[4,680,4,64]{1,3,2,0:T(8,128)}, f32[4,680,4,64]{1,3,2,0:T(8,128)}, bf16[4,680,4,64]{1,3,2,0:T(8,128)(2,1)}, bf16[4,680,4,64]{1,3...) while((s32[]{:T(128)}, f32[4,680,4,64]{1,3,2,0:T(8,128)}, ...), condition=%wide.region_14.15_spmd.clone.clone, body=%wide.region_12.14_spmd.sunk.clone.sunk.clone | while | flops 1205936512 | bytes 70155080 | solution.py:214
  527.5 3.7 multiply_reduce_fusion.6
  594.9 12.0 fusion.74
  606.9 10.5 fusion.73
  625.1 17.2 fusion.77
  642.4 7.9 fusion.123
  653.4 6.7 fusion.90
  660.7 12.5 fusion.82
  674.0 13.7 fusion.110
  688.3 11.6 broadcast_multiply_fusion
  700.2 15.3 fusion.93
  718.8 40.4 %all-reduce.3 = (f32[6144]{0:T(1024)S(1)}, f32[16]{0:T(128)}, f32[4096]{0:T(1024)S(1)}) all-reduce(bf16[6144]{0:T(1024)(128)(2,1)S(1)} %constant_dynamic-update-slice_fusion, f32[16]{0:T(128)S(1)} %exponential_multiply_fusion, f32[4096]{0:T(1024)S(1)} %copy-done.41), channel_id=4, replica_groups=mesh['wide'=8,'narrow'=4] {'wide','narrow'}, use_global_device_ids=true, to_apply=%region_27.28.clone | all-reduce | flops 10256 | bytes 69760
  760.4 32.0 %reduce-scatter.7.cloned.1.call-done = f32[1001,32]{0,1:T(8,128)} async-done(((f32[1001,1024]{0,1:T(8,128)}), f32[1001,32]{0,1:T(8,128)}) %reduce-scatter.7.cloned.1.call-update) | async-done | bytes 128144 | tf_op jit(solution)/shard_map/reduce_scatter | solution.py:261
  792.5 139.7 %reduce-scatter.13.cloned.1.call-done = f32[32,1024]{1,0:T(8,128)} async-done(((f32[1024,1024]{1,0:T(8,128)}), f32[32,1024]{1,0:T(8,128)}) %reduce-scatter.13.cloned.1.call-update) | async-done | bytes 131088 | tf_op jit(solution)/shard_map/reduce_scatter | solution.py:259
  932.1 157.9 %reduce-scatter.11.cloned.1.call-done = f32[32,3072]{1,0:T(8,128)} async-done(((f32[1024,3072]{1,0:T(8,128)}), f32[32,3072]{1,0:T(8,128)}) %reduce-scatter.11.cloned.1.call-update) | async-done | bytes 393232 | tf_op jit(solution)/shard_map/reduce_scatter | solution.py:258
  1090.1 184.6 %reduce-scatter.15.cloned.1.call-done = f32[32,4096]{1,0:T(8,128)} async-done(((f32[1024,4096]{1,0:T(8,128)}), f32[32,4096]{1,0:T(8,128)}) %reduce-scatter.15.cloned.1.call-update) | async-done | bytes 524304 | tf_op jit(solution)/shard_map/reduce_scatter | solution.py:196
  1274.7 255.3 %reduce-scatter.9.cloned.1.call-done = f32[32,6144]{1,0:T(8,128)} async-done(((f32[1024,6144]{1,0:T(8,128)}), f32[32,6144]{1,0:T(8,128)}) %reduce-scatter.9.cloned.1.call-update) | async-done | bytes 786448 | tf_op jit(solution)/shard_map/reduce_scatter | solution.py:256
  1530.0 185.2 %reduce-scatter.17.cloned.1.call-done = f32[128,1024]{1,0:T(8,128)} async-done(((f32[4096,1024]{1,0:T(8,128)}), f32[128,1024]{1,0:T(8,128)}) %reduce-scatter.17.cloned.1.call-update) | async-done | bytes 524304 | tf_op jit(solution)/shard_map/reduce_scatter | solution.py:198
  (298 shorter events, 192.3 us)
Async XLA Ops:
  7.2 94.7 %all-gather.8.cloned.1.call-start = ((), (), s32[]{:S(2)}) async-start(), calls=%async_computation.6 | async-start | bytes 2162688 | tf_op jit(solution)/shard_map/all_gather | solution.py:119
  7.9 159.9 %all-gather.10.cloned.1.call-start = ((), (), s32[]{:S(2)}) async-start(), calls=%async_computation.7 | async-start | bytes 12976128 | tf_op jit(solution)/shard_map/all_gather | solution.py:114
  8.7 53.1 %copy-start.64 = (bf16[192]{0:T(256)(128)(2,1)S(1)}, bf16[192]{0:T(256)(128)(2,1)}, u32[]{:S(2)}) copy-start(bf16[192]{0:T(256)(128)(2,1)} %param.24) | copy-start | bytes 1156
  8.7 91.7 %copy-start.7 = (bf16[1,680,1024]{2,1,0:T(8,128)(2,1)S(1)}, bf16[1,680,1024]{2,1,0:T(8,128)(2,1)}, u32[]{:S(2)}) copy-start(bf16[1,680,1024]{2,1,0:T(8,128)(2,1)} %param.19) | copy-start | bytes 4177924
  8.7 229.8 %all-gather.12.cloned.1.call-start = ((), (), s32[]{:S(2)}) async-start(), calls=%async_computation.8 | async-start | bytes 6488064 | tf_op jit(solution)/shard_map/all_gather | solution.py:116
  9.4 293.6 %all-gather.14.cloned.1.call-start = ((), (), s32[]{:S(2)}) async-start(), calls=%async_computation.9 | async-start | bytes 2162688 | tf_op jit(solution)/shard_map/all_gather | solution.py:117
  10.0 365.3 %all-gather.16.cloned.1.call-start = ((), (), s32[]{:S(2)}) async-start(), calls=%async_computation.10 | async-start | bytes 8650752 | tf_op jit(solution)/shard_map/all_gather | solution.py:159
  10.6 443.4 %all-gather.18.cloned.1.call-start = ((), (), s32[]{:S(2)}) async-start(), calls=%async_computation.11 | async-start | bytes 8650752 | tf_op jit(solution)/shard_map/all_gather | solution.py:161
  11.2 781.3 %reduce-scatter.7.cloned.1.call-start = ((), (), s32[]{:S(2)}) async-start(), calls=%async_computation.12 | async-start | bytes 4325376 | tf_op jit(solution)/shard_map/reduce_scatter | solution.py:261
  12.6 88.1 %copy-start.49 = (f32[16]{0:T(128)}, f32[16]{0:T(128)S(1)}, u32[]{:S(2)}) copy-start(f32[16]{0:T(128)S(1)} %exp.21) | copy-start | bytes 196
  14.0 87.2 %copy-start.59 = (s32[680]{0:T(1024)S(1)}, s32[680]{0:T(1024)}, u32[]{:S(2)}) copy-start(s32[680]{0:T(1024)} %constant.81.clone) | copy-start | bytes 8164
  100.7 137.8 %copy-start.39 = (f32[680]{0:T(1024)}, f32[680]{0:T(1024)S(1)}, u32[]{:S(2)}) copy-start(f32[680]{0:T(1024)S(1)} %broadcast_multiply_fusion.3) | copy-start | bytes 8164
  101.2 137.3 %copy-start.33 = (f32[680]{0:T(1024)}, f32[680]{0:T(1024)S(1)}, u32[]{:S(2)}) copy-start(f32[680]{0:T(1024)S(1)} %fusion.101) | copy-start | bytes 8164
  104.1 70.1 %copy-start.35 = (f32[1,1024]{1,0:T(1,128)}, f32[1,1024]{1,0:T(1,128)S(1)}, u32[]{:S(2)}) copy-start(f32[1,1024]{1,0:T(1,128)S(1)} %fusion.121) | copy-start | bytes 12292
  174.2 71.6 %copy-start.44 = (f32[1,1024]{1,0:T(1,128)}, f32[1,1024]{1,0:T(1,128)S(1)}, u32[]{:S(2)}) copy-start(f32[1,1024]{1,0:T(1,128)S(1)} %get-tuple-element.222) | copy-start | bytes 12292
  174.2 71.6 %copy-start.53 = (f32[1,1024]{1,0:T(1,128)}, f32[1,1024]{1,0:T(1,128)S(1)}, u32[]{:S(2)}) copy-start(f32[1,1024]{1,0:T(1,128)S(1)} %get-tuple-element.221) | copy-start | bytes 12292
  174.2 201.1 %copy-start.31 = (f32[1,1024]{1,0:T(1,128)}, f32[1,1024]{1,0:T(1,128)S(1)}, u32[]{:S(2)}) copy-start(f32[1,1024]{1,0:T(1,128)S(1)} %get-tuple-element.219) | copy-start | bytes 12292
  174.2 279.8 %copy-start.51 = (f32[1,1024]{1,0:T(1,128)}, f32[1,1024]{1,0:T(1,128)S(1)}, u32[]{:S(2)}) copy-start(f32[1,1024]{1,0:T(1,128)S(1)} %get-tuple-element.218) | copy-start | bytes 12292
  174.2 310.8 %copy-start.27 = (f32[1,1024]{1,0:T(1,128)}, f32[1,1024]{1,0:T(1,128)S(1)}, u32[]{:S(2)}) copy-start(f32[1,1024]{1,0:T(1,128)S(1)} %get-tuple-element.220) | copy-start | bytes 12292
  174.2 312.3 %copy-start.55 = (f32[1,1024]{1,0:T(1,128)}, f32[1,1024]{1,0:T(1,128)S(1)}, u32[]{:S(2)}) copy-start(f32[1,1024]{1,0:T(1,128)S(1)} %get-tuple-element.223) | copy-start | bytes 12292
  268.9 34.2 %copy-start.8 = (bf16[1,680,1024]{2,1,0:T(8,128)(2,1)S(1)}, bf16[1,680,1024]{2,1,0:T(8,128)(2,1)}, u32[]{:S(2)}) copy-start(bf16[1,680,1024]{2,1,0:T(8,128)(2,1)} %param.19) | copy-start | bytes 4177924
  308.5 176.5 %copy-start.15 = (f32[680]{0:T(1024)}, f32[680]{0:T(1024)S(1)}, u32[]{:S(2)}) copy-start(f32[680]{0:T(1024)S(1)} %broadcast_multiply_fusion.2) | copy-start | bytes 8164
  310.5 174.5 %copy-start.29 = (f32[680]{0:T(1024)}, f32[680]{0:T(1024)S(1)}, u32[]{:S(2)}) copy-start(f32[680]{0:T(1024)S(1)} %fusion.102) | copy-start | bytes 8164
  375.3 78.8 %copy-start.42 = (f32[32,1,128]{2,1,0:T(1,128)S(1)}, f32[32,1,128]{2,1,0:T(1,128)}, u32[]{:S(2)}) copy-start(f32[32,1,128]{2,1,0:T(1,128)} %convert_element_type.133) | copy-start | bytes 49156
  375.3 78.8 %copy-start.57 = (f32[680]{0:T(1024)S(1)}, f32[680]{0:T(1024)}, u32[]{:S(2)}) copy-start(f32[680]{0:T(1024)} %compare_convert_fusion) | copy-start | bytes 8164
  454.0 19.8 %copy-start.4 = (f32[1,680,1024]{2,1,0:T(8,128)S(1)}, f32[1,680,1024]{2,1,0:T(8,128)}, u32[]{:S(2)}) copy-start(f32[1,680,1024]{2,1,0:T(8,128)} %copy-done.3) | copy-start | bytes 8355844
  625.1 17.2 copy-start.60
  652.7 279.4 %reduce-scatter.13.cloned.1.call-start = ((), (), s32[]{:S(2)}) async-start(), calls=%async_computation.15 | async-start | bytes 4325376 | tf_op jit(solution)/shard_map/reduce_scatter | solution.py:259
  660.1 430.0 %reduce-scatter.11.cloned.1.call-start = ((), (), s32[]{:S(2)}) async-start(), calls=%async_computation.14 | async-start | bytes 12976128 | tf_op jit(solution)/shard_map/reduce_scatter | solution.py:258
  673.3 601.4 %reduce-scatter.15.cloned.1.call-start = ((), (), s32[]{:S(2)}) async-start(), calls=%async_computation.16 | async-start | bytes 17301504 | tf_op jit(solution)/shard_map/reduce_scatter | solution.py:196
  687.6 842.4 %reduce-scatter.9.cloned.1.call-start = ((), (), s32[]{:S(2)}) async-start(), calls=%async_computation.13 | async-start | bytes 25952256 | tf_op jit(solution)/shard_map/reduce_scatter | solution.py:256
  699.9 1015.3 %reduce-scatter.17.cloned.1.call-start = ((), (), s32[]{:S(2)}) async-start(), calls=%async_computation.17 | async-start | bytes 17301504 | tf_op jit(solution)/shard_map/reduce_scatter | solution.py:198
  (55 other events, 179.5 us)
Sparse Core Ops, SparseCore 0:
  10.9 59.1 all-gather.7
  72.9 94.9 all-gather.9
  170.7 67.7 all-gather.11
  241.2 54.9 all-gather.13
  298.9 76.3 all-gather.15
  378.0 76.0 all-gather.17
  652.8 139.6 reduce-scatter.6
  795.3 136.7 reduce-scatter.12
  938.7 151.2 reduce-scatter.10
  1092.9 181.7 reduce-scatter.14
  1282.9 247.1 reduce-scatter.8
  1532.8 182.4 reduce-scatter.16
where the time goes:
time: 1730 us; the launch traced here: 1720 us
  waiting for transfers between devices  1220 us (71%)
  matrix products  229 us (13%)
  blocking collectives  121 us (7%)
  other arithmetic  70.2 us (4%)
  local copies, waits for them, and re-layouts  66.8 us (4%)
    reduce_scatter x1, waiting for transfers between devices, per_device(): lax.psum_scatter(ada_grad, ('wide', 'narrow'), scatter_dimension=0, tiled...  255 us
    reduce_scatter x1, waiting for transfers between devices, per_device(): lax.psum_scatter(down_grad, ('wide', 'narrow'), scatter_dimension=0, tile...  185 us
    reduce_scatter x1, waiting for transfers between devices, per_device(): lax.psum_scatter(up_grad, ('wide', 'narrow'), scatter_dimension=0, tiled=...  185 us
    reduce_scatter x1, waiting for transfers between devices, per_device(): lax.psum_scatter(qkv_grad, ('wide', 'narrow'), scatter_dimension=0, tiled...  158 us
    reduce_scatter x1, waiting for transfers between devices, per_device(): lax.psum_scatter(out_grad, ('wide', 'narrow'), scatter_dimension=0, tiled...  140 us
    unnamed x2, blocking collectives  78.2 us
    all_gather x1, waiting for transfers between devices, per_device(): lax.all_gather(down_weight, ('wide', 'narrow'), axis=0, tiled=True)  66.5 us
    all_gather x1, waiting for transfers between devices, per_device(): lax.all_gather(up_weight, ('wide', 'narrow'), axis=0, tiled=True)  64.8 us
  transfers between devices with their start and end apart: 12, of which 10 were waited for; matrix products, arithmetic and copies ran while one was open for 9% of the time, Pallas kernels for 0%

commit v1 on v0

v1 whole, which is shorter than its diff:
```python
from functools import partial

import jax
import jax.numpy as jnp
import numpy as np
from jax import lax
from jax.experimental import pallas as pl
from jax.experimental.pallas import tpu as pltpu
from jax.sharding import PartitionSpec as P

HDIM = 64
SCALES = 10
AXES = ("wide", "narrow")
BF = jnp.bfloat16
F32 = jnp.float32

scale_sides = (1, 2, 3, 4, 5, 6, 8, 10, 13, 16)
head_block = 4


def position_scale(scale_count):
    return np.concatenate(
        [
            np.full(side_size * side_size, level_index, dtype=np.int32)
            for level_index, side_size in enumerate(scale_sides[:scale_count])
        ]
    )


def normalized(inputs):
    centred = inputs - jnp.mean(inputs, axis=-1, keepdims=True)
    return centred * lax.rsqrt(jnp.mean(centred * centred, axis=-1, keepdims=True) + 1e-06)


def modulate(inputs, scale_vec, shift_vec):
    return normalized(inputs) * (1.0 + scale_vec[:, None, :]) + shift_vec[:, None, :]


def unit_rows(inputs):
    return inputs * lax.rsqrt(jnp.sum(inputs * inputs, axis=-1, keepdims=True) + 1e-06)


def split_heads(matrix, image_count, seq_len):
    blocks = matrix.reshape(image_count, seq_len, -1, head_block, HDIM)
    return jnp.moveaxis(blocks, 2, 1).reshape(-1, seq_len, head_block, HDIM)


def join_heads(blocks, image_count, seq_len):
    shaped = blocks.reshape(image_count, -1, seq_len, head_block, HDIM)
    return jnp.moveaxis(shaped, 1, 2).reshape(image_count * seq_len, -1)


def masked_scores(query_block, key_block, allowed):
    scores = jnp.einsum("qhc,khc->hqk", query_block, key_block, preferred_element_type=F32)
    return jnp.where(allowed[None], scores, -1e30)


def attend_forward(pieces, allowed):
    query_block, key_block, value_block = pieces
    scores = masked_scores(query_block, key_block, allowed)
    row_peak = jnp.max(scores, axis=-1, keepdims=True)
    log_total = row_peak + jnp.log(jnp.sum(jnp.exp(scores - row_peak), axis=-1, keepdims=True))
    probs_low = jnp.exp(scores - log_total).astype(BF)
    attended = jnp.einsum("hqk,khc->qhc", probs_low, value_block, preferred_element_type=F32)
    return (attended, log_total)


def attend_backward(pieces, allowed):
    query_block, key_block, value_block, grad_block, log_total = pieces
    scores = masked_scores(query_block, key_block, allowed)
    probs = jnp.exp(scores - log_total)
    probs_low = probs.astype(BF)
    grad_probs = jnp.einsum("qhc,khc->hqk", grad_block, value_block, preferred_element_type=F32)
    row_inner = jnp.sum(probs * grad_probs, axis=-1, keepdims=True)
    grad_scores = (probs * (grad_probs - row_inner)).astype(BF)
    grad_values = jnp.einsum("hqk,qhc->khc", probs_low, grad_block, preferred_element_type=F32)
    grad_queries = jnp.einsum("hqk,khc->qhc", grad_scores, key_block, preferred_element_type=F32)
    grad_keys = jnp.einsum("hqk,qhc->khc", grad_scores, query_block, preferred_element_type=F32)
    return (grad_queries, grad_keys, grad_values)


def swap(block, count, mask):
    return lax.ppermute(block, AXES, [(i, i ^ mask) for i in range(count)])


def place_body(me_ref, *refs, blocks):
    half = len(refs) // 2
    for src, dst in zip(refs[:half], refs[half:]):
        dst[...] = src[0]


def gather_rows(shard, count, me):
    rows, width = shard.shape
    bits = count.bit_length() - 1
    if count != 1 << bits or bits < 3 or rows % 16 or width % 256:
        return lax.all_gather(shard, AXES, axis=0, tiled=True)
    block, order = shard[None], []
    for bit in range(bits - 1, 2, -1):
        block = jnp.concatenate([block, swap(block, count, 1 << bit)])
        order.append(bit)
    half = width // 2
    parts = []
    for cols, two in ((block[:, :, :half], (2, 1)), (block[:, :, half:], (1, 2))):
        for bit in two:
            cols = jnp.concatenate([cols, swap(cols, count, 1 << bit)])
        parts.append((cols, swap(cols, count, 1), order + list(two)))
    out = []
    total = count // 2
    for own, other, seq in parts:
        code = [0]
        for bit in seq:
            code = code + [c | (1 << bit) for c in code]
        code = jnp.asarray(np.array(code, np.int32)) ^ me
        out.append(place(own, other, code, total, rows, half))
    return out


def place(own, other, code, total, rows, width):
    def body(code_ref, own_ref, other_ref, out_ref):
        core = code_ref[pl.program_id(0)] & 1

        @pl.when(core == 0)
        def _():
            out_ref[0] = own_ref[0]
            out_ref[1] = other_ref[0]

        @pl.when(core == 1)
        def _():
            out_ref[1] = own_ref[0]
            out_ref[0] = other_ref[0]

    out = pl.pallas_call(
        body,
        grid_spec=pltpu.PrefetchScalarGridSpec(
            num_scalar_prefetch=1,
            grid=(total,),
            in_specs=[pl.BlockSpec((1, rows, width), lambda m, code: (m, 0, 0))] * 2,
            out_specs=pl.BlockSpec((2, rows, width), lambda m, code: (code[m] // 2, 0, 0)),
        ),
        out_shape=jax.ShapeDtypeStruct((2 * total, rows, width), own.dtype),
        name="place",
    )(code, own, other)
    return out.reshape(2 * total * rows, width)


def halve(pieces, axis, bit_value, count, mask):
    total = pieces[0]
    if len(pieces) > 1:
        total = (pieces[0].astype(F32) + pieces[1].astype(F32)).astype(BF)
    keep = lax.dynamic_index_in_dim(total, bit_value, axis, keepdims=False)
    send = lax.dynamic_index_in_dim(total, 1 - bit_value, axis, keepdims=False)
    return [keep, swap(send, count, mask)]


def scatter_rows(grad, count, me):
    rows, width = grad.shape
    bits = count.bit_length() - 1
    own = rows // count
    if count != 1 << bits or bits < 3 or width % 256:
        return lax.psum_scatter(grad.astype(F32), AXES, scatter_dimension=0, tiled=True)
    bit = [lax.rem(lax.div(me, np.int32(1 << b)), np.int32(2)) for b in range(bits)]
    pieces = halve([grad.reshape((2,) * bits + (own, width))], bits - 1, bit[0], count, 1)
    half = width // 2
    done = []
    for cols, two in ((slice(0, half), (1, 2)), (slice(half, width), (2, 1))):
        part = [p[..., cols] for p in pieces]
        left = list(range(bits - 1, 0, -1))
        for b in two:
            part = halve(part, left.index(b), bit[b], count, 1 << b)
            left.remove(b)
        done.append(part)
    pieces = [jnp.concatenate([a, b], axis=-1) for a, b in zip(*done)]
    for b in range(3, bits):
        pieces = halve(pieces, left.index(b), bit[b], count, 1 << b)
        left.remove(b)
    return (pieces[0].astype(F32) + pieces[1].astype(F32)).reshape(own, width)


def mlp_body(x_ref, g_ref, up_ref, down_ref, bias_ref, out_ref, gx_ref, up_g, down_g, bias_g):
    @pl.when(pl.program_id(0) == 0)
    def _():
        out_ref[...] = jnp.zeros_like(out_ref)
        gx_ref[...] = jnp.zeros_like(gx_ref)

    x, g, up, down = x_ref[...], g_ref[...], up_ref[...], down_ref[...]
    hidden = jnp.dot(x, up, preferred_element_type=F32) + bias_ref[...]
    root = np.float32(np.sqrt(2.0 / np.pi))
    square = hidden * hidden
    bend = jnp.tanh(root * hidden * (1.0 + 0.044715 * square))
    act = (0.5 * hidden * (1.0 + bend)).astype(BF)
    out_ref[...] += jnp.dot(act, down, preferred_element_type=F32)
    grad_act = lax.dot_general(g, down, (((1,), (1,)), ((), ())), preferred_element_type=F32)
    slope = 0.5 * (1.0 + bend) + 0.5 * hidden * (1.0 - bend * bend) * root * (
        1.0 + (3 * 0.044715) * square
    )
    grad_hidden_wide = grad_act * slope
    grad_hidden = grad_hidden_wide.astype(BF)
    bias_g[...] = jnp.sum(grad_hidden.astype(F32), axis=0, keepdims=True)
    gx_ref[...] += lax.dot_general(
        grad_hidden, up, (((1,), (1,)), ((), ())), preferred_element_type=F32
    )
    down_g[...] = lax.dot_general(
        act, g, (((0,), (0,)), ((), ())), preferred_element_type=F32
    ).astype(BF)
    up_g[...] = lax.dot_general(
        x, grad_hidden, (((0,), (0,)), ((), ())), preferred_element_type=F32
    ).astype(BF)


def mlp(x, g, weights, bias, block=512):
    tokens, width = x.shape
    hidden = bias.shape[1]
    per = width // block
    whole = lambda f: (0, 0)
    return pl.pallas_call(
        mlp_body,
        grid=(hidden // block,),
        in_specs=[
            pl.BlockSpec((tokens, width), whole),
            pl.BlockSpec((tokens, width), whole),
            pl.BlockSpec((width, block), lambda f: (0, f)),
            pl.BlockSpec((block, width), lambda f: (f % per, hidden // width + f // per)),
            pl.BlockSpec((1, block), lambda f: (0, f)),
        ],
        out_specs=[
            pl.BlockSpec((tokens, width), whole),
            pl.BlockSpec((tokens, width), whole),
            pl.BlockSpec((width, block), lambda f: (0, f)),
            pl.BlockSpec((block, width), lambda f: (f % per, f // per)),
            pl.BlockSpec((1, block), lambda f: (0, f)),
        ],
        out_shape=[
            jax.ShapeDtypeStruct((tokens, width), F32),
            jax.ShapeDtypeStruct((tokens, width), F32),
            jax.ShapeDtypeStruct((width, hidden), BF),
            jax.ShapeDtypeStruct((width, hidden), BF),
            jax.ShapeDtypeStruct((1, hidden), F32),
        ],
        compiler_params=pltpu.CompilerParams(vmem_limit_bytes=58 << 20),
        cost_estimate=pl.CostEstimate(
            flops=12 * tokens * width * hidden, bytes_accessed=8 * width * hidden, transcendentals=tokens * hidden
        ),
        name="mlp",
    )(x, g, weights, weights, bias)


def split_low(value):
    high = value.astype(BF)
    return high, (value - high.astype(F32)).astype(BF)


def per_device(
    tokens,
    labels,
    stop_scale,
    class_table,
    ada_weight,
    ada_bias,
    qkv_weight,
    head_scale,
    out_weight,
    up_weight,
    up_bias,
    down_weight,
    cotangent,
    count,
):
    image_count, seq_len, model_width = tokens.shape
    row_count = image_count * seq_len
    me = lax.axis_index(AXES).astype(jnp.int32)
    levels = position_scale(SCALES)
    allowed = jnp.asarray(levels[None, :] <= levels[:, None])
    live_mask = (jnp.asarray(levels)[None, :] < stop_scale[:, None]).astype(F32)[:, :, None]
    class_count = class_table.shape[0]
    own = model_width // count
    ratio = down_weight.shape[0] // own
    hidden_width = up_weight.shape[1]

    def hidden_order(matrix):
        lead = matrix.shape[:-1]
        cut = matrix.reshape(lead + (count, ratio, own))
        return jnp.swapaxes(cut, -3, -2).reshape(lead + (hidden_width,))

    def hidden_back(matrix):
        lead = matrix.shape[:-1]
        cut = matrix.reshape(lead + (ratio, count, own))
        return jnp.swapaxes(cut, -3, -2).reshape(lead + (hidden_width,))

    down_wide = jnp.swapaxes(down_weight.reshape(ratio, own, model_width), 0, 1).reshape(
        own, hidden_width
    )
    mlp_shard = jnp.concatenate([hidden_order(up_weight), down_wide], axis=1)
    mlp_full = lax.all_gather(mlp_shard, AXES, axis=0, tiled=True)

    labels_all = lax.all_to_all(
        jnp.broadcast_to(labels[None, :], (count, image_count)), AXES, 0, 0, tiled=True
    ).reshape(-1)
    onehot = labels_all[:, None] == jnp.arange(class_count, dtype=jnp.int32)[None, :]
    condition = jnp.dot(onehot.astype(BF), class_table, preferred_element_type=F32)
    cond_act = jax.nn.silu(condition).astype(BF)
    modul_part = jnp.dot(cond_act, ada_weight, preferred_element_type=F32)
    bias_own = ada_bias.shape[0]
    bias_row = lax.dynamic_update_slice(
        jnp.zeros((6 * model_width,), F32), ada_bias.astype(F32), (me * bias_own,)
    )
    modul_part = modul_part + bias_row[None, :]
    up_bias_rows = jnp.broadcast_to(
        up_bias.astype(F32)[None, :], (count * image_count, up_bias.shape[0])
    )
    modul_all = lax.all_to_all(
        jnp.concatenate([modul_part, up_bias_rows], axis=1), AXES, 0, 0, tiled=True
    ).reshape(count, image_count, -1)
    modulation = jnp.sum(modul_all[:, :, : 6 * model_width], axis=0)
    up_bias_full = modul_all[:, 0, 6 * model_width :].reshape(1, hidden_width)
    gate_one, gate_two, scale_one, scale_two, shift_one, shift_two = jnp.split(
        modulation, 6, axis=-1
    )

    attn_shard = jnp.concatenate([qkv_weight, out_weight], axis=1)
    gathered = gather_rows(attn_shard, count, me)
    attn_full = (
        jnp.concatenate(gathered, axis=1) if isinstance(gathered, list) else gathered
    )
    qkv_full = attn_full[:, : 3 * model_width]
    out_full = attn_full[:, 3 * model_width :]

    inputs = tokens.astype(F32)
    attn_in = modulate(inputs, scale_one, shift_one).astype(BF).reshape(row_count, model_width)
    qkv_rows = jnp.dot(attn_in, qkv_full, preferred_element_type=F32)
    query_raw, key_raw, value_raw = jnp.split(qkv_rows, 3, axis=-1)

    def scaled_query(query_input, log_scale):
        return unit_rows(query_input.reshape(row_count, -1, HDIM)) * jnp.exp(log_scale)[:, None]

    def key_unit_rows(key_input):
        return unit_rows(key_input.reshape(row_count, -1, HDIM))

    query_low = scaled_query(query_raw, head_scale).astype(BF).reshape(row_count, model_width)
    key_low = key_unit_rows(key_raw).astype(BF).reshape(row_count, model_width)
    value_low = value_raw.astype(BF)
    head_pieces = (
        split_heads(query_low, image_count, seq_len),
        split_heads(key_low, image_count, seq_len),
        split_heads(value_low, image_count, seq_len),
    )
    attended_blocks, log_totals = lax.map(partial(attend_forward, allowed=allowed), head_pieces)
    attended = join_heads(attended_blocks, image_count, seq_len).astype(BF)
    projected = jnp.dot(attended, out_full, preferred_element_type=F32).reshape(
        image_count, seq_len, model_width
    )
    residual = inputs + gate_one[:, None, :] * projected
    mlp_in = (
        modulate(residual, scale_two, shift_two).astype(BF).reshape(row_count, model_width)
    )
    grad_out = cotangent.astype(F32) * live_mask
    grad_mlp = (gate_two[:, None, :] * grad_out).astype(BF).reshape(row_count, model_width)

    mlp_out, grad_mlp_in, up_grad, down_grad, up_bias_grad = mlp(
        mlp_in, grad_mlp, mlp_full, hidden_order(up_bias_full)
    )
    mlp_out = mlp_out.reshape(image_count, seq_len, model_width)
    grad_mlp_in = grad_mlp_in.reshape(image_count, seq_len, model_width)
    down_own = scatter_rows(down_grad, count, me)
    up_own = scatter_rows(up_grad, count, me)
    block_out = ((residual + gate_two[:, None, :] * mlp_out) * live_mask).astype(BF)
    gate_two_grad = jnp.sum(grad_out * mlp_out, axis=1)
    second_back = jax.vjp(modulate, residual, scale_two, shift_two)[1]
    grad_resid_part, scale_two_grad, shift_two_grad = second_back(grad_mlp_in)
    grad_resid = grad_out + grad_resid_part
    gate_one_grad = jnp.sum(grad_resid * projected, axis=1)
    grad_proj = (gate_one[:, None, :] * grad_resid).astype(BF).reshape(row_count, model_width)
    out_grad = jnp.einsum("rd,re->de", attended, grad_proj, preferred_element_type=F32)
    grad_attended = jnp.einsum("re,de->rd", grad_proj, out_full, preferred_element_type=F32).astype(
        BF
    )
    grad_blocks = lax.map(
        partial(attend_backward, allowed=allowed),
        head_pieces + (split_heads(grad_attended, image_count, seq_len), log_totals),
    )
    grad_query_scaled = join_heads(grad_blocks[0], image_count, seq_len)
    grad_key_unit = join_heads(grad_blocks[1], image_count, seq_len)
    grad_values = join_heads(grad_blocks[2], image_count, seq_len)
    query_back = jax.vjp(scaled_query, query_raw, head_scale)[1]
    grad_query_raw, head_scale_part = query_back(grad_query_scaled.reshape(row_count, -1, HDIM))
    key_back = jax.vjp(key_unit_rows, key_raw)[1]
    grad_key_raw = key_back(grad_key_unit.reshape(row_count, -1, HDIM))[0]
    grad_qkv = jnp.concatenate([grad_query_raw, grad_key_raw, grad_values], axis=-1).astype(BF)
    qkv_grad = jnp.einsum("rd,re->de", attn_in, grad_qkv, preferred_element_type=F32)
    attn_own = scatter_rows(
        jnp.concatenate([qkv_grad.astype(BF), out_grad.astype(BF)], axis=1), count, me
    )
    grad_attn_in = jnp.einsum("re,de->rd", grad_qkv, qkv_full, preferred_element_type=F32).reshape(
        image_count, seq_len, model_width
    )
    first_back = jax.vjp(modulate, inputs, scale_one, shift_one)[1]
    grad_token_part, scale_one_grad, shift_one_grad = first_back(grad_attn_in)
    input_grad = grad_resid + grad_token_part
    grad_modul = jnp.concatenate(
        [
            gate_one_grad,
            gate_two_grad,
            scale_one_grad,
            scale_two_grad,
            shift_one_grad,
            shift_two_grad,
        ],
        axis=-1,
    ).astype(BF)
    bias_high, bias_low = split_low(hidden_back(up_bias_grad).reshape(count, -1))
    head_high, head_low = split_low(head_scale_part)
    heads = head_scale.shape[0]
    common = jnp.concatenate([grad_modul.reshape(-1), head_high, head_low])
    small = jnp.concatenate(
        [jnp.broadcast_to(common[None, :], (count, common.shape[0])), bias_high, bias_low], axis=1
    )
    small = lax.all_to_all(small, AXES, 0, 0, tiled=True)
    modul_cols = image_count * 6 * model_width
    grad_modul_all = small[:, :modul_cols].reshape(count * image_count, 6 * model_width)
    tail = jnp.sum(small[:, modul_cols:].astype(F32), axis=0)
    head_scale_grad = tail[:heads] + tail[heads : 2 * heads]
    tail = tail[2 * heads :].reshape(2, -1)
    up_bias_own = tail[0] + tail[1]
    ada_bias_own = jnp.sum(
        lax.dynamic_slice_in_dim(grad_modul_all, me * bias_own, bias_own, axis=1).astype(F32), axis=0
    )
    ada_own = lax.dot_general(
        cond_act, grad_modul_all, (((0,), (0,)), ((), ())), preferred_element_type=F32
    )
    grad_cond_act = lax.dot_general(
        grad_modul_all, ada_weight, (((1,), (1,)), ((), ())), preferred_element_type=F32
    )
    grad_condition = jax.vjp(jax.nn.silu, condition)[1](grad_cond_act)[0]
    table_own = lax.dot_general(
        onehot.astype(F32),
        grad_condition,
        (((0,), (0,)), ((), ())),
        precision=lax.Precision.HIGHEST,
        preferred_element_type=F32,
    )
    qkv_own = attn_own[:, : 3 * model_width]
    out_own = attn_own[:, 3 * model_width :]
    up_own = hidden_back(up_own)
    down_own = jnp.swapaxes(down_own.reshape(own, ratio, model_width), 0, 1).reshape(
        ratio * own, model_width
    )
    return (
        block_out,
        input_grad,
        table_own,
        ada_own,
        ada_bias_own,
        qkv_own,
        head_scale_grad,
        out_own,
        up_own,
        up_bias_own,
        down_own,
    )


def solution(mesh):
    count = mesh.shape["wide"] * mesh.shape["narrow"]
    both = AXES
    in_specs = (
        P(both, None, None),
        P(both),
        P(both),
        P(None, both),
        P(both, None),
        P(both),
        P(both, None),
        P(),
        P(both, None),
        P(both, None),
        P(both),
        P(both, None),
        P(both, None, None),
    )
    out_specs = (
        P(both, None, None),
        P(both, None, None),
        P(None, both),
        P(both, None),
        P(both),
        P(both, None),
        P(),
        P(both, None),
        P(both, None),
        P(both),
        P(both, None),
    )
    return jax.shard_map(
        partial(per_device, count=count),
        mesh=mesh,
        in_specs=in_specs,
        out_specs=out_specs,
        check_vma=False,
    )
```

time: 1730 us -> 664 us (0.38)
  waiting for transfers between devices: 1220 us -> 182 us
  blocking collectives: 121 us -> 0 us
  matrix products: 229 us -> 121 us
  Pallas kernels: 0 us -> 69.3 us
  starting transfers between devices: 0.86 us -> 54.1 us
  local copies, waits for them, and re-layouts: 66.8 us -> 105 us
  other arithmetic: 70.2 us -> 107 us
    reduce_scatter x6 -> x0, waiting for transfers between devices: 955 us -> none  [the longest x1 255 us: per_device(): lax.psum_scatter(ada_grad, ('wide', 'narrow'), scatter_dimension=0, tiled...]
    all_gather x6 -> x1, waiting for transfers between devices: 259 us -> 0.01 us  [per_device(): mlp_full = lax.all_gather(mlp_shard, AXES, axis=0, tiled=True)]
    ppermute x0 -> x29, waiting for transfers between devices: none -> 182 us  [swap(): return lax.ppermute(block, AXES, [(i, i ^ mask) for i in range(count)])]
    dot_general x15 -> x11, matrix products: 150 us -> 42.1 us  [the longest x1 10.4 us: per_device(): jnp.einsum('rd,re->de', attn_in, grad_qkv, preferred_element_type=F32)]
    unnamed x2 -> x0, blocking collectives: 78.2 us -> none
    pallas_call x0 -> x3, Pallas kernels: none -> 69.3 us  [the longest x1 46.9 us: mlp(): pl.pallas_call(mlp_body, grid=(hidden // block,), in_specs=[pl.BlockSpec(...]
    all_gather x1 -> x0, blocking collectives: 43.1 us -> none  [per_device(): lax.all_gather(up_bias, ('wide', 'narrow'), axis=0, tiled=True)]
    ppermute x0 -> x29, starting transfers between devices: none -> 38.8 us  [swap(): return lax.ppermute(block, AXES, [(i, i ^ mask) for i in range(count)])]
  transfers between devices with their start and end apart: 12 -> 33, of which waited for: 10 -> 13; matrix products, arithmetic and copies ran while one was open for 9% -> 44% of each run, Pallas kernels for 0% -> 3%
where the time goes in v1:
time: 664 us; the launch traced here: 655 us
  waiting for transfers between devices  182 us (27%)
  matrix products  121 us (18%)
  other arithmetic  107 us (16%)
  local copies, waits for them, and re-layouts  105 us (16%)
  Pallas kernels  69.3 us (10%)
  starting transfers between devices  54.1 us (8%)
  between operations  16.7 us (3%)
    ppermute x29, waiting for transfers between devices, swap(): return lax.ppermute(block, AXES, [(i, i ^ mask) for i in range(count)])  182 us
    pallas_call x1, Pallas kernels, mlp(): pl.pallas_call(mlp_body, grid=(hidden // block,), in_specs=[pl.BlockSpec(...  46.9 us
    ppermute x29, starting transfers between devices, swap(): return lax.ppermute(block, AXES, [(i, i ^ mask) for i in range(count)])  38.8 us
    pallas_call x2, Pallas kernels, place(): pl.pallas_call(body, grid_spec=pltpu.PrefetchScalarGridSpec(num_scalar_pr...  22.4 us
    squeeze x3, local copies, waits for them, and re-layouts, halve(): keep = lax.dynamic_index_in_dim(total, bit_value, axis, keepdims=False)  19.7 us
    dot_general x8, matrix products, masked_scores(): jnp.einsum('qhc,khc->hqk', query_block, key_block, preferred_element_type...  19.4 us
    dot_general x4, matrix products, attend_backward(): jnp.einsum('qhc,khc->hqk', grad_block, value_block, preferred_element_typ...  14.8 us
    split x5, local copies, waits for them, and re-layouts, per_device(): query_raw, key_raw, value_raw = jnp.split(qkv_rows, 3, axis=-1)  13.9 us
  transfers between devices with their start and end apart: 33, of which 13 were waited for; matrix products, arithmetic and copies ran while one was open for 44% of the time, Pallas kernels for 3%

profile of v1, /device:TPU:0, one launch (start us, length us, event | category | flops | bytes accessed | tf_op | source)
XLA Modules:
  0.0 655.5 jit_solution(11654718789510826149)
XLA Ops:
  16.5 16.6 %collective-permute-done = bf16[1,32,4096]{2,1,0:T(8,128)(2,1)S(1)} collective-permute-done((bf16[1,32,4096]{2,1,0:T(8,128)(2,1)S(1)}, bf16[1,32,4096]{2,1,0:T(8,128)(2,1)S(1)}, u32[]{:S(2)}, u32[]{:S(2)}) %collective-permute-start) | collective-permute-done | bytes 262176 | tf_op jit(solution)/shard_map/ppermute | solution.py:83
  38.4 6.0 all-to-all-start
  45.6 10.4 %collective-permute-done.1 = bf16[2,32,4096]{2,1,0:T(8,128)(2,1)S(1)} collective-permute-done((bf16[2,32,4096]{2,1,0:T(8,128)(2,1)S(1)}, bf16[2,32,4096]{2,1,0:T(8,128)(2,1)S(1)}, u32[]{:S(2)}, u32[]{:S(2)}) %collective-permute-start.1) | collective-permute-done | bytes 524320 | tf_op jit(solution)/shard_map/ppermute | solution.py:83
  66.8 9.3 %collective-permute-done.5 = bf16[4,32,2048]{2,1,0:T(8,128)(2,1)S(1)} collective-permute-done((bf16[4,32,2048]{2,1,0:T(8,128)(2,1)S(1)}, bf16[4,32,2048]{2,1,0:T(8,128)(2,1)S(1)}, u32[]{:S(2)}, u32[]{:S(2)}) %collective-permute-start.5) | collective-permute-done | bytes 524320 | tf_op jit(solution)/shard_map/ppermute | solution.py:83
  82.2 5.0 all-to-all-start.1
  87.2 34.9 %collective-permute-done.6 = bf16[8,32,2048]{2,1,0:T(8,128)(2,1)} collective-permute-done((bf16[8,32,2048]{2,1,0:T(8,128)(2,1)}, bf16[8,32,2048]{2,1,0:T(8,128)(2,1)}, u32[]{:S(2)}, u32[]{:S(2)}) %collective-permute-start.6) | collective-permute-done | bytes 1048608 | tf_op jit(solution)/shard_map/ppermute | solution.py:83
  137.3 11.2 %place.3 = bf16[32,32,2048]{2,1,0:T(8,128)(2,1)} custom-call(s32[16]{0:T(128)} %broadcast_xor_fusion.code_ref, bf16[16,32,2048]{2,1,0:T(8,128)(2,1)} %pad_maximum_fusion.6.own_ref, bf16[16,32,2048]{2,1,0:T(8,128)(2,1)} %collective-permute-done.7.other_ref), custom_call_target="tpu_custom_call" | custom-call | tf_op jit(solution)/shard_map/place/pallas_call | solution.py:132
  148.5 11.2 %place.2 = bf16[32,32,2048]{2,1,0:T(8,128)(2,1)} custom-call(s32[16]{0:T(128)} %broadcast_xor_fusion.1.code_ref, bf16[16,32,2048]{2,1,0:T(8,128)(2,1)} %pad_maximum_fusion.5.own_ref, bf16[16,32,2048]{2,1,0:T(8,128)(2,1)} %collective-permute-done.4.other_ref), custom_call_target="tpu_custom_call" | custom-call | tf_op jit(solution)/shard_map/place/pallas_call | solution.py:132
  159.7 7.5 %fusion.62 = f32[680,3072]{1,0:T(8,128)S(1)} fusion(bf16[1024,2048]{1,0:T(8,128)(2,1)} %bitcast.413, bf16[1024,2048]{1,0:T(8,128)(2,1)} %bitcast.417, bf16[1,680,1024]{2,1,0:T(8,128)(2,1)S(1)} %copy-done.9, f32[1024]{0:T(1024)S(1)} %bitcast.445, f32[1024]{0:T(1024)S(1)} %bitcast.439, f32[680]{0:T(1024)S(1)} %fusion.111, f32[680]{0:T(1024)S(1)} %broadcast_multiply_fusion.1), kind=kOutput, calls=%fused_computation.99 | convolution fusion | flops 4294950912 | bytes 18150720 | tf_op jit(solution)/shard_map/dot_general | solution.py:329
  194.7 5.0 fusion.90
  199.7 34.1 %while.30 = (s32[]{:T(128)}, bf16[4,680,4,64]{1,3,2,0:T(8,128)(2,1)}, f32[4,4,680,1]{2,1,3,0:T(4,128)S(1)}, bf16[4,680,4,64]{1,3,2,0:T(8,128)(2,1)}, bf16[4,680,...) while((s32[]{:T(128)}, ...), condition=%wide.region_8.9_spmd.clone.clone, body=%wide.region_5.8_spmd.sunk.clone.sunk.clone | while | flops 488291680 | bytes 37862984 | solution.py:346
  233.8 5.8 fusion.125
  242.7 46.9 %mlp.1 = (f32[680,1024]{1,0:T(8,128)}, f32[680,1024]{1,0:T(8,128)}, bf16[1024,4096]{1,0:T(8,128)(2,1)}, bf16[1024,4096]{1,0:T(8,128)(2,1)}, f32[1,4096]{1,0:T(1,128)}) custom-call(bf16[680,1024]{1,0:T(8,128)(2,1)} %fusion.92.x_ref, bf16[680,1024]{1,0:T(8,128)(2,1)} %fusion.93.g_ref, bf16[1024,8192]{1,0:T(8,128)(2,1)} %all-gather.2.cloned.1.call-done.up_ref.down_ref, ...), custom_call_target="tpu_custom_call" | custom-call | flops 34225520640 | bytes 33554432 | tf_op jit(solution)/shard_map/mlp/pallas_call | solution.py:215
  289.7 4.2 fusion.71
  306.6 8.0 %dynamic-slice_bitcast_fusion.2 = (bf16[2,2,2,2,32,4096]{5,4,3,2,1,0:T(8,128)(2,1)}, bf16[2,2,2,2,32,4096]{5,4,3,2,1,0:T(8,128)(2,1)}) fusion(bf16[2,2,2,2,2,32,4096]{6,5,4,3,2,1,0:T(8,128)(2,1)} %bitcast.409, s32[]{:T(128)S(6)} %select_n.80, s32[]{:T(128)S(6)} %select_n.81), kind=kLoop, calls=%fused_computation.65 | loop fusion | bytes 16777224 | tf_op jit(solution)/shard_map/jit(dynamic_index_in_dim)/squeeze | solution.py:150
  321.5 64.9 %while.31 = (s32[]{:T(128)}, f32[4,680,4,64]{1,3,2,0:T(8,128)}, f32[4,680,4,64]{1,3,2,0:T(8,128)}, bf16[4,680,4,64]{1,3,2,0:T(8,128)(2,1)}, bf16[4,680,4,64]{1,3...) while((s32[]{:T(128)}, f32[4,680,4,64]{1,3,2,0:T(8,128)}, ...), condition=%wide.region_15.16_spmd.clone.clone, body=%wide.region_13.15_spmd.sunk.clone.sunk.clone | while | flops 1205936512 | bytes 70155080 | solution.py:376
  416.1 11.9 %fusion.69 = (bf16[680,1024]{1,0:T(8,128)(2,1)}, bf16[680,1024]{1,0:T(8,128)(2,1)}) fusion(f32[680,1024]{1,0:T(8,128)} %copy.178, f32[680,1024]{1,0:T(8,128)} %copy.177, f32[680,1024]{1,0:T(8,128)} %copy.176, f32[1024]{0:T(1024)S(1)} %copy-done.48, f32[680,3072]{1,0:T(8,128)} %copy-done.11, f32[680,1024]{1,0:T(8,128)} %copy.181, f32[680,1024]{1,0:T(8,128)} %copy.179, ...), kind=kLoop, calls=%fused_computation.106 | loop fusion | flops 7659520 | bytes 25071616 | tf_op jit(solution)/shard_map/convert.18
  428.1 9.1 %fusion.68 = (f32[680]{0:T(1024)S(1)}, f32[680,1024]{1,0:T(8,128)S(1)}) fusion(bf16[1,680,1024]{2,1,0:T(8,128)(2,1)} %param.21, f32[1024]{0:T(1024)S(1)} %bitcast.440, f32[680]{0:T(1024)S(1)} %copy-done.40, bf16[1024,2048]{1,0:T(8,128)(2,1)} %bitcast.415, bf16[1024,2048]{1,0:T(8,128)(2,1)} %bitcast.418, bf16[680,1024]{1,0:T(8,128)(2,1)} %copy.182, ...), kind=kOutput, calls=%fused_computation.105 | convolution fusion | flops 4306787840 | bytes 16753984 | tf_op jit(solution)/shard_map/re,de->rd/dot_general | solution.py:392
  444.0 7.6 %fusion.72 = (bf16[1024]{0:T(1024)(128)(2,1)S(1)}, bf16[1024]{0:T(1024)(128)(2,1)S(1)}, f32[1,680,1024]{2,1,0:T(8,128)}, bf16[1,680,1024]{2,1,0:T(8,128)(2,1)}) fusion(f32[680,1024]{1,0:T(8,128)} %get-tuple-element.109, bf16[1,680,1024]{2,1,0:T(8,128)(2,1)} %param.33, f32[680]{0:T(1024)S(1)} %compare_convert_fusion, f32[680,1024]{1,0:T(8,128)} %get-tuple-element.259, ...), kind=kLoop, calls=%fused_computation.112 | loop fusion | flops 14620672 | bytes 20918208 | tf_op jit(solution)/shard_map/reduce_sum | solution.py:366
  454.5 4.3 all-to-all-start.2
  458.8 10.4 %convolution_convert_fusion = bf16[1024,3072]{1,0:T(8,128)(2,1)} fusion(bf16[680,1024]{1,0:T(8,128)(2,1)} %copy.182, bf16[680,1024]{1,0:T(8,128)(2,1)} %get-tuple-element.230, bf16[680,1024]{1,0:T(8,128)(2,1)} %get-tuple-element.229, bf16[1,680,1024]{2,1,0:T(8,128)(2,1)S(1)} %copy-done.10, f32[1024]{0:T(1024)S(1)} %bitcast.446, f32[1024]{0:T(1024)S(1)} %bitcast.443, ...), kind=kOutput, calls=%fused_computation.61 | convolution fusion | flops 4298047488 | bytes 11875648 | tf_op jit(solution)/shard_map/rd,re->de/dot_general | solution.py:388
  469.2 7.6 %pad_maximum_fusion = bf16[1024,4096]{1,0:T(8,128)(2,1)} fusion(bf16[1024,1024]{1,0:T(8,128)(2,1)} %convolution_convert_fusion.1, bf16[1024,3072]{1,0:T(8,128)(2,1)} %convolution_convert_fusion), kind=kLoop, calls=%fused_computation.58 | loop fusion | flops 16777216 | bytes 16777216 | tf_op jit(solution)/shard_map/concatenate | solution.py:390
  476.8 7.9 %dynamic-slice_bitcast_fusion.6 = (bf16[2,2,2,2,32,4096]{5,4,3,2,1,0:T(8,128)(2,1)}, bf16[2,2,2,2,32,4096]{5,4,3,2,1,0:T(8,128)(2,1)}) fusion(bf16[2,2,2,2,2,32,4096]{6,5,4,3,2,1,0:T(8,128)(2,1)} %bitcast.398, s32[]{:T(128)S(6)} %select_n.80, s32[]{:T(128)S(6)} %select_n.81), kind=kLoop, calls=%fused_computation.73 | loop fusion | bytes 16777224 | tf_op jit(solution)/shard_map/jit(dynamic_index_in_dim)/squeeze | solution.py:150
  506.3 13.0 %collective-permute-done.23 = bf16[2,2,2,32,2048]{4,3,2,1,0:T(8,128)(2,1)S(1)} collective-permute-done((bf16[2,2,2,32,2048]{4,3,2,1,0:T(8,128)(2,1)S(1)}, bf16[2,2,2,32,2048]{4,3,2,1,0:T(8,128)(2,1)S(1)}, u32[]{:S(2)}, u32[]{:S(2)}) %collective-permute-start.23) | collective-permute-done | bytes 1048608 | tf_op jit(solution)/shard_map/ppermute | solution.py:83
  523.1 18.6 %collective-permute-done.16 = bf16[2,2,2,32,2048]{4,3,2,1,0:T(8,128)(2,1)S(1)} collective-permute-done((bf16[2,2,2,32,2048]{4,3,2,1,0:T(8,128)(2,1)S(1)}, bf16[2,2,2,32,2048]{4,3,2,1,0:T(8,128)(2,1)S(1)}, u32[]{:S(2)}, u32[]{:S(2)}) %collective-permute-start.16) | collective-permute-done | bytes 1048608 | tf_op jit(solution)/shard_map/ppermute | solution.py:83
  546.0 18.3 %collective-permute-done.9 = bf16[2,2,2,32,2048]{4,3,2,1,0:T(8,128)(2,1)S(1)} collective-permute-done((bf16[2,2,2,32,2048]{4,3,2,1,0:T(8,128)(2,1)S(1)}, bf16[2,2,2,32,2048]{4,3,2,1,0:T(8,128)(2,1)S(1)}, u32[]{:S(2)}, u32[]{:S(2)}) %collective-permute-start.9) | collective-permute-done | bytes 1048608 | tf_op jit(solution)/shard_map/ppermute | solution.py:83
  568.4 8.9 %collective-permute-done.25 = bf16[2,2,32,2048]{3,2,1,0:T(8,128)(2,1)S(1)} collective-permute-done((bf16[2,2,32,2048]{3,2,1,0:T(8,128)(2,1)S(1)}, bf16[2,2,32,2048]{3,2,1,0:T(8,128)(2,1)S(1)}, u32[]{:S(2)}, u32[]{:S(2)}) %collective-permute-start.25) | collective-permute-done | bytes 524320 | tf_op jit(solution)/shard_map/ppermute | solution.py:83
  579.8 8.8 %collective-permute-done.18 = bf16[2,2,32,2048]{3,2,1,0:T(8,128)(2,1)S(1)} collective-permute-done((bf16[2,2,32,2048]{3,2,1,0:T(8,128)(2,1)S(1)}, bf16[2,2,32,2048]{3,2,1,0:T(8,128)(2,1)S(1)}, u32[]{:S(2)}, u32[]{:S(2)}) %collective-permute-start.18) | collective-permute-done | bytes 524320 | tf_op jit(solution)/shard_map/ppermute | solution.py:83
  590.4 8.5 %collective-permute-done.11 = bf16[2,2,32,2048]{3,2,1,0:T(8,128)(2,1)S(1)} collective-permute-done((bf16[2,2,32,2048]{3,2,1,0:T(8,128)(2,1)S(1)}, bf16[2,2,32,2048]{3,2,1,0:T(8,128)(2,1)S(1)}, u32[]{:S(2)}, u32[]{:S(2)}) %collective-permute-start.11) | collective-permute-done | bytes 524320 | tf_op jit(solution)/shard_map/ppermute | solution.py:83
  604.2 19.2 %collective-permute-done.13 = bf16[2,32,4096]{2,1,0:T(8,128)(2,1)S(1)} collective-permute-done((bf16[2,32,4096]{2,1,0:T(8,128)(2,1)S(1)}, bf16[2,32,4096]{2,1,0:T(8,128)(2,1)S(1)}, u32[]{:S(2)}, u32[]{:S(2)}) %collective-permute-start.13) | collective-permute-done | bytes 524320 | tf_op jit(solution)/shard_map/ppermute | solution.py:83
  624.5 12.7 %collective-permute-done.14 = bf16[32,4096]{1,0:T(8,128)(2,1)S(1)} collective-permute-done((bf16[32,4096]{1,0:T(8,128)(2,1)S(1)}, bf16[32,4096]{1,0:T(8,128)(2,1)S(1)}, u32[]{:S(2)}, u32[]{:S(2)}) %collective-permute-start.14) | collective-permute-done | bytes 262176 | tf_op jit(solution)/shard_map/ppermute | solution.py:83
  644.1 4.4 reshape.560
  (402 shorter events, 284.9 us)
Async XLA Ops:
  7.2 235.5 %all-gather.2.cloned.1.call-start = ((), (), s32[]{:S(2)}) async-start(), calls=%async_computation.3 | async-start | bytes 17301504 | tf_op jit(solution)/shard_map/all_gather | solution.py:293
  12.4 20.7 %collective-permute-start = (bf16[1,32,4096]{2,1,0:T(8,128)(2,1)S(1)}, bf16[1,32,4096]{2,1,0:T(8,128)(2,1)S(1)}, u32[]{:S(2)}, u32[]{:S(2)}) collective-permute-start(bf16[1,32,4096]{2,1,0:T(8,128)(2,1)S(1)} %maximum_bitcast_fusion.1), channel_id=1, source_target_pairs={{0,16},{1,17},{2,18},{3,19},{4,20},{5,21},{6,22},{7,23},{8,24},{9,... | collective-permute-start | bytes 786440 | tf_op jit(solution)/shard_map/ppermute | solution.py:83
  33.2 22.8 %collective-permute-start.1 = (bf16[2,32,4096]{2,1,0:T(8,128)(2,1)S(1)}, bf16[2,32,4096]{2,1,0:T(8,128)(2,1)S(1)}, u32[]{:S(2)}, u32[]{:S(2)}) collective-permute-start(bf16[2,32,4096]{2,1,0:T(8,128)(2,1)S(1)} %pad_maximum_fusion.12), channel_id=1, source_target_pairs={{0,8},{1,9},{2,10},{3,11},{4,12},{5,13},{6,14},{7,15},{8,0},{9,1},... | collective-permute-start | bytes 1572872 | tf_op jit(solution)/shard_map/ppermute | solution.py:83
  38.4 25.0 %all-to-all-start = ((s32[32,1,1]{2,1,0:T(1,128)}), s32[32,1,1]{2,1,0:T(1,128)S(1)}, u32[]{:S(2)}, u32[]{:S(2)}) async-start(s32[32,1,1]{2,1,0:T(1,128)} %broadcast_in_dim.69), calls=%async_computation | async-start | bytes 32768 | tf_op jit(solution)/shard_map/all_to_all | solution.py:295
  56.2 19.9 %collective-permute-start.5 = (bf16[4,32,2048]{2,1,0:T(8,128)(2,1)S(1)}, bf16[4,32,2048]{2,1,0:T(8,128)(2,1)S(1)}, u32[]{:S(2)}, u32[]{:S(2)}) collective-permute-start(bf16[4,32,2048]{2,1,0:T(8,128)(2,1)S(1)} %get-tuple-element.250), channel_id=1, source_target_pairs={{0,2},{1,3},{2,0},{3,1},{4,6},{5,7},{6,4},{7,5},{8,10},{9,11},{10,... | collective-permute-start | bytes 1572872 | tf_op jit(solution)/shard_map/ppermute | solution.py:83
  64.1 14.6 %collective-permute-start.2 = (bf16[4,32,2048]{2,1,0:T(8,128)(2,1)S(1)}, bf16[4,32,2048]{2,1,0:T(8,128)(2,1)S(1)}, u32[]{:S(2)}, u32[]{:S(2)}) collective-permute-start(bf16[4,32,2048]{2,1,0:T(8,128)(2,1)S(1)} %get-tuple-element.249), channel_id=1, source_target_pairs={{0,4},{1,5},{2,6},{3,7},{4,0},{5,1},{6,2},{7,3},{8,12},{9,13},{10,... | collective-permute-start | bytes 1572872 | tf_op jit(solution)/shard_map/ppermute | solution.py:83
  77.2 44.8 %collective-permute-start.6 = (bf16[8,32,2048]{2,1,0:T(8,128)(2,1)}, bf16[8,32,2048]{2,1,0:T(8,128)(2,1)}, u32[]{:S(2)}, u32[]{:S(2)}) collective-permute-start(bf16[8,32,2048]{2,1,0:T(8,128)(2,1)} %pad_maximum_fusion.11), channel_id=1, source_target_pairs={{0,4},{1,5},{2,6},{3,7},{4,0},{5,1},{6,2},{7,3},{8,12},{9,13},{10,... | collective-permute-start | bytes 3145736 | tf_op jit(solution)/shard_map/ppermute | solution.py:83
  79.8 48.0 %collective-permute-start.3 = (bf16[8,32,2048]{2,1,0:T(8,128)(2,1)}, bf16[8,32,2048]{2,1,0:T(8,128)(2,1)}, u32[]{:S(2)}, u32[]{:S(2)}) collective-permute-start(bf16[8,32,2048]{2,1,0:T(8,128)(2,1)} %pad_maximum_fusion.10), channel_id=1, source_target_pairs={{0,2},{1,3},{2,0},{3,1},{4,6},{5,7},{6,4},{7,5},{8,10},{9,11},{10,... | collective-permute-start | bytes 3145736 | tf_op jit(solution)/shard_map/ppermute | solution.py:83
  82.2 50.0 %all-to-all-start.1 = ((f32[32,1,6272]{2,1,0:T(1,128)}), f32[32,1,6272]{2,1,0:T(1,128)}, u32[]{:S(2)}, u32[]{:S(2)}) async-start(f32[32,1,6272]{2,1,0:T(1,128)} %copy.166), calls=%async_computation.1 | async-start | bytes 1605632 | tf_op jit(solution)/shard_map/all_to_all | solution.py:310
  130.6 17.9 %collective-permute-start.4 = (bf16[16,32,2048]{2,1,0:T(8,128)(2,1)}, bf16[16,32,2048]{2,1,0:T(8,128)(2,1)}, u32[]{:S(2)}, u32[]{:S(2)}) collective-permute-start(bf16[16,32,2048]{2,1,0:T(8,128)(2,1)} %pad_maximum_fusion.5.own_ref), channel_id=1, source_target_pairs={{0,1},{1,0},{2,3},{3,2},{4,5},{5,4},{6,7},{7,6},{8,9},{9,8},{10,11... | collective-permute-start | bytes 6291464 | tf_op jit(solution)/shard_map/ppermute | solution.py:83
  314.6 175.4 %collective-permute-start.22 = (bf16[2,2,2,2,32,4096]{5,4,3,2,1,0:T(8,128)(2,1)}, bf16[2,2,2,2,32,4096]{5,4,3,2,1,0:T(8,128)(2,1)}, u32[]{:S(2)}, u32[]{:S(2)}) collective-permute-start(bf16[2,2,2,2,32,4096]{5,4,3,2,1,0:T(8,128)(2,1)} %get-tuple-element.220), channel_id=1, source_target_pairs={{0,1},{1,0},{2,3},{3,2},{4,5},{5,4},{6,7},{7,6},{8,9},{9,8},{10,11... | collective-permute-start | bytes 12582920 | tf_op jit(solution)/shard_map/ppermute | solution.py:83
  318.9 177.8 %collective-permute-start.15 = (bf16[2,2,2,2,32,4096]{5,4,3,2,1,0:T(8,128)(2,1)}, bf16[2,2,2,2,32,4096]{5,4,3,2,1,0:T(8,128)(2,1)}, u32[]{:S(2)}, u32[]{:S(2)}) collective-permute-start(bf16[2,2,2,2,32,4096]{5,4,3,2,1,0:T(8,128)(2,1)} %get-tuple-element.224), channel_id=1, source_target_pairs={{0,1},{1,0},{2,3},{3,2},{4,5},{5,4},{6,7},{7,6},{8,9},{9,8},{10,11... | collective-permute-start | bytes 12582920 | tf_op jit(solution)/shard_map/ppermute | solution.py:83
  454.5 30.6 %all-to-all-start.2 = ((bf16[32,2,3216]{2,1,0:T(2,128)(2,1)}), bf16[32,2,3216]{2,1,0:T(2,128)(2,1)S(1)}, u32[]{:S(2)}, u32[]{:S(2)}) async-start(bf16[32,2,3216]{2,1,0:T(2,128)(2,1)} %reshape.592), calls=%async_computation.2 | async-start | bytes 851968 | tf_op jit(solution)/shard_map/all_to_all | solution.py:416
  484.7 17.3 %collective-permute-start.8 = (bf16[2,2,2,2,32,4096]{5,4,3,2,1,0:T(8,128)(2,1)}, bf16[2,2,2,2,32,4096]{5,4,3,2,1,0:T(8,128)(2,1)}, u32[]{:S(2)}, u32[]{:S(2)}) collective-permute-start(bf16[2,2,2,2,32,4096]{5,4,3,2,1,0:T(8,128)(2,1)} %get-tuple-element.228), channel_id=1, source_target_pairs={{0,1},{1,0},{2,3},{3,2},{4,5},{5,4},{6,7},{7,6},{8,9},{9,8},{10,11... | collective-permute-start | bytes 12582920 | tf_op jit(solution)/shard_map/ppermute | solution.py:83
  493.2 26.0 %collective-permute-start.23 = (bf16[2,2,2,32,2048]{4,3,2,1,0:T(8,128)(2,1)S(1)}, bf16[2,2,2,32,2048]{4,3,2,1,0:T(8,128)(2,1)S(1)}, u32[]{:S(2)}, u32[]{:S(2)}) collective-permute-start(bf16[2,2,2,32,2048]{4,3,2,1,0:T(8,128)(2,1)S(1)} %dynamic-slice_bitcast_fusion.8), channel_id=1, source_target_pairs={{0,2},{1,3},{2,0},{3,1},{4,6},{5,7},{6,4},{7,5},{8,10},{9,11},{10,... | collective-permute-start | bytes 3145736 | tf_op jit(solution)/shard_map/ppermute | solution.py:83
  495.1 26.4 %collective-permute-start.24 = (bf16[2,2,2,32,2048]{4,3,2,1,0:T(8,128)(2,1)S(1)}, bf16[2,2,2,32,2048]{4,3,2,1,0:T(8,128)(2,1)S(1)}, u32[]{:S(2)}, u32[]{:S(2)}) collective-permute-start(bf16[2,2,2,32,2048]{4,3,2,1,0:T(8,128)(2,1)S(1)} %dynamic-slice_bitcast_fusion.7), channel_id=1, source_target_pairs={{0,4},{1,5},{2,6},{3,7},{4,0},{5,1},{6,2},{7,3},{8,12},{9,13},{10,... | collective-permute-start | bytes 3145736 | tf_op jit(solution)/shard_map/ppermute | solution.py:83
  499.9 41.8 %collective-permute-start.16 = (bf16[2,2,2,32,2048]{4,3,2,1,0:T(8,128)(2,1)S(1)}, bf16[2,2,2,32,2048]{4,3,2,1,0:T(8,128)(2,1)S(1)}, u32[]{:S(2)}, u32[]{:S(2)}) collective-permute-start(bf16[2,2,2,32,2048]{4,3,2,1,0:T(8,128)(2,1)S(1)} %dynamic-slice_bitcast_fusion.10), channel_id=1, source_target_pairs={{0,2},{1,3},{2,0},{3,1},{4,6},{5,7},{6,4},{7,5},{8,10},{9,11},{10,... | collective-permute-start | bytes 3145736 | tf_op jit(solution)/shard_map/ppermute | solution.py:83
  500.6 43.3 %collective-permute-start.17 = (bf16[2,2,2,32,2048]{4,3,2,1,0:T(8,128)(2,1)S(1)}, bf16[2,2,2,32,2048]{4,3,2,1,0:T(8,128)(2,1)S(1)}, u32[]{:S(2)}, u32[]{:S(2)}) collective-permute-start(bf16[2,2,2,32,2048]{4,3,2,1,0:T(8,128)(2,1)S(1)} %dynamic-slice_bitcast_fusion.9), channel_id=1, source_target_pairs={{0,4},{1,5},{2,6},{3,7},{4,0},{5,1},{6,2},{7,3},{8,12},{9,13},{10,... | collective-permute-start | bytes 3145736 | tf_op jit(solution)/shard_map/ppermute | solution.py:83
  505.4 58.8 %collective-permute-start.9 = (bf16[2,2,2,32,2048]{4,3,2,1,0:T(8,128)(2,1)S(1)}, bf16[2,2,2,32,2048]{4,3,2,1,0:T(8,128)(2,1)S(1)}, u32[]{:S(2)}, u32[]{:S(2)}) collective-permute-start(bf16[2,2,2,32,2048]{4,3,2,1,0:T(8,128)(2,1)S(1)} %dynamic-slice_bitcast_fusion.12), channel_id=1, source_target_pairs={{0,2},{1,3},{2,0},{3,1},{4,6},{5,7},{6,4},{7,5},{8,10},{9,11},{10,... | collective-permute-start | bytes 3145736 | tf_op jit(solution)/shard_map/ppermute | solution.py:83
  519.3 47.1 %collective-permute-start.10 = (bf16[2,2,2,32,2048]{4,3,2,1,0:T(8,128)(2,1)S(1)}, bf16[2,2,2,32,2048]{4,3,2,1,0:T(8,128)(2,1)S(1)}, u32[]{:S(2)}, u32[]{:S(2)}) collective-permute-start(bf16[2,2,2,32,2048]{4,3,2,1,0:T(8,128)(2,1)S(1)} %dynamic-slice_bitcast_fusion.11), channel_id=1, source_target_pairs={{0,4},{1,5},{2,6},{3,7},{4,0},{5,1},{6,2},{7,3},{8,12},{9,13},{10,... | collective-permute-start | bytes 3145736 | tf_op jit(solution)/shard_map/ppermute | solution.py:83
  521.5 55.9 %collective-permute-start.25 = (bf16[2,2,32,2048]{3,2,1,0:T(8,128)(2,1)S(1)}, bf16[2,2,32,2048]{3,2,1,0:T(8,128)(2,1)S(1)}, u32[]{:S(2)}, u32[]{:S(2)}) collective-permute-start(bf16[2,2,32,2048]{3,2,1,0:T(8,128)(2,1)S(1)} %get-tuple-element.237), channel_id=1, source_target_pairs={{0,4},{1,5},{2,6},{3,7},{4,0},{5,1},{6,2},{7,3},{8,12},{9,13},{10,... | collective-permute-start | bytes 1572872 | tf_op jit(solution)/shard_map/ppermute | solution.py:83
  541.8 35.9 %collective-permute-start.26 = (bf16[2,2,32,2048]{3,2,1,0:T(8,128)(2,1)S(1)}, bf16[2,2,32,2048]{3,2,1,0:T(8,128)(2,1)S(1)}, u32[]{:S(2)}, u32[]{:S(2)}) collective-permute-start(bf16[2,2,32,2048]{3,2,1,0:T(8,128)(2,1)S(1)} %get-tuple-element.239), channel_id=1, source_target_pairs={{0,2},{1,3},{2,0},{3,1},{4,6},{5,7},{6,4},{7,5},{8,10},{9,11},{10,... | collective-permute-start | bytes 1572872 | tf_op jit(solution)/shard_map/ppermute | solution.py:83
  544.0 44.6 %collective-permute-start.18 = (bf16[2,2,32,2048]{3,2,1,0:T(8,128)(2,1)S(1)}, bf16[2,2,32,2048]{3,2,1,0:T(8,128)(2,1)S(1)}, u32[]{:S(2)}, u32[]{:S(2)}) collective-permute-start(bf16[2,2,32,2048]{3,2,1,0:T(8,128)(2,1)S(1)} %get-tuple-element.241), channel_id=1, source_target_pairs={{0,4},{1,5},{2,6},{3,7},{4,0},{5,1},{6,2},{7,3},{8,12},{9,13},{10,... | collective-permute-start | bytes 1572872 | tf_op jit(solution)/shard_map/ppermute | solution.py:83
  564.2 24.4 %collective-permute-start.19 = (bf16[2,2,32,2048]{3,2,1,0:T(8,128)(2,1)S(1)}, bf16[2,2,32,2048]{3,2,1,0:T(8,128)(2,1)S(1)}, u32[]{:S(2)}, u32[]{:S(2)}) collective-permute-start(bf16[2,2,32,2048]{3,2,1,0:T(8,128)(2,1)S(1)} %get-tuple-element.243), channel_id=1, source_target_pairs={{0,2},{1,3},{2,0},{3,1},{4,6},{5,7},{6,4},{7,5},{8,10},{9,11},{10,... | collective-permute-start | bytes 1572872 | tf_op jit(solution)/shard_map/ppermute | solution.py:83
  566.4 32.5 %collective-permute-start.11 = (bf16[2,2,32,2048]{3,2,1,0:T(8,128)(2,1)S(1)}, bf16[2,2,32,2048]{3,2,1,0:T(8,128)(2,1)S(1)}, u32[]{:S(2)}, u32[]{:S(2)}) collective-permute-start(bf16[2,2,32,2048]{3,2,1,0:T(8,128)(2,1)S(1)} %get-tuple-element.245), channel_id=1, source_target_pairs={{0,4},{1,5},{2,6},{3,7},{4,0},{5,1},{6,2},{7,3},{8,12},{9,13},{10,... | collective-permute-start | bytes 1572872 | tf_op jit(solution)/shard_map/ppermute | solution.py:83
  577.4 21.6 %collective-permute-start.12 = (bf16[2,2,32,2048]{3,2,1,0:T(8,128)(2,1)S(1)}, bf16[2,2,32,2048]{3,2,1,0:T(8,128)(2,1)S(1)}, u32[]{:S(2)}, u32[]{:S(2)}) collective-permute-start(bf16[2,2,32,2048]{3,2,1,0:T(8,128)(2,1)S(1)} %get-tuple-element.247), channel_id=1, source_target_pairs={{0,2},{1,3},{2,0},{3,1},{4,6},{5,7},{6,4},{7,5},{8,10},{9,11},{10,... | collective-permute-start | bytes 1572872 | tf_op jit(solution)/shard_map/ppermute | solution.py:83
  578.0 22.8 %collective-permute-start.27 = (bf16[2,32,4096]{2,1,0:T(8,128)(2,1)S(1)}, bf16[2,32,4096]{2,1,0:T(8,128)(2,1)S(1)}, u32[]{:S(2)}, u32[]{:S(2)}) collective-permute-start(bf16[2,32,4096]{2,1,0:T(8,128)(2,1)S(1)} %dynamic-slice_bitcast_fusion.13), channel_id=1, source_target_pairs={{0,8},{1,9},{2,10},{3,11},{4,12},{5,13},{6,14},{7,15},{8,0},{9,1},... | collective-permute-start | bytes 1572872 | tf_op jit(solution)/shard_map/ppermute | solution.py:83
  588.9 14.6 %collective-permute-start.20 = (bf16[2,32,4096]{2,1,0:T(8,128)(2,1)S(1)}, bf16[2,32,4096]{2,1,0:T(8,128)(2,1)S(1)}, u32[]{:S(2)}, u32[]{:S(2)}) collective-permute-start(bf16[2,32,4096]{2,1,0:T(8,128)(2,1)S(1)} %dynamic-slice_bitcast_fusion.18), channel_id=1, source_target_pairs={{0,8},{1,9},{2,10},{3,11},{4,12},{5,13},{6,14},{7,15},{8,0},{9,1},... | collective-permute-start | bytes 1572872 | tf_op jit(solution)/shard_map/ppermute | solution.py:83
  599.3 24.2 %collective-permute-start.13 = (bf16[2,32,4096]{2,1,0:T(8,128)(2,1)S(1)}, bf16[2,32,4096]{2,1,0:T(8,128)(2,1)S(1)}, u32[]{:S(2)}, u32[]{:S(2)}) collective-permute-start(bf16[2,32,4096]{2,1,0:T(8,128)(2,1)S(1)} %dynamic-slice_bitcast_fusion.23), channel_id=1, source_target_pairs={{0,8},{1,9},{2,10},{3,11},{4,12},{5,13},{6,14},{7,15},{8,0},{9,1},... | collective-permute-start | bytes 1572872 | tf_op jit(solution)/shard_map/ppermute | solution.py:83
  601.0 23.5 %collective-permute-start.28 = (bf16[32,4096]{1,0:T(8,128)(2,1)S(1)}, bf16[32,4096]{1,0:T(8,128)(2,1)S(1)}, u32[]{:S(2)}, u32[]{:S(2)}) collective-permute-start(bf16[32,4096]{1,0:T(8,128)(2,1)S(1)} %dynamic-slice_bitcast_fusion.28), channel_id=1, source_target_pairs={{0,16},{1,17},{2,18},{3,19},{4,20},{5,21},{6,22},{7,23},{8,24},{9,... | collective-permute-start | bytes 786440 | tf_op jit(solution)/shard_map/ppermute | solution.py:83
  603.6 36.6 %collective-permute-start.21 = (bf16[32,4096]{1,0:T(8,128)(2,1)S(1)}, bf16[32,4096]{1,0:T(8,128)(2,1)S(1)}, u32[]{:S(2)}, u32[]{:S(2)}) collective-permute-start(bf16[32,4096]{1,0:T(8,128)(2,1)S(1)} %dynamic-slice_bitcast_fusion.29), channel_id=1, source_target_pairs={{0,16},{1,17},{2,18},{3,19},{4,20},{5,21},{6,22},{7,23},{8,24},{9,... | collective-permute-start | bytes 786440 | tf_op jit(solution)/shard_map/ppermute | solution.py:83
  623.6 13.6 %collective-permute-start.14 = (bf16[32,4096]{1,0:T(8,128)(2,1)S(1)}, bf16[32,4096]{1,0:T(8,128)(2,1)S(1)}, u32[]{:S(2)}, u32[]{:S(2)}) collective-permute-start(bf16[32,4096]{1,0:T(8,128)(2,1)S(1)} %dynamic-slice_bitcast_fusion.30), channel_id=1, source_target_pairs={{0,16},{1,17},{2,18},{3,19},{4,20},{5,21},{6,22},{7,23},{8,24},{9,... | collective-permute-start | bytes 786440 | tf_op jit(solution)/shard_map/ppermute | solution.py:83
  (76 other events, 651.9 us)
Sparse Core Ops, SparseCore 0:
  11.7 152.1 all-gather.1

commit v2 on v1

v2 whole, which is shorter than its diff:
```python
from functools import partial

import jax
import jax.numpy as jnp
import numpy as np
from jax import lax
from jax.experimental import pallas as pl
from jax.experimental.pallas import tpu as pltpu
from jax.sharding import PartitionSpec as P

HDIM = 64
SCALES = 10
AXES = ("wide", "narrow")
BF = jnp.bfloat16
F32 = jnp.float32

scale_sides = (1, 2, 3, 4, 5, 6, 8, 10, 13, 16)


def position_scale(scale_count):
    return np.concatenate(
        [
            np.full(side_size * side_size, level_index, dtype=np.int32)
            for level_index, side_size in enumerate(scale_sides[:scale_count])
        ]
    )


BLOCKS = 32
LEVEL_ENDS = np.cumsum(np.square(np.array(scale_sides))).astype(np.int32)
LAST = (((1,), (1,)), ((), ()))
FIRST = (((0,), (0,)), ((), ()))
PARAMS = pltpu.CompilerParams(vmem_limit_bytes=58 << 20)


def dot(left, right, dims=(((1,), (0,)), ((), ()))):
    return lax.dot_general(left, right, dims, preferred_element_type=F32)


def split_low(value):
    high = value.astype(BF)
    return high, (value - high.astype(F32)).astype(BF)


def row_chunks(total, step=80):
    return [slice(i, min(i + step, total)) for i in range(0, total, step)]


def norm_parts(value):
    centred = value - jnp.mean(value, axis=-1, keepdims=True)
    inverse = lax.rsqrt(jnp.mean(centred * centred, axis=-1, keepdims=True) + 1e-06)
    return centred * inverse, inverse


def cost(flops, read, exps=0, scale=20):
    return pl.CostEstimate(flops=int(scale * flops), bytes_accessed=int(scale * read), transcendentals=int(scale * exps))


def whole(shape):
    return pl.BlockSpec(shape, lambda *_: (0,) * len(shape))


def fill(dst, code, own, other, block):
    for m in range(own.shape[0]):
        at = code[m]
        dst[pl.ds(pl.multiple_of(at * block, block), block), :] = own[m]
        at = at ^ 1
        dst[pl.ds(pl.multiple_of(at * block, block), block), :] = other[m]


def halves_of(value, core, count=None):
    rows, cols = value.shape
    block = rows // (count or BLOCKS)
    cut = value.reshape(rows // (2 * block), 2, block, cols)
    even, odd = cut[:, 0], cut[:, 1]
    return (
        jnp.where(core == 0, even, odd).astype(BF),
        jnp.where(core == 0, odd, even).astype(BF),
    )


def qkv_body(
    code_ref, x_ref, mod_ref, own_a, other_a, own_b, other_b, gain_ref, seg_ref,
    attn_ref, out_ref, inv_ref, w_ref,
):
    step = pl.program_id(0)
    block = own_a.shape[1]

    @pl.when(step == 0)
    def _():
        for rows in row_chunks(x_ref.shape[0]):
            unit, _ = norm_parts(x_ref[rows, :].astype(F32))
            attn_ref[rows, :] = (unit * (1.0 + mod_ref[2:3, :]) + mod_ref[4:5, :]).astype(BF)

    @pl.when(step < 2)
    def _():
        fill(w_ref, code_ref.at[0], own_a, other_a, block)
        raw = dot(attn_ref[...], w_ref[...])
        seg = seg_ref[...]
        high, low = split_low(raw * raw)
        inverse = lax.rsqrt(dot(high, seg) + dot(low, seg) + 1e-06)
        high, low = split_low(inverse)
        spread = dot(high, seg, LAST) + dot(low, seg, LAST)
        gain = jnp.where(step == 0, gain_ref[...], 1.0)
        out_ref[...] = (raw * spread * gain).astype(BF)
        inv_ref[...] = spread

    @pl.when(step >= 2)
    def _():
        fill(w_ref, code_ref.at[1], own_b, other_b, block)

    @pl.when(step == 2)
    def _():
        out_ref[...] = dot(attn_ref[...], w_ref[...]).astype(BF)


def qkv_rows(x, mod, pieces, gain, seg):
    tokens, width = x.shape
    code, own_a, other_a, own_b, other_b = pieces
    part = (own_a.shape[0], own_a.shape[1], width)
    first = pl.BlockSpec(part, lambda n: (0, 0, jnp.minimum(n, 1)))
    second = pl.BlockSpec(part, lambda n: (0, 0, jnp.maximum(n - 2, 0)))
    return pl.pallas_call(
        qkv_body,
        grid=(4,),
        in_specs=[
            pl.BlockSpec(memory_space=pltpu.SMEM),
            whole((tokens, width)),
            whole(mod.shape),
            first,
            first,
            second,
            second,
            whole(gain.shape),
            whole(seg.shape),
        ],
        out_specs=[
            whole((tokens, width)),
            pl.BlockSpec((tokens, width), lambda n: (0, jnp.minimum(n, 2))),
            pl.BlockSpec((tokens, width), lambda n: (0, jnp.minimum(n, 1))),
            pl.BlockSpec((width, width), lambda n: (0, n)),
        ],
        out_shape=[
            jax.ShapeDtypeStruct((tokens, width), BF),
            jax.ShapeDtypeStruct((tokens, 3 * width), BF),
            jax.ShapeDtypeStruct((tokens, 2 * width), F32),
            jax.ShapeDtypeStruct((width, 4 * width), BF),
        ],
        compiler_params=PARAMS,
        cost_estimate=cost(6 * tokens * width * width, 16 * tokens * width + 16 * width * width, 0, 1),
        name="qkv",
    )(code, x, mod, own_a, other_a, own_b, other_b, gain, seg)


def attend_body(q_ref, k_ref, v_ref, start_ref, out_ref, low_ref, inv_ref):
    q, k, v = q_ref[...], k_ref[...], v_ref[...]
    lane = lax.broadcasted_iota(jnp.int32, q.shape, 1)
    zero = jnp.zeros_like(q)
    one = jnp.ones_like(q)
    tokens = q.shape[0]
    queries = [jnp.where(lane < HDIM, q, zero), jnp.where(lane >= HDIM, q, zero)]
    values = [
        jnp.where(lane < HDIM, v, jnp.where(lane == HDIM, one, zero)),
        jnp.where(lane >= HDIM, v, jnp.where(lane == 0, one, zero)),
    ]
    for first, last, keys in ((0, 240, 256), (240, 416, 432), (416, tokens, tokens)):
        row = lax.broadcasted_iota(jnp.int32, (last - first, keys), 0) + first
        seen = row >= start_ref[:, :keys]
        tiles, sums = [], []
        for h in range(2):
            score = dot(queries[h][first:last], k[:keys], LAST)
            weight = jnp.where(seen, jnp.exp(score), 0.0).astype(BF)
            tile = dot(weight, values[h][:keys])
            inverse = 1.0 / tile[:, HDIM * (1 - h) : HDIM * (1 - h) + 1]
            tiles.append(tile * inverse)
            sums.append(jnp.broadcast_to(inverse, tile.shape))
        left = lane[first:last] < HDIM
        high, low = split_low(jnp.where(left, tiles[0], tiles[1]))
        out_ref[first:last, :] = high
        low_ref[first:last, :] = low
        inv_ref[first:last, :] = jnp.where(left, sums[0], sums[1])


def attend(qkv, start):
    tokens = qkv.shape[0]
    pairs = qkv.shape[1] // (6 * HDIM)
    pair = lambda base: pl.BlockSpec((tokens, 2 * HDIM), lambda p: (0, base + p))
    return pl.pallas_call(
        attend_body,
        grid=(pairs,),
        in_specs=[pair(0), pair(pairs), pair(2 * pairs), whole(start.shape)],
        out_specs=[pair(0), pair(0), pair(0)],
        out_shape=[
            jax.ShapeDtypeStruct((tokens, 2 * HDIM * pairs), BF),
            jax.ShapeDtypeStruct((tokens, 2 * HDIM * pairs), BF),
            jax.ShapeDtypeStruct((tokens, 2 * HDIM * pairs), F32),
        ],
        compiler_params=PARAMS,
        cost_estimate=cost(
            16 * pairs * tokens * tokens * HDIM, 20 * tokens * HDIM * pairs, 2 * pairs * tokens * tokens, 1
        ),
        name="attend",
    )(qkv, qkv, qkv, start)


def attend_back_body(
    q_ref, k_ref, v_ref, g_ref, att_ref, low_ref, inv_ref, rq_ref, rk_ref, gain_ref, limit_ref,
    grad_ref, hs_ref, acc_q, acc_k, acc_v,
):
    q, k, v = q_ref[...], k_ref[...], v_ref[...]
    tokens = q.shape[0]
    lane = lax.broadcasted_iota(jnp.int32, q.shape, 1)
    zero, one = jnp.zeros_like(q), jnp.ones_like(q)
    left = lane < HDIM

    def head_sums(value):
        first = jnp.sum(jnp.where(left, value, 0.0), axis=1, keepdims=True)
        second = jnp.sum(jnp.where(left, 0.0, value), axis=1, keepdims=True)
        return first, second

    scaled = (g_ref[...].astype(F32) * inv_ref[...]).astype(BF)
    fine = att_ref[...].astype(F32) + low_ref[...].astype(F32)
    inner = head_sums(scaled.astype(F32) * fine)
    acc_q[...] = jnp.zeros_like(acc_q)
    for h in range(2):
        mine = left if h == 0 else lane >= HDIM
        spare = HDIM * (1 - h)
        q_own = jnp.where(mine, q, zero)
        k_own = jnp.where(mine, k, zero)
        g_own = jnp.where(mine, scaled, zero)
        high, low = split_low(-inner[h])
        wide = q.shape
        g_more = jnp.where(
            lane == spare,
            jnp.broadcast_to(high, wide),
            jnp.where(lane == spare + 1, jnp.broadcast_to(low, wide), g_own),
        )
        v_more = jnp.where(mine, v, jnp.where((lane >= spare) & (lane < spare + 2), one, zero))
        for first, last, row in ((0, 256, 0), (256, 432, 128), (432, tokens, 384)):
            score = dot(k[first:last], q_own[row:], LAST)
            key = lax.broadcasted_iota(jnp.int32, score.shape, 0) + first
            weight = jnp.where(key < limit_ref[:, row:], jnp.exp(score), 0.0).astype(BF)
            slope = dot(v_more[first:last], g_more[row:], LAST)
            slope = (weight.astype(F32) * slope).astype(BF)
            dv = dot(weight, g_own[row:])
            dk = dot(slope, q_own[row:])
            if h == 0:
                acc_v[first:last, :] = dv
                acc_k[first:last, :] = dk
            else:
                acc_v[first:last, :] += dv
                acc_k[first:last, :] += dk
            acc_q[row:, :] += dot(slope, k_own[first:last], FIRST)
    gain = gain_ref[...]
    dq, dk = acc_q[...], acc_k[...]
    q, k = q.astype(F32), k.astype(F32)
    along = dq * q
    first, second = head_sums(along)
    grad_ref[0] = (
        rq_ref[...] * (dq * gain - q * (jnp.where(left, first, second) / gain))
    ).astype(BF)
    hs_ref[...] = jnp.broadcast_to(jnp.sum(along, axis=0, keepdims=True), hs_ref.shape)
    first, second = head_sums(dk * k)
    grad_ref[1] = (rk_ref[...] * (dk - k * jnp.where(left, first, second))).astype(BF)
    grad_ref[2] = acc_v[...].astype(BF)


def attend_back(qkv, grad, attended, low, inverse, norms, gain, limit, base, some):
    tokens = qkv.shape[0]
    pairs = qkv.shape[1] // (6 * HDIM)
    pair = lambda at: pl.BlockSpec((tokens, 2 * HDIM), lambda p: (0, at + base + p))
    return pl.pallas_call(
        attend_back_body,
        grid=(some,),
        in_specs=[
            pair(0),
            pair(pairs),
            pair(2 * pairs),
            pair(0),
            pair(0),
            pair(0),
            pair(0),
            pair(0),
            pair(pairs),
            pl.BlockSpec((1, 2 * HDIM), lambda p: (0, base + p)),
            whole(limit.shape),
        ],
        out_specs=[
            pl.BlockSpec((3, tokens, 2 * HDIM), lambda p: (0, 0, p)),
            pl.BlockSpec((8, 2 * HDIM), lambda p: (0, p)),
        ],
        out_shape=[
            jax.ShapeDtypeStruct((3, tokens, 2 * HDIM * some), BF),
            jax.ShapeDtypeStruct((8, 2 * HDIM * some), F32),
        ],
        scratch_shapes=[pltpu.VMEM((tokens, 2 * HDIM), F32)] * 3,
        compiler_params=PARAMS,
        cost_estimate=cost(
            40 * some * tokens * tokens * HDIM, 60 * tokens * HDIM * some, 2 * some * tokens * tokens
        ),
        name="attend_back",
    )(qkv, qkv, qkv, grad, attended, low, inverse, norms, norms, gain, limit)


def project_body(live_ref, x_ref, att_ref, w_ref, mod_ref, cot_ref, proj_ref, mlp_ref, grad_ref):
    proj_ref[...] = dot(att_ref[...], w_ref[...])
    for rows in row_chunks(x_ref.shape[0]):
        residual = x_ref[rows, :].astype(F32) + mod_ref[0:1, :] * proj_ref[rows, :]
        unit, _ = norm_parts(residual)
        mlp_ref[rows, :] = (unit * (1.0 + mod_ref[3:4, :]) + mod_ref[5:6, :]).astype(BF)
        at = lax.broadcasted_iota(jnp.int32, residual.shape, 0) + rows.start
        live = jnp.where(at < live_ref[0], 1.0, 0.0)
        grad_ref[rows, :] = (mod_ref[1:2, :] * (cot_ref[rows, :].astype(F32) * live)).astype(BF)


def project(live, x, attended, w_vo, mod, cot):
    tokens, width = x.shape
    full = whole((tokens, width))
    return pl.pallas_call(
        project_body,
        grid=(1,),
        in_specs=[
            pl.BlockSpec(memory_space=pltpu.SMEM),
            full,
            full,
            pl.BlockSpec((width, width), lambda _: (0, 3)),
            whole(mod.shape),
            full,
        ],
        out_specs=[full] * 3,
        out_shape=[jax.ShapeDtypeStruct((tokens, width), t) for t in (F32, BF, BF)],
        compiler_params=PARAMS,
        cost_estimate=cost(2 * tokens * width * width, 14 * tokens * width + 2 * width * width, 0, 1),
        name="project",
    )(live, x, attended, w_vo, mod, cot)


def residual_back_body(
    live_ref, x_ref, proj_ref, out_ref, gx_ref, cot_ref, mod_ref, w_ref,
    block_ref, resid_ref, gatt_ref, gproj, sums_ref,
):
    totals = [0.0] * 4
    for rows in row_chunks(x_ref.shape[0]):
        proj, mlp_out, g = proj_ref[rows, :], out_ref[rows, :], gx_ref[rows, :]
        residual = x_ref[rows, :].astype(F32) + mod_ref[0:1, :] * proj
        at = lax.broadcasted_iota(jnp.int32, residual.shape, 0) + rows.start
        live = jnp.where(at < live_ref[0], 1.0, 0.0)
        block_ref[rows, :] = ((residual + mod_ref[1:2, :] * mlp_out) * live).astype(BF)
        grad_out = cot_ref[rows, :].astype(F32) * live
        unit, inverse = norm_parts(residual)
        dn = g * (1.0 + mod_ref[3:4, :])
        mean_dn = jnp.mean(dn, axis=-1, keepdims=True)
        mean_in = jnp.mean(dn * unit, axis=-1, keepdims=True)
        grad_resid = grad_out + inverse * (dn - mean_dn - unit * mean_in)
        resid_ref[rows, :] = grad_resid
        gproj[rows, :] = (mod_ref[0:1, :] * grad_resid).astype(BF)
        for i, part in enumerate((grad_resid * proj, grad_out * mlp_out, g * unit, g)):
            totals[i] = totals[i] + jnp.sum(part, axis=0, keepdims=True)
    for i in range(4):
        sums_ref[i : i + 1, :] = totals[i]
    sums_ref[4:, :] = jnp.zeros((4, sums_ref.shape[1]), F32)
    gatt_ref[...] = dot(gproj[...], w_ref[...], LAST).astype(BF)


def residual_back(live, x, proj, mlp_out, gx, cot, mod, weights):
    tokens, width = x.shape
    full = whole((tokens, width))
    return pl.pallas_call(
        residual_back_body,
        grid=(1,),
        in_specs=[
            pl.BlockSpec(memory_space=pltpu.SMEM),
            full,
            full,
            full,
            full,
            full,
            whole(mod.shape),
            pl.BlockSpec((width, width), lambda _: (0, 3)),
        ],
        out_specs=[full, full, full, full, whole((8, width))],
        out_shape=[jax.ShapeDtypeStruct((tokens, width), t) for t in (BF, F32, BF, BF)]
        + [jax.ShapeDtypeStruct((8, width), F32)],
        compiler_params=PARAMS,
        cost_estimate=cost(2 * tokens * width * width, 28 * tokens * width + 4 * width * width),
        name="residual_back",
    )(live, x, proj, mlp_out, gx, cot, mod, weights)


def weight_grad_body(core_ref, x_ref, g_ref, att_ref, proj_ref, keep_a, send_a, keep_b, send_b):
    step = pl.program_id(0)
    core = core_ref[0]

    @pl.when(step < 2)
    def _():
        keep_a[...], send_a[...] = halves_of(dot(x_ref[...], g_ref[0], FIRST), core)

    @pl.when(step == 2)
    def _():
        keep_b[...], send_b[...] = halves_of(dot(x_ref[...], g_ref[0], FIRST), core)

    @pl.when(step == 3)
    def _():
        keep_b[...], send_b[...] = halves_of(dot(att_ref[...], proj_ref[...], FIRST), core)


def weight_grad(core, x, g, attended, grad_proj):
    tokens, width = x.shape
    full = whole((tokens, width))
    part = (BLOCKS // 2, width // BLOCKS, width)
    first = pl.BlockSpec(part, lambda n: (0, 0, jnp.minimum(n, 1)))
    second = pl.BlockSpec(part, lambda n: (0, 0, jnp.maximum(n - 2, 0)))
    return pl.pallas_call(
        weight_grad_body,
        grid=(4,),
        in_specs=[
            pl.BlockSpec(memory_space=pltpu.SMEM),
            full,
            pl.BlockSpec((1, tokens, width), lambda n: (jnp.minimum(n, 2), 0, 0)),
            full,
            full,
        ],
        out_specs=[first, first, second, second],
        out_shape=[jax.ShapeDtypeStruct(part[:2] + (2 * width,), BF)] * 4,
        compiler_params=PARAMS,
        cost_estimate=cost(8 * tokens * width * width, 12 * tokens * width + 8 * width * width),
        name="weight_grad",
    )(core, x, g, attended, grad_proj)


def input_back_body(x_ref, resid_ref, mod_ref, g_ref, w_ref, out_ref, sums_ref):
    step = pl.program_id(0)
    part = dot(g_ref[0], w_ref[...], LAST)

    @pl.when(step == 0)
    def _():
        out_ref[...] = part

    @pl.when(step > 0)
    def _():
        out_ref[...] += part

    @pl.when(step == 2)
    def _():
        totals = [0.0] * 2
        for rows in row_chunks(x_ref.shape[0]):
            g = out_ref[rows, :]
            unit, inverse = norm_parts(x_ref[rows, :].astype(F32))
            dn = g * (1.0 + mod_ref[2:3, :])
            mean_dn = jnp.mean(dn, axis=-1, keepdims=True)
            mean_in = jnp.mean(dn * unit, axis=-1, keepdims=True)
            out_ref[rows, :] = resid_ref[rows, :] + inverse * (dn - mean_dn - unit * mean_in)
            for i, part in enumerate((g * unit, g)):
                totals[i] = totals[i] + jnp.sum(part, axis=0, keepdims=True)
        for i in range(2):
            sums_ref[i : i + 1, :] = totals[i]
        sums_ref[2:, :] = jnp.zeros((6, x_ref.shape[1]), F32)


def input_back(x, resid, mod, g, weights):
    tokens, width = x.shape
    full = whole((tokens, width))
    return pl.pallas_call(
        input_back_body,
        grid=(3,),
        in_specs=[
            full,
            full,
            whole(mod.shape),
            pl.BlockSpec((1, tokens, width), lambda n: (n, 0, 0)),
            pl.BlockSpec((width, width), lambda n: (0, n)),
        ],
        out_specs=[full, whole((8, width))],
        out_shape=[
            jax.ShapeDtypeStruct((tokens, width), F32),
            jax.ShapeDtypeStruct((8, width), F32),
        ],
        compiler_params=PARAMS,
        cost_estimate=cost(6 * tokens * width * width, 16 * tokens * width + 6 * width * width),
        name="input_back",
    )(x, resid, mod, g, weights)


def mlp_body(
    info_ref, x_ref, g_ref, own_a, other_a, own_b, other_b, bias_ref, *refs, first
):
    if first:
        out_ref, gx_ref, keep_a, send_a, keep_b, send_b, bias_g, up_w, down_w = refs
    else:
        out_in, gx_in, out_ref, gx_ref, keep_a, send_a, keep_b, send_b, bias_g, up_w, down_w = refs
    core = info_ref[2, 0]
    block = own_a.shape[1]

    @pl.when(pl.program_id(0) == 0)
    def _():
        out_ref[...] = jnp.zeros_like(out_ref) if first else out_in[...]
        gx_ref[...] = jnp.zeros_like(gx_ref) if first else gx_in[...]

    step = pl.program_id(0)
    size = up_w.shape[1]
    per = down_w.shape[0] // size
    fill(up_w, info_ref.at[0], own_a, other_a, block)

    @pl.when(step % per == 0)
    def _():
        fill(down_w, info_ref.at[1], own_b, other_b, block)

    root = np.float32(np.sqrt(2.0 / np.pi))
    x, g, up = x_ref[...], g_ref[...], up_w[...]
    down = down_w[pl.ds(pl.multiple_of(step % per * size, size), size), :]
    hidden = dot(x, up) + bias_ref[...]
    square = hidden * hidden
    bend = jnp.tanh(root * hidden * (1.0 + 0.044715 * square))
    act = (0.5 * hidden * (1.0 + bend)).astype(BF)
    out_ref[...] += dot(act, down)
    slope = 0.5 * (1.0 + bend) + 0.5 * hidden * (1.0 - bend * bend) * root * (
        1.0 + (3 * 0.044715) * square
    )
    grad_hidden = (dot(g, down, LAST) * slope).astype(BF)
    bias_g[...] = jnp.sum(grad_hidden.astype(F32), axis=0, keepdims=True)
    gx_ref[...] += dot(grad_hidden, up, LAST)
    keep_b[...], send_b[...] = halves_of(dot(act, g, FIRST), core, BLOCKS // per)
    keep_a[...], send_a[...] = halves_of(dot(x, grad_hidden, FIRST), core)


def mlp(info, x, g, pieces, bias, at, carried=None):
    tokens, width = x.shape
    block, per = 512, width // 512
    lead, rows = BLOCKS // 2, width // BLOCKS
    part_a = pl.BlockSpec((lead, rows, block), lambda f: (0, 0, f))
    part_b = pl.BlockSpec((lead, rows, width), lambda f: (0, 0, f // per))
    if len(pieces) == 5:
        matrices = pieces[1:]
        total = matrices[0].shape[2]
        sources = [part_a, part_a, part_b, part_b]
    else:
        matrices = [pieces[0].reshape(lead, 2, rows, -1)] * 4
        total = matrices[0].shape[3] // 2
        skip = total // width
        sources = [
            pl.BlockSpec((lead, None, rows, block), lambda f: (0, 0, 0, f)),
            pl.BlockSpec((lead, None, rows, block), lambda f: (0, 1, 0, f)),
            pl.BlockSpec((lead, None, rows, width), lambda f: (0, 0, 0, skip + f // per)),
            pl.BlockSpec((lead, None, rows, width), lambda f: (0, 1, 0, skip + f // per)),
        ]
    steps = total // block
    grad_b = pl.BlockSpec((lead // per, rows, width), lambda f: (f % per, 0, f // per))
    single = pl.BlockSpec((tokens, width), lambda f: (0, 0), pipeline_mode=pl.Buffered(1))
    carried = () if carried is None else tuple(carried)
    return pl.pallas_call(
        partial(mlp_body, first=not carried),
        grid=(steps,),
        in_specs=[pl.BlockSpec(memory_space=pltpu.SMEM), single, single]
        + sources
        + [pl.BlockSpec((1, block), lambda f: (0, at * per + f))]
        + [single] * len(carried),
        out_specs=[single, single, part_a, part_a, grad_b, grad_b]
        + [pl.BlockSpec((1, block), lambda f: (0, f))],
        out_shape=[jax.ShapeDtypeStruct((tokens, width), F32)] * 2
        + [jax.ShapeDtypeStruct((lead, rows, total), BF)] * 4
        + [jax.ShapeDtypeStruct((1, total), F32)],
        scratch_shapes=[pltpu.VMEM((width, block), BF), pltpu.VMEM((width, width), BF)],
        input_output_aliases={8 + i: i for i in range(len(carried))},
        compiler_params=PARAMS,
        cost_estimate=cost(
            12 * tokens * width * total,
            (8 + 8 * len(carried)) * tokens * width + 8 * total * width,
            tokens * total,
            20 if carried else 0.3,
        ),
        name="mlp",
    )(info, x, g, *matrices, bias, *carried)


def fold_body(bit_ref, *refs, plan, out_count):
    ins, outs = refs[:-out_count], refs[-out_count:]
    for source, cols, bit, stride, out, column in plan:
        kept, came = ins[2 * source], ins[2 * source + 1]
        at_cols = slice(column, column + cols.stop - cols.start)
        if bit is None:
            outs[out][:, :, at_cols] = kept[:, :, cols].astype(F32) + came[:, :, cols].astype(F32)
            continue
        mine = bit_ref[bit]
        for m in range(kept.shape[0] // 2):
            base = m // stride * 2 * stride + m % stride
            for side, value in ((0, mine), (1, 1 - mine)):
                at = base + value * stride
                outs[out + side][m, :, at_cols] = (
                    kept[at, :, cols].astype(F32) + came[at, :, cols].astype(F32)
                ).astype(BF)


def fold(bits, parts, plan, outs, split=1, weight=0):
    def spec(shape):
        return pl.BlockSpec(tuple(shape[:2]) + (shape[2] // split,), lambda n: (0, 0, n))

    return pl.pallas_call(
        partial(fold_body, plan=plan, out_count=len(outs)),
        grid=(split,),
        in_specs=[pl.BlockSpec(memory_space=pltpu.SMEM)] + [spec(p.shape) for p in parts],
        out_specs=[spec(s) for s, _ in outs],
        out_shape=[jax.ShapeDtypeStruct(s, t) for s, t in outs],
        compiler_params=PARAMS,
        cost_estimate=cost(weight, 8),
        name="fold",
    )(bits, *parts)


def swap(block, count, mask):
    return lax.ppermute(block, AXES, [(i, i ^ mask) for i in range(count)])


def after(value, *others):
    return lax.optimization_barrier((value,) + others)


def join(block, came):
    return jnp.concatenate([block, came])


def codes(order, me):
    code = [0]
    for bit in order:
        code = code + [c | (1 << bit) for c in code]
    return jnp.asarray(np.array(code, np.int32)) ^ me


def gathered_pieces(full):
    rows, cols = full.shape
    cut = full.reshape(BLOCKS // 2, 2, rows // BLOCKS, 2, cols // 2)
    return [cut[:, i, :, j] for j in range(2) for i in range(2)]


def halve(pieces, axis, bit_value, count, mask):
    total = pieces[0]
    if len(pieces) > 1:
        total = (pieces[0].astype(F32) + pieces[1].astype(F32)).astype(BF)
    keep = lax.dynamic_index_in_dim(total, bit_value, axis, keepdims=False)
    send = lax.dynamic_index_in_dim(total, 1 - bit_value, axis, keepdims=False)
    return [keep, swap(send, count, mask)]


def scatter_rows(kept, send, count, me):
    grads = [jnp.stack(pair, axis=1).reshape(-1, pair[0].shape[2]) for pair in zip(kept, send)]
    grad = jnp.concatenate(grads, axis=1)
    rows, width = grad.shape
    bits = count.bit_length() - 1
    own = rows // count
    bit = [lax.rem(lax.div(me, np.int32(1 << b)), np.int32(2)) for b in range(bits)]
    part = [grad.reshape((2,) * bits + (own, width))]
    for b in range(bits):
        part = halve(part, bits - 1 - b, bit[b], count, 1 << b)
    return (part[0].astype(F32) + part[1].astype(F32)).reshape(own, width)


def tie(*groups):
    flat = lax.optimization_barrier(tuple(a for g in groups for a in g))
    for g in groups:
        g[:], flat = flat[: len(g)], flat[len(g) :]


def land(value, *moves):
    box = [value]
    tie(box, *[m.came for m in moves])
    return box[0]


def leave(value, *scatters):
    for s in scatters:
        s.add()
    box = [value]
    tie(box, *[s.send for s in scatters])
    for s in scatters:
        if s.done is None:
            s.start()
    return box[0]


class Gather:
    def __init__(self, shard, count):
        self.count = count
        self.block = shard[None]
        self.came = None

    def start_z(self, bit):
        self.came = [swap(self.block, self.count, 1 << bit)]

    def end_z(self):
        self.block = join(self.block, self.came[0])

    def start_xy(self, first, second):
        if not isinstance(self.block, list):
            half = self.block.shape[2] // 2
            self.block = [self.block[:, :, :half], self.block[:, :, half:]]
        self.came = [
            swap(b, self.count, 1 << bit) for b, bit in zip(self.block, (first, second))
        ]

    def end_xy(self):
        self.block = [join(b, c) for b, c in zip(self.block, self.came)]

    def start_core(self):
        self.came = [swap(b, self.count, 1) for b in self.block]

    def pieces(self, code):
        return (code, self.block[0], self.came[0], self.block[1], self.came[1])


class Scatter:
    def __init__(self, kept, send, bits, count, heavy=0):
        self.bits, self.count, self.heavy = bits, count, heavy
        self.kept, self.send = list(kept), list(send)
        self.left = 0
        self.done = None
        self.start()

    def start(self):
        masks = ([1] * len(self.send), (2, 4), (4, 2), (8,), (16,))[self.left]
        self.came = [swap(s, self.count, mask) for s, mask in zip(self.send, masks)]
        self.left += 1

    def add(self):
        parts = [p for pair in zip(self.kept, self.came) for p in pair]
        lead, own, width = self.kept[0].shape
        split = {1: 4, 2: 2}.get(self.left, 1)
        everything = slice(0, width // split)
        half = lambda cols: ((lead // 2, own, cols), BF)
        if self.left == 5:
            plan = ((0, everything, None, 1, 0, 0),)
            outs = [((lead, own, width), F32)]
        elif self.left == 1:
            plan, sums = [], [0, 0]
            for side in range(2):
                plan.append((side, everything, (1, 2)[side], (1, 2)[side], 2 * side, 0))
            outs = [half(width)] * 4
        elif self.left == 2:
            plan = tuple((i, everything, 2 - i, 1, 2 * i, 0) for i in range(2))
            outs = [half(width)] * 4
        elif self.left == 3:
            plan = tuple((i, everything, 3, 1, 0, i * width) for i in range(2))
            outs = [half(2 * width)] * 2
        else:
            plan = ((0, everything, 4, 1, 0, 0),)
            outs = [half(width)] * 2
        weight = self.heavy if self.left == 5 else 0
        outs = fold(self.bits, parts, tuple(plan), outs, split, weight)
        if self.left == 5:
            self.done, self.send = outs[0][0], list(outs)
        else:
            self.kept, self.send = list(outs[0::2]), list(outs[1::2])


def per_device(
    tokens,
    labels,
    stop_scale,
    class_table,
    ada_weight,
    ada_bias,
    qkv_weight,
    head_scale,
    out_weight,
    up_weight,
    up_bias,
    down_weight,
    cotangent,
    count,
):
    image_count, seq_len, model_width = tokens.shape
    row_count = image_count * seq_len
    me = lax.axis_index(AXES).astype(jnp.int32)
    levels = position_scale(SCALES)
    ends = jnp.asarray(LEVEL_ENDS)
    live = jnp.take(ends, stop_scale - 1).astype(jnp.int32)
    limit = jnp.asarray(LEVEL_ENDS[levels][None, :])
    start = jnp.asarray((LEVEL_ENDS - np.square(np.array(scale_sides)))[levels][None, :].astype(np.int32))
    class_count = class_table.shape[0]
    own = model_width // count
    ratio = down_weight.shape[0] // own
    hidden_width = up_weight.shape[1]

    def hidden_order(matrix):
        lead = matrix.shape[:-1]
        cut = matrix.reshape(lead + (count, ratio, own))
        return jnp.swapaxes(cut, -3, -2).reshape(lead + (hidden_width,))

    def hidden_back(matrix):
        lead = matrix.shape[:-1]
        cut = matrix.reshape(lead + (ratio, count, own))
        return jnp.swapaxes(cut, -3, -2).reshape(lead + (hidden_width,))

    down_wide = jnp.swapaxes(down_weight.reshape(ratio, own, model_width), 0, 1).reshape(
        own, hidden_width
    )
    half = hidden_width // 2
    up_order = hidden_order(up_weight)
    shards = [jnp.concatenate([qkv_weight, out_weight], axis=1)] + [
        jnp.concatenate([m[:, i : i + half] for m in (up_order, down_wide)], axis=1)
        for i in (0, half)
    ]
    quick = count == BLOCKS and own % 16 == 0
    plain = jnp.asarray(np.tile(np.arange(0, BLOCKS, 2, dtype=np.int32), (2, 1)))
    if quick:
        one, two = [Gather(s, count) for s in shards[:2]]
        orders = ((4, 3, 2, 1), (4, 3, 1, 2))
        code = jnp.stack([codes(o, me) for o in orders])
        bits = jnp.stack([lax.rem(lax.div(me, np.int32(1 << b)), np.int32(2)) for b in range(5)])
        one.start_z(4)
    else:
        wide = [lax.all_gather(s, AXES, axis=0, tiled=True) for s in shards]
        code = plain
        bits = jnp.zeros((5,), jnp.int32)
    core = bits[:1]
    info, info_plain = [
        jnp.concatenate([c, jnp.full((1, c.shape[1]), bits[0])]) for c in (code, plain)
    ]

    first_row = jnp.concatenate(
        [lax.div(labels, 32).astype(BF), lax.rem(labels, 32).astype(BF), up_bias]
    )
    rows = lax.all_to_all(
        jnp.broadcast_to(first_row[None, :], (count, first_row.shape[0])), AXES, 0, 0, tiled=True
    )
    labels_all = 32 * rows[:, 0].astype(jnp.int32) + rows[:, 1].astype(jnp.int32)
    up_bias_full = rows[:, 2:].astype(F32).reshape(1, hidden_width)
    onehot = labels_all[:, None] == jnp.arange(class_count, dtype=jnp.int32)[None, :]
    condition = jnp.dot(onehot.astype(BF), class_table, preferred_element_type=F32)
    cond_act = jax.nn.silu(condition).astype(BF)
    exponent = count.bit_length() - 1
    order = tuple(range(exponent - 1, -1, -1)) + (exponent,)
    backwards = cond_act.reshape((2,) * exponent + (own,)).transpose(order).reshape(count, own)
    modul_part = jnp.dot(backwards, ada_weight, preferred_element_type=F32)
    bias_own = ada_bias.shape[0]
    bias_row = lax.dynamic_update_slice(
        jnp.zeros((6 * model_width,), F32), ada_bias.astype(F32), (me * bias_own,)
    )
    part = modul_part + bias_row[None, :]
    if quick:
        part = land(part, one)
        one.end_z()
        one.start_z(3)
    bit_values = [lax.rem(lax.div(me, np.int32(1 << b)), np.int32(2)) for b in range(exponent)]
    for b in range(exponent):
        size = part.shape[0] // 2
        keep = lax.dynamic_slice_in_dim(part, bit_values[b] * size, size)
        send = lax.dynamic_slice_in_dim(part, (1 - bit_values[b]) * size, size)
        came = swap(send, count, 1 << b)
        if quick and b == 0:
            came = land(came, one)
            one.end_z()
            came, two.block = after(came, two.block)
            one.start_xy(2, 1)
            two.start_z(4)
        elif quick and b == 2:
            came = land(came, one, two)
            one.end_xy()
            two.end_z()
            came, last_shard = after(came, shards[2])
            last_full = lax.all_gather(last_shard, AXES, axis=0, tiled=True)
            one.start_xy(1, 2)
            two.start_z(3)
        part = keep + came
    mod = part.reshape(6, model_width)
    if quick:
        mod = land(mod, one, two)
        one.end_xy()
        two.end_z()
        one.start_core()
        two.start_xy(2, 1)
        mod = land(mod, one)
        pieces = one.pieces(code)
    else:
        pieces = (code, *gathered_pieces(wide[0]))
    heads = head_scale.shape[0]
    gain = jnp.repeat(jnp.exp(head_scale), HDIM)[None, :]
    seg = jnp.asarray(
        np.arange(model_width)[:, None] // HDIM == np.arange(128)[None, :], dtype=BF
    )
    x = tokens.reshape(row_count, model_width)
    cot = cotangent.reshape(row_count, model_width)

    attn_in, qkv, norms, weights = qkv_rows(x, mod, pieces, gain, seg)
    if quick:
        qkv = land(qkv, two)
        two.end_xy()
        qkv, *two.block = after(qkv, *two.block)
        two.start_xy(1, 2)
    attended, low, inverse = attend(qkv, start)
    projected, mlp_in, grad_mlp = project(live, x, attended, weights, mod, cot)
    if quick:
        mlp_in = land(mlp_in, two)
        two.end_xy()
        two.start_core()
    bias = hidden_order(up_bias_full)
    pieces = two.pieces(code) if quick else (wide[1],)
    *carried, keep_a, send_a, keep_b, send_b, bias_one = mlp(info, mlp_in, grad_mlp, pieces, bias, 0)
    kept_one, send_one = (keep_a, keep_b), (send_a, send_b)
    if quick:
        first = Scatter(kept_one, send_one, bits, count, 1 << 33)
        carried[0] = land(carried[0], first)
        carried[0] = leave(carried[0], first)
    pieces = (last_full if quick else wide[2],)
    mlp_out, grad_mlp_in, keep_a, send_a, keep_b, send_b, bias_two = mlp(
        info_plain, mlp_in, grad_mlp, pieces, bias, half // model_width, carried
    )
    kept_two, send_two = (keep_a, keep_b), (send_a, send_b)
    up_bias_grad = jnp.concatenate([bias_one, bias_two], axis=1)
    if quick:
        second = Scatter(kept_two, send_two, bits, count)
        mlp_out = land(mlp_out, first)
        mlp_out = leave(mlp_out, first)
    block_out, grad_resid, grad_attended, grad_proj, sums_two = residual_back(
        live, x, projected, mlp_out, grad_mlp_in, cot, mod, weights
    )
    if quick:
        grad_attended = land(grad_attended, first, second)
        grad_attended = leave(grad_attended, first, second)
    dqkv, head_sums = attend_back(
        qkv, grad_attended, attended, low, inverse, norms, gain, limit, 0, heads // 2
    )
    if quick:
        dqkv = land(dqkv, first, second)
        dqkv = leave(dqkv, first, second)
    head_scale_part = jnp.sum(head_sums[0].reshape(heads, HDIM), axis=1)
    keep_a, send_a, keep_b, send_b = weight_grad(core, attn_in, dqkv, attended, grad_proj)
    kept_three, send_three = (keep_a, keep_b), (send_a, send_b)
    if quick:
        third = Scatter(kept_three, send_three, bits, count)
        dqkv = land(dqkv, first, second)
        dqkv = leave(dqkv, first, second)
        dqkv = land(dqkv, third)
        dqkv = leave(dqkv, third)
    input_grad, sums_one = input_back(x, grad_resid, mod, dqkv, weights)
    if not quick:
        mlp_own = [scatter_rows(kept_one, send_one, count, me), scatter_rows(kept_two, send_two, count, me)]
        attn_own = scatter_rows(kept_three, send_three, count, me)
    block_out = block_out.reshape(tokens.shape)
    input_grad = input_grad.reshape(tokens.shape)
    grad_modul = jnp.concatenate(
        [sums_two[0], sums_two[1], sums_one[0], sums_two[2], sums_one[1], sums_two[3]]
    ).astype(BF)
    bias_high, bias_low = split_low(hidden_back(up_bias_grad).reshape(count, -1))
    head_high, head_low = split_low(head_scale_part)
    common = jnp.concatenate([grad_modul.reshape(-1), head_high, head_low])
    small = jnp.concatenate(
        [jnp.broadcast_to(common[None, :], (count, common.shape[0])), bias_high, bias_low], axis=1
    )
    small = lax.all_to_all(small, AXES, 0, 0, tiled=True)
    if quick:
        input_grad = land(input_grad, second, third)
        input_grad = leave(input_grad, second, third)
        input_grad = land(input_grad, second, third)
        input_grad = leave(input_grad, second, third)
        input_grad = land(input_grad, third)
        small, input_grad = after(small, input_grad)
        small = leave(small, third)
        third.add()
        mlp_own = [first.done, second.done]
        attn_own = third.done
    up_own = jnp.concatenate([m[:, :half] for m in mlp_own], axis=1)
    down_own = jnp.concatenate([m[:, half:] for m in mlp_own], axis=1)
    modul_cols = image_count * 6 * model_width
    grad_modul_all = small[:, :modul_cols].reshape(count * image_count, 6 * model_width)
    tail = jnp.sum(small[:, modul_cols:].astype(F32), axis=0)
    head_scale_grad = tail[:heads] + tail[heads : 2 * heads]
    tail = tail[2 * heads :].reshape(2, -1)
    up_bias_own = tail[0] + tail[1]
    ada_bias_own = jnp.sum(
        lax.dynamic_slice_in_dim(grad_modul_all, me * bias_own, bias_own, axis=1).astype(F32), axis=0
    )
    ada_own = lax.dot_general(
        cond_act, grad_modul_all, (((0,), (0,)), ((), ())), preferred_element_type=F32
    )
    grad_cond_act = lax.dot_general(
        grad_modul_all, ada_weight, (((1,), (1,)), ((), ())), preferred_element_type=F32
    )
    grad_condition = jax.vjp(jax.nn.silu, condition)[1](grad_cond_act)[0]
    table_own = lax.dot_general(
        onehot.astype(F32),
        grad_condition,
        (((0,), (0,)), ((), ())),
        precision=lax.Precision.HIGHEST,
        preferred_element_type=F32,
    )
    qkv_own = attn_own[:, : 3 * model_width]
    out_own = attn_own[:, 3 * model_width :]
    up_own = hidden_back(up_own)
    down_own = jnp.swapaxes(down_own.reshape(own, ratio, model_width), 0, 1).reshape(
        ratio * own, model_width
    )
    return (
        block_out,
        input_grad,
        table_own,
        ada_own,
        ada_bias_own,
        qkv_own,
        head_scale_grad,
        out_own,
        up_own,
        up_bias_own,
        down_own,
    )


def solution(mesh):
    count = mesh.shape["wide"] * mesh.shape["narrow"]
    both = AXES
    in_specs = (
        P(both, None, None),
        P(both),
        P(both),
        P(None, both),
        P(both, None),
        P(both),
        P(both, None),
        P(),
        P(both, None),
        P(both, None),
        P(both),
        P(both, None),
        P(both, None, None),
    )
    out_specs = (
        P(both, None, None),
        P(both, None, None),
        P(None, both),
        P(both, None),
        P(both),
        P(both, None),
        P(),
        P(both, None),
        P(both, None),
        P(both),
        P(both, None),
    )
    return jax.shard_map(
        partial(per_device, count=count),
        mesh=mesh,
        in_specs=in_specs,
        out_specs=out_specs,
        check_vma=False,
    )
```

time: 664 us -> 436 us (0.66)
  Pallas kernels: 69.3 us -> 206 us
  matrix products: 121 us -> 3.38 us
  waiting for transfers between devices: 182 us -> 85.9 us
  other arithmetic: 107 us -> 23 us
  local copies, waits for them, and re-layouts: 105 us -> 41.2 us
    pallas_call x3 -> x24, Pallas kernels: 69.3 us -> 206 us  [the longest x2 54.8 us: mlp(): pl.pallas_call(partial(mlp_body, first=not carried), grid=(steps,), in_sp...]
    dot_general x35 -> x1, matrix products: 118 us -> 0.24 us  [per_device(): modul_part = jnp.dot(backwards, ada_weight, preferred_element_type=F32)]
    ppermute x29 -> x45, waiting for transfers between devices: 182 us -> 85.9 us  [swap(): return lax.ppermute(block, AXES, [(i, i ^ mask) for i in range(count)])]
    reduce_sum x19 -> x1, other arithmetic: 38.7 us -> 0.12 us  [per_device(): head_scale_part = jnp.sum(head_sums[0].reshape(heads, HDIM), axis=1)]
    convert_element_type x20 -> x0, other arithmetic: 21.6 us -> none  [the longest x15 13.1 us: halve(): total = (pieces[0].astype(F32) + pieces[1].astype(F32)).astype(BF)]
    squeeze x21 -> x0, local copies, waits for them, and re-layouts: 20.9 us -> none  [the longest x3 19.7 us: halve(): keep = lax.dynamic_index_in_dim(total, bit_value, axis, keepdims=False)]
    split x5 -> x0, local copies, waits for them, and re-layouts: 13.9 us -> none  [per_device(): query_raw, key_raw, value_raw = jnp.split(qkv_rows, 3, axis=-1)]
    broadcast_in_dim x5 -> x2, local copies, waits for them, and re-layouts: 11.5 us -> 0.71 us  [the longest x1 0.64 us: per_device(): jnp.broadcast_to(first_row[None, :], (count, first_row.shape[0]))]
  transfers between devices with their start and end apart: 33 -> 48, of which waited for: 13 -> 20; matrix products, arithmetic and copies ran while one was open for 44% -> 14% of each run, Pallas kernels for 3% -> 42%
where the time goes in v2:
time: 436 us; the launch traced here: 430 us
  Pallas kernels  206 us (47%)
  waiting for transfers between devices  85.9 us (20%)
  starting transfers between devices  53.2 us (12%)
  local copies, waits for them, and re-layouts  41.2 us (9%)
  other arithmetic  23 us (5%)
  between operations  17.1 us (4%)
    ppermute x45, waiting for transfers between devices, swap(): return lax.ppermute(block, AXES, [(i, i ^ mask) for i in range(count)])  85.9 us
    pallas_call x2, Pallas kernels, mlp(): pl.pallas_call(partial(mlp_body, first=not carried), grid=(steps,), in_sp...  54.8 us
    pallas_call x15, Pallas kernels, fold(): pl.pallas_call(partial(fold_body, plan=plan, out_count=len(outs)), grid=(...  48.7 us
    ppermute x45, starting transfers between devices, swap(): return lax.ppermute(block, AXES, [(i, i ^ mask) for i in range(count)])  43 us
    pallas_call x1, Pallas kernels, attend_back(): pl.pallas_call(attend_back_body, grid=(some,), in_specs=[pair(0), pair(pa...  26.9 us
    pallas_call x1, Pallas kernels, qkv_rows(): pl.pallas_call(qkv_body, grid=(4,), in_specs=[pl.BlockSpec(memory_space=p...  17.7 us
    pallas_call x1, Pallas kernels, attend(): pl.pallas_call(attend_body, grid=(pairs,), in_specs=[pair(0), pair(pairs)...  14.2 us
    pallas_call x1, Pallas kernels, weight_grad(): pl.pallas_call(weight_grad_body, grid=(4,), in_specs=[pl.BlockSpec(memory...  12.8 us
  transfers between devices with their start and end apart: 48, of which 20 were waited for; matrix products, arithmetic and copies ran while one was open for 14% of the time, Pallas kernels for 42%

profile of v2, /device:TPU:0, one launch (start us, length us, event | category | flops | bytes accessed | tf_op | source)
XLA Modules:
  0.0 429.7 jit_solution(8517321476869319499)
XLA Ops:
  9.3 7.3 %all-to-all-start = ((bf16[32,1,130]{2,1,0:T(2,128)(2,1)}), bf16[32,1,130]{2,1,0:T(2,128)(2,1)S(1)}, u32[]{:S(2)}, u32[]{:S(2)}) async-start(bf16[32,1,130]{2,1,0:T(2,128)(2,1)} %broadcast_in_dim.17), calls=%async_computation | async-start | bytes 65536 | tf_op jit(solution)/shard_map/all_to_all | solution.py:821
  25.3 7.6 %collective-permute-done = bf16[1,32,4096]{2,1,0:T(8,128)(2,1)S(1)} collective-permute-done((bf16[1,32,4096]{2,1,0:T(8,128)(2,1)S(1)}, bf16[1,32,4096]{2,1,0:T(8,128)(2,1)S(1)}, u32[]{:S(2)}, u32[]{:S(2)}) %collective-permute-start) | collective-permute-done | bytes 262176 | tf_op jit(solution)/shard_map/ppermute | solution.py:610
  35.3 11.3 %collective-permute-done.2 = bf16[2,32,4096]{2,1,0:T(8,128)(2,1)S(1)} collective-permute-done((bf16[2,32,4096]{2,1,0:T(8,128)(2,1)S(1)}, bf16[2,32,4096]{2,1,0:T(8,128)(2,1)S(1)}, u32[]{:S(2)}, u32[]{:S(2)}) %collective-permute-start.2) | collective-permute-done | bytes 524320 | tf_op jit(solution)/shard_map/ppermute | solution.py:610
  57.4 6.3 %collective-permute-done.7 = bf16[1,32,4096]{2,1,0:T(8,128)(2,1)S(1)} collective-permute-done((bf16[1,32,4096]{2,1,0:T(8,128)(2,1)S(1)}, bf16[1,32,4096]{2,1,0:T(8,128)(2,1)S(1)}, u32[]{:S(2)}, u32[]{:S(2)}) %collective-permute-start.7) | collective-permute-done | bytes 262176 | tf_op jit(solution)/shard_map/ppermute | solution.py:610
  74.4 3.4 collective-permute-start.9
  77.8 9.9 %collective-permute-done.9 = f32[1,6144]{1,0:T(1,128)} collective-permute-done((f32[1,6144]{1,0:T(1,128)}, f32[1,6144]{1,0:T(1,128)}, u32[]{:S(2)}, u32[]{:S(2)}) %collective-permute-start.9) | collective-permute-done | bytes 24608 | tf_op jit(solution)/shard_map/ppermute | solution.py:610
  90.5 2.9 collective-permute-done.10
  105.9 17.7 %qkv.1 = (bf16[680,1024]{1,0:T(8,128)(2,1)}, bf16[680,3072]{1,0:T(8,128)(2,1)}, f32[680,2048]{1,0:T(8,128)}, bf16[1024,4096]{1,0:T(8,128)(2,1)}) custom-call(s32[2,16]{1,0:T(2,128)} %pad_add_fusion.code_ref, bf16[680,1024]{1,0:T(8,128)(2,1)} %bitcast.72, f32[6,1024]{1,0:T(8,128)} %reshape.109.mod_ref, bf16[16,32,2048]{2,1,0:T(8,128)(2,1)} %pad_maximum_fusion.own_a, ...), custom_call_target="tpu_custom_call" | custom-call | flops 4278190080 | bytes 27918336 | tf_op jit(solution)/shard_map/qkv/pallas_call | solution.py:123
  127.6 14.2 %attend.1 = (bf16[680,1024]{1,0:T(8,128)(2,1)}, bf16[680,1024]{1,0:T(8,128)(2,1)}, f32[680,1024]{1,0:T(8,128)}) custom-call(bf16[680,3072]{1,0:T(8,128)(2,1)} %get-tuple-element.195.q_ref.k_ref.v_ref, bf16[680,3072]{1,0:T(8,128)(2,1)} %get-tuple-element.195.q_ref.k_ref.v_ref, bf16[680,3072]{1,0:T(8,128)(2,1)} %get-tuple-element.195.q_ref.k_ref.v_ref, ...), custom_call_target="tpu_custom_call" | custom-call | flops 3787980800 | bytes 6963200 | tf_op jit(solution)/shard_map/attend/pallas_call | solution.py:188
  141.8 7.1 %project.1 = (f32[680,1024]{1,0:T(8,128)}, bf16[680,1024]{1,0:T(8,128)(2,1)}, bf16[680,1024]{1,0:T(8,128)(2,1)}) custom-call(s32[1]{0:T(128)S(6)} %select_n.44.live_ref, bf16[680,1024]{1,0:T(8,128)(2,1)} %bitcast.73, bf16[680,1024]{1,0:T(8,128)(2,1)} %get-tuple-element.196.att_ref, bf16[1024,4096]{1,0:T(8,128)(2,1)} %get-tuple-element.197.w_ref, ...), custom_call_target="tpu_custom_call" | custom-call | flops 1426063360 | bytes 11845632 | tf_op jit(solution)/shard_map/project/pallas_call | solution.py:319
  151.0 4.1 collective-permute-done.17
  160.8 3.0 collective-permute-done.20.other_b
  163.8 26.6 %mlp.2 = (f32[680,1024]{1,0:T(8,128)}, f32[680,1024]{1,0:T(8,128)}, bf16[16,32,2048]{2,1,0:T(8,128)(2,1)}, bf16[16,32,2048]{2,1,0:T(8,128)(2,1)}, bf16[16,32,204...) custom-call(s32[3,16]{1,0:T(4,128)} %add_add_fusion.info_ref, ...), custom_call_target="tpu_custom_call" | custom-call | flops 5133828096 | bytes 6704332 | tf_op jit(solution)/shard_map/mlp/pallas_call | solution.py:550
  192.2 4.2 collective-permute-done.21.refs_1_
  197.9 5.9 %fold.15 = (bf16[8,32,2048]{2,1,0:T(8,128)(2,1)}, bf16[8,32,2048]{2,1,0:T(8,128)(2,1)}, bf16[8,32,2048]{2,1,0:T(8,128)(2,1)}, bf16[8,32,2048]{2,1,0:T(8,128)(2,1)}) custom-call(s32[5]{0:T(128)} %stack.35.bit_ref, bf16[16,32,2048]{2,1,0:T(8,128)(2,1)} %get-tuple-element.211.refs_0_, bf16[16,32,2048]{2,1,0:T(8,128)(2,1)} %copy-done.3, ...), custom_call_target="tpu_custom_call" | custom-call | bytes 160 | tf_op jit(solution)/shard_map/fold/pallas_call | solution.py:597
  205.9 28.2 %mlp.3 = (f32[680,1024]{1,0:T(8,128)}, f32[680,1024]{1,0:T(8,128)}, bf16[16,32,2048]{2,1,0:T(8,128)(2,1)}, bf16[16,32,2048]{2,1,0:T(8,128)(2,1)}, bf16[16,32,204...) custom-call(s32[3,16]{1,0:T(4,128)} %concatenate.91.info_ref, ...), custom_call_target="tpu_custom_call", output_to_operand_aliasing={{0}: (8, {}), {1}: (9, {})} | custom-call | flops 342255206400 | bytes 669777920 | tf_op jit(solution)/shard_map/mlp/pallas_call | solution.py:550
  234.2 3.5 fold.16
  240.3 11.0 %residual_back.1 = (bf16[680,1024]{1,0:T(8,128)(2,1)}, f32[680,1024]{1,0:T(8,128)}, bf16[680,1024]{1,0:T(8,128)(2,1)}, bf16[680,1024]{1,0:T(8,128)(2,1)}, f32[8,1024]{1,0:T(8,128)}) custom-call(s32[1]{0:T(128)S(6)} %select_n.44.live_ref, bf16[680,1024]{1,0:T(8,128)(2,1)} %bitcast.74, f32[680,1024]{1,0:T(8,128)} %get-tuple-element.198.proj_ref, ...), custom_call_target="tpu_custom_call" | custom-call | flops 28521267200 | bytes 473825280 | tf_op jit(solution)/shard_map/residual_back/pallas_call | solution.py:368
  260.2 2.8 fold.17
  263.0 6.0 %fold.18 = (bf16[8,32,2048]{2,1,0:T(8,128)(2,1)}, bf16[8,32,2048]{2,1,0:T(8,128)(2,1)}, bf16[8,32,2048]{2,1,0:T(8,128)(2,1)}, bf16[8,32,2048]{2,1,0:T(8,128)(2,1)}) custom-call(s32[5]{0:T(128)} %stack.35.bit_ref, bf16[16,32,2048]{2,1,0:T(8,128)(2,1)} %get-tuple-element.245.refs_0_, bf16[16,32,2048]{2,1,0:T(8,128)(2,1)} %copy-done.2, ...), custom_call_target="tpu_custom_call" | custom-call | bytes 160 | tf_op jit(solution)/shard_map/fold/pallas_call | solution.py:597
  272.5 26.9 %attend_back.1 = (bf16[3,680,1024]{2,1,0:T(8,128)(2,1)}, f32[8,1024]{1,0:T(8,128)}) custom-call(bf16[680,3072]{1,0:T(8,128)(2,1)} %get-tuple-element.195.q_ref.k_ref.v_ref, bf16[680,3072]{1,0:T(8,128)(2,1)} %get-tuple-element.195.q_ref.k_ref.v_ref, bf16[680,3072]{1,0:T(8,128)(2,1)} %get-tuple-element.195.q_ref.k_ref.v_ref, ...), custom_call_target="tpu_custom_call" | custom-call | flops 189399040000 | bytes 417792000 | tf_op jit(solution)/shard_map/attend_back/pallas_call | solution.py:272
  303.0 3.4 fold.20
  310.8 12.8 %weight_grad.1 = (bf16[16,32,2048]{2,1,0:T(8,128)(2,1)}, bf16[16,32,2048]{2,1,0:T(8,128)(2,1)}, bf16[16,32,2048]{2,1,0:T(8,128)(2,1)}, bf16[16,32,2048]{2,1,0:T(8,128)(2,1)}) custom-call(s32[1]{0:T(128)} %bitcast.33.core_ref, bf16[680,1024]{1,0:T(8,128)(2,1)} %get-tuple-element.282.x_ref, bf16[3,680,1024]{2,1,0:T(8,128)(2,1)} %get-tuple-element.293.g_ref, ...), custom_call_target="tpu_custom_call" | custom-call | flops 114085068800 | bytes 334888960 | tf_op jit(solution)/shard_map/weight_grad/pallas_call | solution.py:413
  331.1 5.9 %fold.23 = (bf16[8,32,2048]{2,1,0:T(8,128)(2,1)}, bf16[8,32,2048]{2,1,0:T(8,128)(2,1)}, bf16[8,32,2048]{2,1,0:T(8,128)(2,1)}, bf16[8,32,2048]{2,1,0:T(8,128)(2,1)}) custom-call(s32[5]{0:T(128)} %stack.35.bit_ref, bf16[16,32,2048]{2,1,0:T(8,128)(2,1)} %get-tuple-element.287.refs_0_, bf16[16,32,2048]{2,1,0:T(8,128)(2,1)} %collective-permute-done.35.refs_1_, ...), custom_call_target="tpu_custom_call" | custom-call | bytes 160 | tf_op jit(solution)/shard_map/fold/pallas_call | solution.py:597
  339.2 12.8 %input_back.1 = (f32[680,1024]{1,0:T(8,128)}, f32[8,1024]{1,0:T(8,128)}) custom-call(bf16[680,1024]{1,0:T(8,128)(2,1)} %bitcast.75, f32[680,1024]{1,0:T(8,128)} %get-tuple-element.233.resid_ref, f32[6,1024]{1,0:T(8,128)} %reshape.109.mod_ref, bf16[3,680,1024]{2,1,0:T(8,128)(2,1)} %get-tuple-element.293.g_ref, bf16[1024,4096]{1,0:T(8,128)(2,1)} %get-tuple-element.197.w_ref), custom_call_target="tpu_custom_call" | custom-call | flops 85563801600 | bytes 348651520 | tf_op jit(solution)/shard_map/input_back/pallas_call | solution.py:463
  358.5 5.9 %collective-permute-done.38.refs_1_ = bf16[8,32,2048]{2,1,0:T(8,128)(2,1)S(1)} collective-permute-done((bf16[8,32,2048]{2,1,0:T(8,128)(2,1)}, bf16[8,32,2048]{2,1,0:T(8,128)(2,1)S(1)}, u32[]{:S(2)}, u32[]{:S(2)}) %collective-permute-start.38) | collective-permute-done | bytes 1048608 | tf_op jit(solution)/shard_map/ppermute | solution.py:610
  368.6 3.4 fold.25
  375.7 9.1 %collective-permute-done.40.refs_1_ = bf16[1,32,4096]{2,1,0:T(8,128)(2,1)} collective-permute-done((bf16[1,32,4096]{2,1,0:T(8,128)(2,1)}, bf16[1,32,4096]{2,1,0:T(8,128)(2,1)}, u32[]{:S(2)}, u32[]{:S(2)}) %collective-permute-start.40) | collective-permute-done | bytes 262176 | tf_op jit(solution)/shard_map/ppermute | solution.py:610
  387.2 2.8 fold.27
  391.4 3.1 copy.58
  394.5 4.5 %reshape.118 = f32[32,4096]{1,0:T(8,128)} reshape(f32[32,32,4,32]{3,2,1,0:T(4,128)} %copy.58) | data formatting | bytes 1048576 | tf_op jit(solution)/shard_map/reshape | solution.py:790
  409.8 6.9 %collective-permute-done.44.refs_1_ = bf16[1,32,4096]{2,1,0:T(8,128)(2,1)S(1)} collective-permute-done((bf16[1,32,4096]{2,1,0:T(8,128)(2,1)}, bf16[1,32,4096]{2,1,0:T(8,128)(2,1)S(1)}, u32[]{:S(2)}, u32[]{:S(2)}) %collective-permute-start.44) | collective-permute-done | bytes 262176 | tf_op jit(solution)/shard_map/ppermute | solution.py:610
  (272 shorter events, 132.2 us)
Async XLA Ops:
  9.3 14.7 %all-to-all-start = ((bf16[32,1,130]{2,1,0:T(2,128)(2,1)}), bf16[32,1,130]{2,1,0:T(2,128)(2,1)S(1)}, u32[]{:S(2)}, u32[]{:S(2)}) async-start(bf16[32,1,130]{2,1,0:T(2,128)(2,1)} %broadcast_in_dim.17), calls=%async_computation | async-start | bytes 65536 | tf_op jit(solution)/shard_map/all_to_all | solution.py:821
  16.6 189.3 %all-gather.2.cloned.1.call-start = ((), (), s32[]{:S(2)}) async-start(), calls=%async_computation.2 | async-start | bytes 8650752 | tf_op jit(solution)/shard_map/all_gather | solution.py:859
  17.6 15.3 %collective-permute-start = (bf16[1,32,4096]{2,1,0:T(8,128)(2,1)S(1)}, bf16[1,32,4096]{2,1,0:T(8,128)(2,1)S(1)}, u32[]{:S(2)}, u32[]{:S(2)}) collective-permute-start(bf16[1,32,4096]{2,1,0:T(8,128)(2,1)S(1)} %maximum_bitcast_fusion), channel_id=1, source_target_pairs={{0,16},{1,17},{2,18},{3,19},{4,20},{5,21},{6,22},{7,23},{8,24},{9,... | collective-permute-start | bytes 786440 | tf_op jit(solution)/shard_map/ppermute | solution.py:610
  33.0 13.6 %collective-permute-start.2 = (bf16[2,32,4096]{2,1,0:T(8,128)(2,1)S(1)}, bf16[2,32,4096]{2,1,0:T(8,128)(2,1)S(1)}, u32[]{:S(2)}, u32[]{:S(2)}) collective-permute-start(bf16[2,32,4096]{2,1,0:T(8,128)(2,1)S(1)} %pad_maximum_fusion.7), channel_id=1, source_target_pairs={{0,8},{1,9},{2,10},{3,11},{4,12},{5,13},{6,14},{7,15},{8,0},{9,1},... | collective-permute-start | bytes 1572872 | tf_op jit(solution)/shard_map/ppermute | solution.py:610
  48.3 15.3 %collective-permute-start.5 = (bf16[4,32,2048]{2,1,0:T(8,128)(2,1)S(1)}, bf16[4,32,2048]{2,1,0:T(8,128)(2,1)S(1)}, u32[]{:S(2)}, u32[]{:S(2)}) collective-permute-start(bf16[4,32,2048]{2,1,0:T(8,128)(2,1)S(1)} %get-tuple-element.366), channel_id=1, source_target_pairs={{0,4},{1,5},{2,6},{3,7},{4,0},{5,1},{6,2},{7,3},{8,12},{9,13},{10,... | collective-permute-start | bytes 1572872 | tf_op jit(solution)/shard_map/ppermute | solution.py:610
  49.8 13.8 %collective-permute-start.6 = (bf16[4,32,2048]{2,1,0:T(8,128)(2,1)S(1)}, bf16[4,32,2048]{2,1,0:T(8,128)(2,1)S(1)}, u32[]{:S(2)}, u32[]{:S(2)}) collective-permute-start(bf16[4,32,2048]{2,1,0:T(8,128)(2,1)S(1)} %get-tuple-element.365), channel_id=1, source_target_pairs={{0,2},{1,3},{2,0},{3,1},{4,6},{5,7},{6,4},{7,5},{8,10},{9,11},{10,... | collective-permute-start | bytes 1572872 | tf_op jit(solution)/shard_map/ppermute | solution.py:610
  50.4 13.2 %collective-permute-start.7 = (bf16[1,32,4096]{2,1,0:T(8,128)(2,1)S(1)}, bf16[1,32,4096]{2,1,0:T(8,128)(2,1)S(1)}, u32[]{:S(2)}, u32[]{:S(2)}) collective-permute-start(bf16[1,32,4096]{2,1,0:T(8,128)(2,1)S(1)} %maximum_bitcast_fusion.1), channel_id=1, source_target_pairs={{0,16},{1,17},{2,18},{3,19},{4,20},{5,21},{6,22},{7,23},{8,24},{9,... | collective-permute-start | bytes 786440 | tf_op jit(solution)/shard_map/ppermute | solution.py:610
  66.8 26.6 %collective-permute-start.10 = (bf16[8,32,2048]{2,1,0:T(8,128)(2,1)}, bf16[8,32,2048]{2,1,0:T(8,128)(2,1)}, u32[]{:S(2)}, u32[]{:S(2)}) collective-permute-start(bf16[8,32,2048]{2,1,0:T(8,128)(2,1)} %pad_maximum_fusion.3), channel_id=1, source_target_pairs={{0,2},{1,3},{2,0},{3,1},{4,6},{5,7},{6,4},{7,5},{8,10},{9,11},{10,... | collective-permute-start | bytes 3145736 | tf_op jit(solution)/shard_map/ppermute | solution.py:610
  69.4 26.3 %collective-permute-start.11 = (bf16[8,32,2048]{2,1,0:T(8,128)(2,1)}, bf16[8,32,2048]{2,1,0:T(8,128)(2,1)}, u32[]{:S(2)}, u32[]{:S(2)}) collective-permute-start(bf16[8,32,2048]{2,1,0:T(8,128)(2,1)} %pad_maximum_fusion.4), channel_id=1, source_target_pairs={{0,4},{1,5},{2,6},{3,7},{4,0},{5,1},{6,2},{7,3},{8,12},{9,13},{10,... | collective-permute-start | bytes 3145736 | tf_op jit(solution)/shard_map/ppermute | solution.py:610
  71.7 18.8 %collective-permute-start.12 = (bf16[2,32,4096]{2,1,0:T(8,128)(2,1)}, bf16[2,32,4096]{2,1,0:T(8,128)(2,1)S(1)}, u32[]{:S(2)}, u32[]{:S(2)}) collective-permute-start(bf16[2,32,4096]{2,1,0:T(8,128)(2,1)} %pad_maximum_fusion.8), channel_id=1, source_target_pairs={{0,8},{1,9},{2,10},{3,11},{4,12},{5,13},{6,14},{7,15},{8,0},{9,1},... | collective-permute-start | bytes 1572872 | tf_op jit(solution)/shard_map/ppermute | solution.py:610
  74.4 13.3 %collective-permute-start.9 = (f32[1,6144]{1,0:T(1,128)}, f32[1,6144]{1,0:T(1,128)}, u32[]{:S(2)}, u32[]{:S(2)}) collective-permute-start(f32[1,6144]{1,0:T(1,128)} %constant_dynamic-slice_fusion), channel_id=1, source_target_pairs={{0,16},{1,17},{2,18},{3,19},{4,20},{5,21},{6,22},{7,23},{8,24},{9,... | collective-permute-start | bytes 73736 | tf_op jit(solution)/shard_map/ppermute | solution.py:610
  101.9 21.8 %collective-permute-start.15 = (bf16[4,32,2048]{2,1,0:T(8,128)(2,1)S(1)}, bf16[4,32,2048]{2,1,0:T(8,128)(2,1)S(1)}, u32[]{:S(2)}, u32[]{:S(2)}) collective-permute-start(bf16[4,32,2048]{2,1,0:T(8,128)(2,1)S(1)} %get-tuple-element.364), channel_id=1, source_target_pairs={{0,4},{1,5},{2,6},{3,7},{4,0},{5,1},{6,2},{7,3},{8,12},{9,13},{10,... | collective-permute-start | bytes 1572872 | tf_op jit(solution)/shard_map/ppermute | solution.py:610
  102.5 21.2 %collective-permute-start.16 = (bf16[4,32,2048]{2,1,0:T(8,128)(2,1)S(1)}, bf16[4,32,2048]{2,1,0:T(8,128)(2,1)S(1)}, u32[]{:S(2)}, u32[]{:S(2)}) collective-permute-start(bf16[4,32,2048]{2,1,0:T(8,128)(2,1)S(1)} %get-tuple-element.363), channel_id=1, source_target_pairs={{0,2},{1,3},{2,0},{3,1},{4,6},{5,7},{6,4},{7,5},{8,10},{9,11},{10,... | collective-permute-start | bytes 1572872 | tf_op jit(solution)/shard_map/ppermute | solution.py:610
  123.9 31.3 %collective-permute-start.17 = (bf16[8,32,2048]{2,1,0:T(8,128)(2,1)S(1)}, bf16[8,32,2048]{2,1,0:T(8,128)(2,1)S(1)}, u32[]{:S(2)}, u32[]{:S(2)}) collective-permute-start(bf16[8,32,2048]{2,1,0:T(8,128)(2,1)S(1)} %pad_maximum_fusion.5), channel_id=1, source_target_pairs={{0,2},{1,3},{2,0},{3,1},{4,6},{5,7},{6,4},{7,5},{8,10},{9,11},{10,... | collective-permute-start | bytes 3145736 | tf_op jit(solution)/shard_map/ppermute | solution.py:610
  124.5 30.6 %collective-permute-start.18 = (bf16[8,32,2048]{2,1,0:T(8,128)(2,1)S(1)}, bf16[8,32,2048]{2,1,0:T(8,128)(2,1)S(1)}, u32[]{:S(2)}, u32[]{:S(2)}) collective-permute-start(bf16[8,32,2048]{2,1,0:T(8,128)(2,1)S(1)} %pad_maximum_fusion.6), channel_id=1, source_target_pairs={{0,4},{1,5},{2,6},{3,7},{4,0},{5,1},{6,2},{7,3},{8,12},{9,13},{10,... | collective-permute-start | bytes 3145736 | tf_op jit(solution)/shard_map/ppermute | solution.py:610
  203.9 30.3 %collective-permute-start.23 = (bf16[8,32,2048]{2,1,0:T(8,128)(2,1)}, bf16[8,32,2048]{2,1,0:T(8,128)(2,1)}, u32[]{:S(2)}, u32[]{:S(2)}) collective-permute-start(bf16[8,32,2048]{2,1,0:T(8,128)(2,1)} %get-tuple-element.220), channel_id=1, source_target_pairs={{0,2},{1,3},{2,0},{3,1},{4,6},{5,7},{6,4},{7,5},{8,10},{9,11},{10,... | collective-permute-start | bytes 3145736 | tf_op jit(solution)/shard_map/ppermute | solution.py:610
  205.3 28.8 %collective-permute-start.24 = (bf16[8,32,2048]{2,1,0:T(8,128)(2,1)}, bf16[8,32,2048]{2,1,0:T(8,128)(2,1)}, u32[]{:S(2)}, u32[]{:S(2)}) collective-permute-start(bf16[8,32,2048]{2,1,0:T(8,128)(2,1)} %get-tuple-element.221), channel_id=1, source_target_pairs={{0,4},{1,5},{2,6},{3,7},{4,0},{5,1},{6,2},{7,3},{8,12},{9,13},{10,... | collective-permute-start | bytes 3145736 | tf_op jit(solution)/shard_map/ppermute | solution.py:610
  237.7 21.5 %collective-permute-start.25 = (bf16[4,32,2048]{2,1,0:T(8,128)(2,1)}, bf16[4,32,2048]{2,1,0:T(8,128)(2,1)S(1)}, u32[]{:S(2)}, u32[]{:S(2)}) collective-permute-start(bf16[4,32,2048]{2,1,0:T(8,128)(2,1)} %get-tuple-element.235), channel_id=1, source_target_pairs={{0,4},{1,5},{2,6},{3,7},{4,0},{5,1},{6,2},{7,3},{8,12},{9,13},{10,... | collective-permute-start | bytes 1572872 | tf_op jit(solution)/shard_map/ppermute | solution.py:610
  239.2 20.0 %collective-permute-start.26 = (bf16[4,32,2048]{2,1,0:T(8,128)(2,1)}, bf16[4,32,2048]{2,1,0:T(8,128)(2,1)S(1)}, u32[]{:S(2)}, u32[]{:S(2)}) collective-permute-start(bf16[4,32,2048]{2,1,0:T(8,128)(2,1)} %get-tuple-element.236), channel_id=1, source_target_pairs={{0,2},{1,3},{2,0},{3,1},{4,6},{5,7},{6,4},{7,5},{8,10},{9,11},{10,... | collective-permute-start | bytes 1572872 | tf_op jit(solution)/shard_map/ppermute | solution.py:610
  239.8 19.5 %collective-permute-start.27 = (bf16[16,32,2048]{2,1,0:T(8,128)(2,1)}, bf16[16,32,2048]{2,1,0:T(8,128)(2,1)S(1)}, u32[]{:S(2)}, u32[]{:S(2)}) collective-permute-start(bf16[16,32,2048]{2,1,0:T(8,128)(2,1)} %get-tuple-element.237), channel_id=1, source_target_pairs={{0,1},{1,0},{2,3},{3,2},{4,5},{5,4},{6,7},{7,6},{8,9},{9,8},{10,11... | collective-permute-start | bytes 6291464 | tf_op jit(solution)/shard_map/ppermute | solution.py:610
  239.8 19.5 %collective-permute-start.28 = (bf16[16,32,2048]{2,1,0:T(8,128)(2,1)}, bf16[16,32,2048]{2,1,0:T(8,128)(2,1)}, u32[]{:S(2)}, u32[]{:S(2)}) collective-permute-start(bf16[16,32,2048]{2,1,0:T(8,128)(2,1)} %get-tuple-element.238), channel_id=1, source_target_pairs={{0,1},{1,0},{2,3},{3,2},{4,5},{5,4},{6,7},{7,6},{8,9},{9,8},{10,11... | collective-permute-start | bytes 6291464 | tf_op jit(solution)/shard_map/ppermute | solution.py:610
  269.0 31.9 %collective-permute-start.29 = (bf16[2,32,4096]{2,1,0:T(8,128)(2,1)}, bf16[2,32,4096]{2,1,0:T(8,128)(2,1)}, u32[]{:S(2)}, u32[]{:S(2)}) collective-permute-start(bf16[2,32,4096]{2,1,0:T(8,128)(2,1)} %get-tuple-element.256), channel_id=1, source_target_pairs={{0,8},{1,9},{2,10},{3,11},{4,12},{5,13},{6,14},{7,15},{8,0},{9,1},... | collective-permute-start | bytes 1572872 | tf_op jit(solution)/shard_map/ppermute | solution.py:610
  270.5 30.4 %collective-permute-start.30 = (bf16[8,32,2048]{2,1,0:T(8,128)(2,1)}, bf16[8,32,2048]{2,1,0:T(8,128)(2,1)}, u32[]{:S(2)}, u32[]{:S(2)}) collective-permute-start(bf16[8,32,2048]{2,1,0:T(8,128)(2,1)} %get-tuple-element.257), channel_id=1, source_target_pairs={{0,2},{1,3},{2,0},{3,1},{4,6},{5,7},{6,4},{7,5},{8,10},{9,11},{10,... | collective-permute-start | bytes 3145736 | tf_op jit(solution)/shard_map/ppermute | solution.py:610
  271.9 29.0 %collective-permute-start.31 = (bf16[8,32,2048]{2,1,0:T(8,128)(2,1)}, bf16[8,32,2048]{2,1,0:T(8,128)(2,1)}, u32[]{:S(2)}, u32[]{:S(2)}) collective-permute-start(bf16[8,32,2048]{2,1,0:T(8,128)(2,1)} %get-tuple-element.258), channel_id=1, source_target_pairs={{0,4},{1,5},{2,6},{3,7},{4,0},{5,1},{6,2},{7,3},{8,12},{9,13},{10,... | collective-permute-start | bytes 3145736 | tf_op jit(solution)/shard_map/ppermute | solution.py:610
  306.3 17.8 %collective-permute-start.32 = (bf16[1,32,4096]{2,1,0:T(8,128)(2,1)S(1)}, bf16[1,32,4096]{2,1,0:T(8,128)(2,1)S(1)}, u32[]{:S(2)}, u32[]{:S(2)}) collective-permute-start(bf16[1,32,4096]{2,1,0:T(8,128)(2,1)S(1)} %copy-done.36), channel_id=1, source_target_pairs={{0,16},{1,17},{2,18},{3,19},{4,20},{5,21},{6,22},{7,23},{8,24},{9,... | collective-permute-start | bytes 786440 | tf_op jit(solution)/shard_map/ppermute | solution.py:610
  308.8 15.4 %collective-permute-start.33 = (bf16[4,32,2048]{2,1,0:T(8,128)(2,1)}, bf16[4,32,2048]{2,1,0:T(8,128)(2,1)S(1)}, u32[]{:S(2)}, u32[]{:S(2)}) collective-permute-start(bf16[4,32,2048]{2,1,0:T(8,128)(2,1)} %get-tuple-element.271), channel_id=1, source_target_pairs={{0,4},{1,5},{2,6},{3,7},{4,0},{5,1},{6,2},{7,3},{8,12},{9,13},{10,... | collective-permute-start | bytes 1572872 | tf_op jit(solution)/shard_map/ppermute | solution.py:610
  310.3 13.9 %collective-permute-start.34 = (bf16[4,32,2048]{2,1,0:T(8,128)(2,1)}, bf16[4,32,2048]{2,1,0:T(8,128)(2,1)S(1)}, u32[]{:S(2)}, u32[]{:S(2)}) collective-permute-start(bf16[4,32,2048]{2,1,0:T(8,128)(2,1)} %get-tuple-element.272), channel_id=1, source_target_pairs={{0,2},{1,3},{2,0},{3,1},{4,6},{5,7},{6,4},{7,5},{8,10},{9,11},{10,... | collective-permute-start | bytes 1572872 | tf_op jit(solution)/shard_map/ppermute | solution.py:610
  329.5 29.0 %collective-permute-start.37 = (bf16[2,32,4096]{2,1,0:T(8,128)(2,1)}, bf16[2,32,4096]{2,1,0:T(8,128)(2,1)S(1)}, u32[]{:S(2)}, u32[]{:S(2)}) collective-permute-start(bf16[2,32,4096]{2,1,0:T(8,128)(2,1)} %get-tuple-element.299), channel_id=1, source_target_pairs={{0,8},{1,9},{2,10},{3,11},{4,12},{5,13},{6,14},{7,15},{8,0},{9,1},... | collective-permute-start | bytes 1572872 | tf_op jit(solution)/shard_map/ppermute | solution.py:610
  337.1 27.3 %collective-permute-start.38 = (bf16[8,32,2048]{2,1,0:T(8,128)(2,1)}, bf16[8,32,2048]{2,1,0:T(8,128)(2,1)S(1)}, u32[]{:S(2)}, u32[]{:S(2)}) collective-permute-start(bf16[8,32,2048]{2,1,0:T(8,128)(2,1)} %get-tuple-element.300), channel_id=1, source_target_pairs={{0,2},{1,3},{2,0},{3,1},{4,6},{5,7},{6,4},{7,5},{8,10},{9,11},{10,... | collective-permute-start | bytes 3145736 | tf_op jit(solution)/shard_map/ppermute | solution.py:610
  338.6 27.9 %collective-permute-start.39 = (bf16[8,32,2048]{2,1,0:T(8,128)(2,1)}, bf16[8,32,2048]{2,1,0:T(8,128)(2,1)}, u32[]{:S(2)}, u32[]{:S(2)}) collective-permute-start(bf16[8,32,2048]{2,1,0:T(8,128)(2,1)} %get-tuple-element.301), channel_id=1, source_target_pairs={{0,4},{1,5},{2,6},{3,7},{4,0},{5,1},{6,2},{7,3},{8,12},{9,13},{10,... | collective-permute-start | bytes 3145736 | tf_op jit(solution)/shard_map/ppermute | solution.py:610
  355.7 19.4 %all-to-all-start.1 = ((bf16[32,2,3216]{2,1,0:T(2,128)(2,1)}), bf16[32,2,3216]{2,1,0:T(2,128)(2,1)S(1)}, u32[]{:S(2)}, u32[]{:S(2)}) async-start(bf16[32,2,3216]{2,1,0:T(2,128)(2,1)} %reshape.183), calls=%async_computation.1 | async-start | bytes 851968 | tf_op jit(solution)/shard_map/all_to_all | solution.py:948
  372.0 12.9 %collective-permute-start.41 = (bf16[4,32,2048]{2,1,0:T(8,128)(2,1)}, bf16[4,32,2048]{2,1,0:T(8,128)(2,1)S(1)}, u32[]{:S(2)}, u32[]{:S(2)}) collective-permute-start(bf16[4,32,2048]{2,1,0:T(8,128)(2,1)} %get-tuple-element.314), channel_id=1, source_target_pairs={{0,4},{1,5},{2,6},{3,7},{4,0},{5,1},{6,2},{7,3},{8,12},{9,13},{10,... | collective-permute-start | bytes 1572872 | tf_op jit(solution)/shard_map/ppermute | solution.py:610
  (57 other events, 412.6 us)
Sparse Core Ops, SparseCore 0:
  63.8 86.6 all-gather.1

commit v3 on v2

--- a/solution.py
+++ b/solution.py
@@ -60,12 +60,19 @@
     return pl.BlockSpec(shape, lambda *_: (0,) * len(shape))
 
 
-def fill(dst, code, own, other, block):
-    for m in range(own.shape[0]):
-        at = code[m]
-        dst[pl.ds(pl.multiple_of(at * block, block), block), :] = own[m]
-        at = at ^ 1
-        dst[pl.ds(pl.multiple_of(at * block, block), block), :] = other[m]
+def fill(dst, code, pairs, block):
+    position = 0
+    for own, other in pairs:
+        for m in range(own.shape[0]):
+            at = code[position]
+            dst[pl.ds(pl.multiple_of(at * block, block), block), :] = own[m]
+            at = at ^ 1
+            dst[pl.ds(pl.multiple_of(at * block, block), block), :] = other[m]
+            position += 1
+
+
+def paired(refs):
+    return list(zip(refs[0::2], refs[1::2]))
 
 
 def halves_of(value, core, count=None):
@@ -79,12 +86,12 @@
     )
 
 
-def qkv_body(
-    code_ref, x_ref, mod_ref, own_a, other_a, own_b, other_b, gain_ref, seg_ref,
-    attn_ref, out_ref, inv_ref, w_ref,
-):
+def qkv_body(code_ref, x_ref, mod_ref, gain_ref, seg_ref, *refs):
+    *sources, attn_ref, out_ref, inv_ref, w_ref = refs
+    half = len(sources) // 2
+    first, second = paired(sources[:half]), paired(sources[half:])
     step = pl.program_id(0)
-    block = own_a.shape[1]
+    block = x_ref.shape[1] // BLOCKS
 
     @pl.when(step == 0)
     def _():
@@ -94,7 +101,7 @@
 
     @pl.when(step < 2)
     def _():
-        fill(w_ref, code_ref.at[0], own_a, other_a, block)
+        fill(w_ref, code_ref.at[0], first, block)
         raw = dot(attn_ref[...], w_ref[...])
         seg = seg_ref[...]
         high, low = split_low(raw * raw)
@@ -107,7 +114,7 @@
 
     @pl.when(step >= 2)
     def _():
-        fill(w_ref, code_ref.at[1], own_b, other_b, block)
+        fill(w_ref, code_ref.at[1], second, block)
 
     @pl.when(step == 2)
     def _():
@@ -116,10 +123,14 @@
 
 def qkv_rows(x, mod, pieces, gain, seg):
     tokens, width = x.shape
-    code, own_a, other_a, own_b, other_b = pieces
-    part = (own_a.shape[0], own_a.shape[1], width)
-    first = pl.BlockSpec(part, lambda n: (0, 0, jnp.minimum(n, 1)))
-    second = pl.BlockSpec(part, lambda n: (0, 0, jnp.maximum(n - 2, 0)))
+    code, first, second = pieces
+    one = [
+        pl.BlockSpec(a.shape[:2] + (width,), lambda n: (0, 0, jnp.minimum(n, 1))) for a in first
+    ]
+    two = [
+        pl.BlockSpec(a.shape[:2] + (width,), lambda n: (0, 0, jnp.maximum(n - 2, 0)))
+        for a in second
+    ]
     return pl.pallas_call(
         qkv_body,
         grid=(4,),
@@ -127,12 +138,10 @@
             pl.BlockSpec(memory_space=pltpu.SMEM),
             whole((tokens, width)),
             whole(mod.shape),
-            first,
-            first,
-            second,
-            second,
             whole(gain.shape),
             whole(seg.shape),
+            *one,
+            *two,
         ],
         out_specs=[
             whole((tokens, width)),
@@ -147,9 +156,9 @@
             jax.ShapeDtypeStruct((width, 4 * width), BF),
         ],
         compiler_params=PARAMS,
-        cost_estimate=cost(6 * tokens * width * width, 16 * tokens * width + 16 * width * width, 0, 1),
+        cost_estimate=cost(6 * tokens * width * width, 16 * tokens * width + 16 * width * width, 0, 2),
         name="qkv",
-    )(code, x, mod, own_a, other_a, own_b, other_b, gain, seg)
+    )(code, x, mod, gain, seg, *first, *second)
 
 
 def attend_body(q_ref, k_ref, v_ref, start_ref, out_ref, low_ref, inv_ref):
@@ -197,7 +206,7 @@
         ],
         compiler_params=PARAMS,
         cost_estimate=cost(
-            16 * pairs * tokens * tokens * HDIM, 20 * tokens * HDIM * pairs, 2 * pairs * tokens * tokens, 1
+            16 * pairs * tokens * tokens * HDIM, 20 * tokens * HDIM * pairs, 2 * pairs * tokens * tokens, 0.02
         ),
         name="attend",
     )(qkv, qkv, qkv, start)
@@ -481,15 +490,14 @@
     )(x, resid, mod, g, weights)
 
 
-def mlp_body(
-    info_ref, x_ref, g_ref, own_a, other_a, own_b, other_b, bias_ref, *refs, first
-):
+def mlp_body(info_ref, x_ref, g_ref, bias_ref, *refs, first, sources):
+    a_refs, b_refs, refs = refs[:sources], refs[sources : 2 * sources], refs[2 * sources :]
     if first:
         out_ref, gx_ref, keep_a, send_a, keep_b, send_b, bias_g, up_w, down_w = refs
     else:
         out_in, gx_in, out_ref, gx_ref, keep_a, send_a, keep_b, send_b, bias_g, up_w, down_w = refs
     core = info_ref[2, 0]
-    block = own_a.shape[1]
+    block = x_ref.shape[1] // BLOCKS
 
     @pl.when(pl.program_id(0) == 0)
     def _():
@@ -499,11 +507,11 @@
     step = pl.program_id(0)
     size = up_w.shape[1]
     per = down_w.shape[0] // size
-    fill(up_w, info_ref.at[0], own_a, other_a, block)
+    fill(up_w, info_ref.at[0], paired(a_refs), block)
 
     @pl.when(step % per == 0)
     def _():
-        fill(down_w, info_ref.at[1], own_b, other_b, block)
+        fill(down_w, info_ref.at[1], paired(b_refs), block)
 
     root = np.float32(np.sqrt(2.0 / np.pi))
     x, g, up = x_ref[...], g_ref[...], up_w[...]
@@ -528,11 +536,12 @@
     block, per = 512, width // 512
     lead, rows = BLOCKS // 2, width // BLOCKS
     part_a = pl.BlockSpec((lead, rows, block), lambda f: (0, 0, f))
-    part_b = pl.BlockSpec((lead, rows, width), lambda f: (0, 0, f // per))
-    if len(pieces) == 5:
-        matrices = pieces[1:]
+    if len(pieces) == 3:
+        matrices = (*pieces[1], *pieces[2])
         total = matrices[0].shape[2]
-        sources = [part_a, part_a, part_b, part_b]
+        sources = [
+            pl.BlockSpec(m.shape[:2] + (block,), lambda f: (0, 0, f)) for m in pieces[1]
+        ] + [pl.BlockSpec(m.shape[:2] + (width,), lambda f: (0, 0, f // per)) for m in pieces[2]]
     else:
         matrices = [pieces[0].reshape(lead, 2, rows, -1)] * 4
         total = matrices[0].shape[3] // 2
@@ -548,11 +557,11 @@
     single = pl.BlockSpec((tokens, width), lambda f: (0, 0), pipeline_mode=pl.Buffered(1))
     carried = () if carried is None else tuple(carried)
     return pl.pallas_call(
-        partial(mlp_body, first=not carried),
+        partial(mlp_body, first=not carried, sources=len(matrices) // 2),
         grid=(steps,),
         in_specs=[pl.BlockSpec(memory_space=pltpu.SMEM), single, single]
+        + [pl.BlockSpec((1, block), lambda f: (0, at * per + f))]
         + sources
-        + [pl.BlockSpec((1, block), lambda f: (0, at * per + f))]
         + [single] * len(carried),
         out_specs=[single, single, part_a, part_a, grad_b, grad_b]
         + [pl.BlockSpec((1, block), lambda f: (0, f))],
@@ -560,7 +569,7 @@
         + [jax.ShapeDtypeStruct((lead, rows, total), BF)] * 4
         + [jax.ShapeDtypeStruct((1, total), F32)],
         scratch_shapes=[pltpu.VMEM((width, block), BF), pltpu.VMEM((width, width), BF)],
-        input_output_aliases={8 + i: i for i in range(len(carried))},
+        input_output_aliases={4 + len(matrices) + i: i for i in range(len(carried))},
         compiler_params=PARAMS,
         cost_estimate=cost(
             12 * tokens * width * total,
@@ -569,7 +578,7 @@
             20 if carried else 0.3,
         ),
         name="mlp",
-    )(info, x, g, *matrices, bias, *carried)
+    )(info, x, g, bias, *matrices, *carried)
 
 
 def fold_body(bit_ref, *refs, plan, out_count):
@@ -628,7 +637,7 @@
 def gathered_pieces(full):
     rows, cols = full.shape
     cut = full.reshape(BLOCKS // 2, 2, rows // BLOCKS, 2, cols // 2)
-    return [cut[:, i, :, j] for j in range(2) for i in range(2)]
+    return [tuple(cut[:, i, :, j] for i in range(2)) for j in range(2)]
 
 
 def halve(pieces, axis, bit_value, count, mask):
@@ -699,16 +708,23 @@
     def end_xy(self):
         self.block = [join(b, c) for b, c in zip(self.block, self.came)]
 
-    def start_core(self):
-        self.came = [swap(b, self.count, 1) for b in self.block]
+    def start_early(self):
+        self.early = [swap(b, self.count, 1) for b in self.block]
+
+    def start_late(self):
+        self.late = [swap(c, self.count, 1) for c in self.came]
 
     def pieces(self, code):
-        return (code, self.block[0], self.came[0], self.block[1], self.came[1])
+        sides = [
+            (b, e, c, l) for b, e, c, l in zip(self.block, self.early, self.came, self.late)
+        ]
+        return (code, *sides)
 
 
 class Scatter:
-    def __init__(self, kept, send, bits, count, heavy=0):
+    def __init__(self, kept, send, pieces, bits, count, heavy=0):
         self.bits, self.count, self.heavy = bits, count, heavy
+        self.pieces = pieces
         self.kept, self.send = list(kept), list(send)
         self.left = 0
         self.done = None
@@ -726,8 +742,11 @@
         everything = slice(0, width // split)
         half = lambda cols: ((lead // 2, own, cols), BF)
         if self.left == 5:
-            plan = ((0, everything, None, 1, 0, 0),)
-            outs = [((lead, own, width), F32)]
+            plan, outs, at = [], [], 0
+            for i, cols in enumerate(self.pieces):
+                plan.append((0, slice(at, at + cols), None, 1, i, 0))
+                outs.append(((lead, own, cols), F32))
+                at += cols
         elif self.left == 1:
             plan, sums = [], [0, 0]
             for side in range(2):
@@ -745,7 +764,7 @@
         weight = self.heavy if self.left == 5 else 0
         outs = fold(self.bits, parts, tuple(plan), outs, split, weight)
         if self.left == 5:
-            self.done, self.send = outs[0][0], list(outs)
+            self.done, self.send = [o[0] for o in outs], list(outs)
         else:
             self.kept, self.send = list(outs[0::2]), list(outs[1::2])
 
@@ -806,6 +825,9 @@
         code = jnp.stack([codes(o, me) for o in orders])
         bits = jnp.stack([lax.rem(lax.div(me, np.int32(1 << b)), np.int32(2)) for b in range(5)])
         one.start_z(4)
+        one.came[0], two.block = after(one.came[0], two.block)
+        one.end_z()
+        one.start_z(3)
     else:
         wide = [lax.all_gather(s, AXES, axis=0, tiled=True) for s in shards]
         code = plain
@@ -835,10 +857,6 @@
         jnp.zeros((6 * model_width,), F32), ada_bias.astype(F32), (me * bias_own,)
     )
     part = modul_part + bias_row[None, :]
-    if quick:
-        part = land(part, one)
-        one.end_z()
-        one.start_z(3)
     bit_values = [lax.rem(lax.div(me, np.int32(1 << b)), np.int32(2)) for b in range(exponent)]
     for b in range(exponent):
         size = part.shape[0] // 2
@@ -855,19 +873,16 @@
             came = land(came, one, two)
             one.end_xy()
             two.end_z()
-            came, last_shard = after(came, shards[2])
-            last_full = lax.all_gather(last_shard, AXES, axis=0, tiled=True)
+            one.start_early()
             one.start_xy(1, 2)
             two.start_z(3)
         part = keep + came
     mod = part.reshape(6, model_width)
     if quick:
         mod = land(mod, one, two)
-        one.end_xy()
         two.end_z()
-        one.start_core()
+        one.start_late()
         two.start_xy(2, 1)
-        mod = land(mod, one)
         pieces = one.pieces(code)
     else:
         pieces = (code, *gathered_pieces(wide[0]))
@@ -883,20 +898,21 @@
     if quick:
         qkv = land(qkv, two)
         two.end_xy()
-        qkv, *two.block = after(qkv, *two.block)
+        qkv, last_shard, *two.block = after(qkv, shards[2], *two.block)
+        last_full = lax.all_gather(last_shard, AXES, axis=0, tiled=True)
+        two.start_early()
         two.start_xy(1, 2)
     attended, low, inverse = attend(qkv, start)
     projected, mlp_in, grad_mlp = project(live, x, attended, weights, mod, cot)
     if quick:
         mlp_in = land(mlp_in, two)
-        two.end_xy()
-        two.start_core()
+        two.start_late()
     bias = hidden_order(up_bias_full)
     pieces = two.pieces(code) if quick else (wide[1],)
     *carried, keep_a, send_a, keep_b, send_b, bias_one = mlp(info, mlp_in, grad_mlp, pieces, bias, 0)
     kept_one, send_one = (keep_a, keep_b), (send_a, send_b)
     if quick:
-        first = Scatter(kept_one, send_one, bits, count, 1 << 33)
+        first = Scatter(kept_one, send_one, (half, half), bits, count, 1 << 33)
         carried[0] = land(carried[0], first)
         carried[0] = leave(carried[0], first)
     pieces = (last_full if quick else wide[2],)
@@ -904,9 +920,8 @@
         info_plain, mlp_in, grad_mlp, pieces, bias, half // model_width, carried
     )
     kept_two, send_two = (keep_a, keep_b), (send_a, send_b)
-    up_bias_grad = jnp.concatenate([bias_one, bias_two], axis=1)
     if quick:
-        second = Scatter(kept_two, send_two, bits, count)
+        second = Scatter(kept_two, send_two, (half, half), bits, count)
         mlp_out = land(mlp_out, first)
         mlp_out = leave(mlp_out, first)
     block_out, grad_resid, grad_attended, grad_proj, sums_two = residual_back(
@@ -921,24 +936,37 @@
     if quick:
         dqkv = land(dqkv, first, second)
         dqkv = leave(dqkv, first, second)
-    head_scale_part = jnp.sum(head_sums[0].reshape(heads, HDIM), axis=1)
     keep_a, send_a, keep_b, send_b = weight_grad(core, attn_in, dqkv, attended, grad_proj)
     kept_three, send_three = (keep_a, keep_b), (send_a, send_b)
     if quick:
-        third = Scatter(kept_three, send_three, bits, count)
+        third = Scatter(
+            kept_three, send_three, (3 * model_width, model_width), bits, count
+        )
         dqkv = land(dqkv, first, second)
         dqkv = leave(dqkv, first, second)
         dqkv = land(dqkv, third)
         dqkv = leave(dqkv, third)
     input_grad, sums_one = input_back(x, grad_resid, mod, dqkv, weights)
     if not quick:
-        mlp_own = [scatter_rows(kept_one, send_one, count, me), scatter_rows(kept_two, send_two, count, me)]
+        mlp_own = [
+            scatter_rows(kept_one, send_one, count, me),
+            scatter_rows(kept_two, send_two, count, me),
+        ]
+        up_own = jnp.concatenate([m[:, :half] for m in mlp_own], axis=1)
+        down_own = jnp.concatenate([m[:, half:] for m in mlp_own], axis=1)
         attn_own = scatter_rows(kept_three, send_three, count, me)
+        qkv_own, out_own = attn_own[:, : 3 * model_width], attn_own[:, 3 * model_width :]
     block_out = block_out.reshape(tokens.shape)
     input_grad = input_grad.reshape(tokens.shape)
+    if quick:
+        sums_one, bias_one, bias_two, head_sums, sums_two = after(
+            sums_one, bias_one, bias_two, head_sums, sums_two
+        )
+    up_bias_grad = jnp.concatenate([bias_one, bias_two], axis=1)
     grad_modul = jnp.concatenate(
         [sums_two[0], sums_two[1], sums_one[0], sums_two[2], sums_one[1], sums_two[3]]
     ).astype(BF)
+    head_scale_part = jnp.sum(head_sums[0].reshape(heads, HDIM), axis=1)
     bias_high, bias_low = split_low(hidden_back(up_bias_grad).reshape(count, -1))
     head_high, head_low = split_low(head_scale_part)
     common = jnp.concatenate([grad_modul.reshape(-1), head_high, head_low])
@@ -955,10 +983,8 @@
         small, input_grad = after(small, input_grad)
         small = leave(small, third)
         third.add()
-        mlp_own = [first.done, second.done]
-        attn_own = third.done
-    up_own = jnp.concatenate([m[:, :half] for m in mlp_own], axis=1)
-    down_own = jnp.concatenate([m[:, half:] for m in mlp_own], axis=1)
+        up_own, down_own = [jnp.concatenate(m, axis=1) for m in zip(first.done, second.done)]
+        qkv_own, out_own = third.done
     modul_cols = image_count * 6 * model_width
     grad_modul_all = small[:, :modul_cols].reshape(count * image_count, 6 * model_width)
     tail = jnp.sum(small[:, modul_cols:].astype(F32), axis=0)
@@ -982,8 +1008,6 @@
         precision=lax.Precision.HIGHEST,
         preferred_element_type=F32,
     )
-    qkv_own = attn_own[:, : 3 * model_width]
-    out_own = attn_own[:, 3 * model_width :]
     up_own = hidden_back(up_own)
     down_own = jnp.swapaxes(down_own.reshape(own, ratio, model_width), 0, 1).reshape(
         ratio * own, model_width

time: 436 us -> 416 us (0.954)
  local copies, waits for them, and re-layouts: 41.2 us -> 24.4 us
  other arithmetic: 23 us -> 11.7 us
    concatenate x9 -> x7, other arithmetic: 8.79 us -> 2.36 us  [join(): return jnp.concatenate([block, came])]
    slice x4 -> x0, local copies, waits for them, and re-layouts: 4.81 us -> none  [the longest x1 1.77 us: per_device(): qkv_own = attn_own[:, :3 * model_width]]
    ppermute x45 -> x49, starting transfers between devices: 43 us -> 46 us  [swap(): return lax.ppermute(block, AXES, [(i, i ^ mask) for i in range(count)])]
    ppermute x45 -> x49, waiting for transfers between devices: 85.9 us -> 86.4 us  [swap(): return lax.ppermute(block, AXES, [(i, i ^ mask) for i in range(count)])]
  transfers between devices with their start and end apart: 48 -> 52, of which waited for: 20 -> 26; matrix products, arithmetic and copies ran while one was open for 14% -> 8% of each run, Pallas kernels for 42% -> 45%
where the time goes in v3:
time: 416 us; the launch traced here: 410 us
  Pallas kernels  207 us (50%)
  waiting for transfers between devices  89.6 us (22%)
  starting transfers between devices  56.8 us (14%)
  local copies, waits for them, and re-layouts  24.4 us (6%)
  between operations  17.1 us (4%)
  other arithmetic  11.7 us (3%)
    ppermute x49, waiting for transfers between devices, swap(): return lax.ppermute(block, AXES, [(i, i ^ mask) for i in range(count)])  86.4 us
    pallas_call x2, Pallas kernels, mlp(): pl.pallas_call(partial(mlp_body, first=not carried, sources=len(matrices)...  55.6 us
    pallas_call x15, Pallas kernels, fold(): pl.pallas_call(partial(fold_body, plan=plan, out_count=len(outs)), grid=(...  48.8 us
    ppermute x49, starting transfers between devices, swap(): return lax.ppermute(block, AXES, [(i, i ^ mask) for i in range(count)])  46 us
    pallas_call x1, Pallas kernels, attend_back(): pl.pallas_call(attend_back_body, grid=(some,), in_specs=[pair(0), pair(pa...  26.9 us
    pallas_call x1, Pallas kernels, qkv_rows(): pl.pallas_call(qkv_body, grid=(4,), in_specs=[pl.BlockSpec(memory_space=p...  17.6 us
    pallas_call x1, Pallas kernels, attend(): pl.pallas_call(attend_body, grid=(pairs,), in_specs=[pair(0), pair(pairs)...  14.2 us
    pallas_call x1, Pallas kernels, weight_grad(): pl.pallas_call(weight_grad_body, grid=(4,), in_specs=[pl.BlockSpec(memory...  12.8 us
  transfers between devices with their start and end apart: 52, of which 26 were waited for; matrix products, arithmetic and copies ran while one was open for 8% of the time, Pallas kernels for 45%

profile of v3, /device:TPU:0, one launch (start us, length us, event | category | flops | bytes accessed | tf_op | source)
XLA Modules:
  0.0 409.9 jit_solution(9519991499975496023)
XLA Ops:
  9.3 7.3 %all-to-all-start = ((bf16[32,1,130]{2,1,0:T(2,128)(2,1)}), bf16[32,1,130]{2,1,0:T(2,128)(2,1)S(1)}, u32[]{:S(2)}, u32[]{:S(2)}) async-start(bf16[32,1,130]{2,1,0:T(2,128)(2,1)} %broadcast_in_dim.17), calls=%async_computation | async-start | bytes 65536 | tf_op jit(solution)/shard_map/all_to_all | solution.py:843
  17.6 2.7 collective-permute-start.1
  26.2 6.7 %collective-permute-done.1 = bf16[1,32,4096]{2,1,0:T(8,128)(2,1)S(1)} collective-permute-done((bf16[1,32,4096]{2,1,0:T(8,128)(2,1)S(1)}, bf16[1,32,4096]{2,1,0:T(8,128)(2,1)S(1)}, u32[]{:S(2)}, u32[]{:S(2)}) %collective-permute-start.1) | collective-permute-done | bytes 262176 | tf_op jit(solution)/shard_map/ppermute | solution.py:619
  36.3 10.3 %collective-permute-done.2 = bf16[2,32,4096]{2,1,0:T(8,128)(2,1)S(1)} collective-permute-done((bf16[2,32,4096]{2,1,0:T(8,128)(2,1)S(1)}, bf16[2,32,4096]{2,1,0:T(8,128)(2,1)S(1)}, u32[]{:S(2)}, u32[]{:S(2)}) %collective-permute-start.2) | collective-permute-done | bytes 524320 | tf_op jit(solution)/shard_map/ppermute | solution.py:619
  57.6 7.0 %collective-permute-done.7 = bf16[1,32,4096]{2,1,0:T(8,128)(2,1)S(1)} collective-permute-done((bf16[1,32,4096]{2,1,0:T(8,128)(2,1)S(1)}, bf16[1,32,4096]{2,1,0:T(8,128)(2,1)S(1)}, u32[]{:S(2)}, u32[]{:S(2)}) %collective-permute-start.7) | collective-permute-done | bytes 262176 | tf_op jit(solution)/shard_map/ppermute | solution.py:619
  71.5 3.5 collective-permute-start.9
  75.1 6.1 %collective-permute-done.9 = f32[1,6144]{1,0:T(1,128)S(1)} collective-permute-done((f32[1,6144]{1,0:T(1,128)S(1)}, f32[1,6144]{1,0:T(1,128)S(1)}, u32[]{:S(2)}, u32[]{:S(2)}) %collective-permute-start.9) | collective-permute-done | bytes 24608 | tf_op jit(solution)/shard_map/ppermute | solution.py:619
  83.3 7.2 %collective-permute-done.10.refs_2_ = bf16[8,32,2048]{2,1,0:T(8,128)(2,1)} collective-permute-done((bf16[8,32,2048]{2,1,0:T(8,128)(2,1)S(1)}, bf16[8,32,2048]{2,1,0:T(8,128)(2,1)}, u32[]{:S(2)}, u32[]{:S(2)}) %collective-permute-start.10) | collective-permute-done | bytes 1048608 | tf_op jit(solution)/shard_map/ppermute | solution.py:619
  98.3 17.6 %qkv.1 = (bf16[680,1024]{1,0:T(8,128)(2,1)}, bf16[680,3072]{1,0:T(8,128)(2,1)}, f32[680,2048]{1,0:T(8,128)}, bf16[1024,4096]{1,0:T(8,128)(2,1)}) custom-call(s32[2,16]{1,0:T(2,128)} %pad_add_fusion.code_ref, bf16[680,1024]{1,0:T(8,128)(2,1)} %bitcast.68, f32[6,1024]{1,0:T(8,128)} %reshape.113.mod_ref, f32[1,1024]{1,0:T(1,128)} %broadcast_in_dim_reshape.3.gain_ref, ...), custom_call_target="tpu_custom_call" | custom-call | flops 8556380160 | bytes 55836672 | tf_op jit(solution)/shard_map/qkv/pallas_call | solution.py:134
  119.8 14.2 %attend.1 = (bf16[680,1024]{1,0:T(8,128)(2,1)}, bf16[680,1024]{1,0:T(8,128)(2,1)}, f32[680,1024]{1,0:T(8,128)}) custom-call(bf16[680,3072]{1,0:T(8,128)(2,1)} %get-tuple-element.198.q_ref.k_ref.v_ref, bf16[680,3072]{1,0:T(8,128)(2,1)} %get-tuple-element.198.q_ref.k_ref.v_ref, bf16[680,3072]{1,0:T(8,128)(2,1)} %get-tuple-element.198.q_ref.k_ref.v_ref, ...), custom_call_target="tpu_custom_call" | custom-call | flops 75759616 | bytes 139264 | tf_op jit(solution)/shard_map/attend/pallas_call | solution.py:197
  134.0 7.1 %project.1 = (f32[680,1024]{1,0:T(8,128)}, bf16[680,1024]{1,0:T(8,128)(2,1)}, bf16[680,1024]{1,0:T(8,128)(2,1)}) custom-call(s32[1]{0:T(128)S(6)} %select_n.44.live_ref, bf16[680,1024]{1,0:T(8,128)(2,1)} %bitcast.69, bf16[680,1024]{1,0:T(8,128)(2,1)} %get-tuple-element.199.att_ref, bf16[1024,4096]{1,0:T(8,128)(2,1)} %get-tuple-element.200.w_ref, ...), custom_call_target="tpu_custom_call" | custom-call | flops 1426063360 | bytes 11845632 | tf_op jit(solution)/shard_map/project/pallas_call | solution.py:328
  148.2 27.4 %mlp.2 = (f32[680,1024]{1,0:T(8,128)}, f32[680,1024]{1,0:T(8,128)}, bf16[16,32,2048]{2,1,0:T(8,128)(2,1)}, bf16[16,32,2048]{2,1,0:T(8,128)(2,1)}, bf16[16,32,204...) custom-call(s32[3,16]{1,0:T(4,128)} %add_add_fusion.info_ref, ...), custom_call_target="tpu_custom_call" | custom-call | flops 5133828096 | bytes 6704332 | tf_op jit(solution)/shard_map/mlp/pallas_call | solution.py:559
  177.3 4.1 collective-permute-done.25.refs_1_
  183.3 6.0 %fold.15 = (bf16[8,32,2048]{2,1,0:T(8,128)(2,1)}, bf16[8,32,2048]{2,1,0:T(8,128)(2,1)}, bf16[8,32,2048]{2,1,0:T(8,128)(2,1)}, bf16[8,32,2048]{2,1,0:T(8,128)(2,1)}) custom-call(s32[5]{0:T(128)} %stack.35.bit_ref, bf16[16,32,2048]{2,1,0:T(8,128)(2,1)} %get-tuple-element.214.refs_0_, bf16[16,32,2048]{2,1,0:T(8,128)(2,1)} %copy-done.3, ...), custom_call_target="tpu_custom_call" | custom-call | bytes 160 | tf_op jit(solution)/shard_map/fold/pallas_call | solution.py:606
  191.3 3.2 all-gather.2.cloned.1.call-done
  194.5 28.2 %mlp.3 = (f32[680,1024]{1,0:T(8,128)}, f32[680,1024]{1,0:T(8,128)}, bf16[16,32,2048]{2,1,0:T(8,128)(2,1)}, bf16[16,32,2048]{2,1,0:T(8,128)(2,1)}, bf16[16,32,204...) custom-call(s32[3,16]{1,0:T(4,128)} %concatenate.85.info_ref, ...), custom_call_target="tpu_custom_call", output_to_operand_aliasing={{0}: (8, {}), {1}: (9, {})} | custom-call | flops 342255206400 | bytes 669777920 | tf_op jit(solution)/shard_map/mlp/pallas_call | solution.py:559
  222.7 3.5 fold.16
  228.8 11.0 %residual_back.1 = (bf16[680,1024]{1,0:T(8,128)(2,1)}, f32[680,1024]{1,0:T(8,128)}, bf16[680,1024]{1,0:T(8,128)(2,1)}, bf16[680,1024]{1,0:T(8,128)(2,1)}, f32[8,1024]{1,0:T(8,128)}) custom-call(s32[1]{0:T(128)S(6)} %select_n.44.live_ref, bf16[680,1024]{1,0:T(8,128)(2,1)} %bitcast.70, f32[680,1024]{1,0:T(8,128)} %get-tuple-element.201.proj_ref, ...), custom_call_target="tpu_custom_call" | custom-call | flops 28521267200 | bytes 473825280 | tf_op jit(solution)/shard_map/residual_back/pallas_call | solution.py:377
  242.6 3.6 fold.17
  246.2 5.9 %fold.18 = (bf16[8,32,2048]{2,1,0:T(8,128)(2,1)}, bf16[8,32,2048]{2,1,0:T(8,128)(2,1)}, bf16[8,32,2048]{2,1,0:T(8,128)(2,1)}, bf16[8,32,2048]{2,1,0:T(8,128)(2,1)}) custom-call(s32[5]{0:T(128)} %stack.35.bit_ref, bf16[16,32,2048]{2,1,0:T(8,128)(2,1)} %get-tuple-element.247.refs_0_, bf16[16,32,2048]{2,1,0:T(8,128)(2,1)} %copy-done.1, ...), custom_call_target="tpu_custom_call" | custom-call | bytes 160 | tf_op jit(solution)/shard_map/fold/pallas_call | solution.py:606
  255.6 26.9 %attend_back.1 = (bf16[3,680,1024]{2,1,0:T(8,128)(2,1)}, f32[8,1024]{1,0:T(8,128)}) custom-call(bf16[680,3072]{1,0:T(8,128)(2,1)} %get-tuple-element.198.q_ref.k_ref.v_ref, bf16[680,3072]{1,0:T(8,128)(2,1)} %get-tuple-element.198.q_ref.k_ref.v_ref, bf16[680,3072]{1,0:T(8,128)(2,1)} %get-tuple-element.198.q_ref.k_ref.v_ref, ...), custom_call_target="tpu_custom_call" | custom-call | flops 189399040000 | bytes 417792000 | tf_op jit(solution)/shard_map/attend_back/pallas_call | solution.py:281
  284.6 3.3 fold.20
  291.0 12.8 %weight_grad.1 = (bf16[16,32,2048]{2,1,0:T(8,128)(2,1)}, bf16[16,32,2048]{2,1,0:T(8,128)(2,1)}, bf16[16,32,2048]{2,1,0:T(8,128)(2,1)}, bf16[16,32,2048]{2,1,0:T(8,128)(2,1)}) custom-call(s32[1]{0:T(128)} %bitcast.32.core_ref, bf16[680,1024]{1,0:T(8,128)(2,1)} %get-tuple-element.286.x_ref, bf16[3,680,1024]{2,1,0:T(8,128)(2,1)} %get-tuple-element.297.g_ref, ...), custom_call_target="tpu_custom_call" | custom-call | flops 114085068800 | bytes 334888960 | tf_op jit(solution)/shard_map/weight_grad/pallas_call | solution.py:422
  311.4 5.9 %fold.23 = (bf16[8,32,2048]{2,1,0:T(8,128)(2,1)}, bf16[8,32,2048]{2,1,0:T(8,128)(2,1)}, bf16[8,32,2048]{2,1,0:T(8,128)(2,1)}, bf16[8,32,2048]{2,1,0:T(8,128)(2,1)}) custom-call(s32[5]{0:T(128)} %stack.35.bit_ref, bf16[16,32,2048]{2,1,0:T(8,128)(2,1)} %get-tuple-element.291.refs_0_, bf16[16,32,2048]{2,1,0:T(8,128)(2,1)} %collective-permute-done.39.refs_1_, ...), custom_call_target="tpu_custom_call" | custom-call | bytes 160 | tf_op jit(solution)/shard_map/fold/pallas_call | solution.py:606
  319.3 12.8 %input_back.1 = (f32[680,1024]{1,0:T(8,128)}, f32[8,1024]{1,0:T(8,128)}) custom-call(bf16[680,1024]{1,0:T(8,128)(2,1)} %bitcast.71, f32[680,1024]{1,0:T(8,128)} %get-tuple-element.235.resid_ref, f32[6,1024]{1,0:T(8,128)} %reshape.113.mod_ref, bf16[3,680,1024]{2,1,0:T(8,128)(2,1)} %get-tuple-element.297.g_ref, bf16[1024,4096]{1,0:T(8,128)(2,1)} %get-tuple-element.200.w_ref), custom_call_target="tpu_custom_call" | custom-call | flops 85563801600 | bytes 348651520 | tf_op jit(solution)/shard_map/input_back/pallas_call | solution.py:472
  337.1 3.5 all-to-all-start.1
  345.2 3.3 fold.25
  352.6 12.1 %collective-permute-done.44.refs_1_ = bf16[1,32,4096]{2,1,0:T(8,128)(2,1)S(1)} collective-permute-done((bf16[1,32,4096]{2,1,0:T(8,128)(2,1)S(1)}, bf16[1,32,4096]{2,1,0:T(8,128)(2,1)S(1)}, u32[]{:S(2)}, u32[]{:S(2)}) %collective-permute-start.44) | collective-permute-done | bytes 262176 | tf_op jit(solution)/shard_map/ppermute | solution.py:619
  375.1 2.7 reshape.121
  379.1 4.1 %collective-permute-done.47.refs_1_ = bf16[2,32,4096]{2,1,0:T(8,128)(2,1)} collective-permute-done((bf16[2,32,4096]{2,1,0:T(8,128)(2,1)}, bf16[2,32,4096]{2,1,0:T(8,128)(2,1)}, u32[]{:S(2)}, u32[]{:S(2)}) %collective-permute-start.47) | collective-permute-done | bytes 524320 | tf_op jit(solution)/shard_map/ppermute | solution.py:619
  385.6 2.9 collective-permute-start.48
  392.5 7.8 %collective-permute-done.48.refs_1_ = bf16[1,32,4096]{2,1,0:T(8,128)(2,1)S(1)} collective-permute-done((bf16[1,32,4096]{2,1,0:T(8,128)(2,1)}, bf16[1,32,4096]{2,1,0:T(8,128)(2,1)S(1)}, u32[]{:S(2)}, u32[]{:S(2)}) %collective-permute-start.48) | collective-permute-done | bytes 262176 | tf_op jit(solution)/shard_map/ppermute | solution.py:619
  (278 shorter events, 111.8 us)
Async XLA Ops:
  9.3 15.6 %all-to-all-start = ((bf16[32,1,130]{2,1,0:T(2,128)(2,1)}), bf16[32,1,130]{2,1,0:T(2,128)(2,1)S(1)}, u32[]{:S(2)}, u32[]{:S(2)}) async-start(bf16[32,1,130]{2,1,0:T(2,128)(2,1)} %broadcast_in_dim.17), calls=%async_computation | async-start | bytes 65536 | tf_op jit(solution)/shard_map/all_to_all | solution.py:843
  16.6 177.9 %all-gather.2.cloned.1.call-start = ((), (), s32[]{:S(2)}) async-start(), calls=%async_computation.2 | async-start | bytes 8650752 | tf_op jit(solution)/shard_map/all_gather | solution.py:902
  17.6 15.3 %collective-permute-start.1 = (bf16[1,32,4096]{2,1,0:T(8,128)(2,1)S(1)}, bf16[1,32,4096]{2,1,0:T(8,128)(2,1)S(1)}, u32[]{:S(2)}, u32[]{:S(2)}) collective-permute-start(bf16[1,32,4096]{2,1,0:T(8,128)(2,1)S(1)} %maximum_bitcast_fusion.2), channel_id=1, source_target_pairs={{0,16},{1,17},{2,18},{3,19},{4,20},{5,21},{6,22},{7,23},{8,24},{9,... | collective-permute-start | bytes 786440 | tf_op jit(solution)/shard_map/ppermute | solution.py:619
  49.3 15.3 %collective-permute-start.5 = (bf16[4,32,2048]{2,1,0:T(8,128)(2,1)S(1)}, bf16[4,32,2048]{2,1,0:T(8,128)(2,1)S(1)}, u32[]{:S(2)}, u32[]{:S(2)}) collective-permute-start(bf16[4,32,2048]{2,1,0:T(8,128)(2,1)S(1)} %get-tuple-element.380), channel_id=1, source_target_pairs={{0,4},{1,5},{2,6},{3,7},{4,0},{5,1},{6,2},{7,3},{8,12},{9,13},{10,... | collective-permute-start | bytes 1572872 | tf_op jit(solution)/shard_map/ppermute | solution.py:619
  50.8 13.8 %collective-permute-start.6 = (bf16[4,32,2048]{2,1,0:T(8,128)(2,1)S(1)}, bf16[4,32,2048]{2,1,0:T(8,128)(2,1)S(1)}, u32[]{:S(2)}, u32[]{:S(2)}) collective-permute-start(bf16[4,32,2048]{2,1,0:T(8,128)(2,1)S(1)} %get-tuple-element.379), channel_id=1, source_target_pairs={{0,2},{1,3},{2,0},{3,1},{4,6},{5,7},{6,4},{7,5},{8,10},{9,11},{10,... | collective-permute-start | bytes 1572872 | tf_op jit(solution)/shard_map/ppermute | solution.py:619
  65.9 24.6 %collective-permute-start.10 = (bf16[8,32,2048]{2,1,0:T(8,128)(2,1)S(1)}, bf16[8,32,2048]{2,1,0:T(8,128)(2,1)}, u32[]{:S(2)}, u32[]{:S(2)}) collective-permute-start(bf16[8,32,2048]{2,1,0:T(8,128)(2,1)S(1)} %pad_maximum_fusion.1.refs_0_), channel_id=1, source_target_pairs={{0,2},{1,3},{2,0},{3,1},{4,6},{5,7},{6,4},{7,5},{8,10},{9,11},{10,... | collective-permute-start | bytes 3145736 | tf_op jit(solution)/shard_map/ppermute | solution.py:619
  68.5 24.5 %collective-permute-start.11 = (bf16[8,32,2048]{2,1,0:T(8,128)(2,1)}, bf16[8,32,2048]{2,1,0:T(8,128)(2,1)}, u32[]{:S(2)}, u32[]{:S(2)}) collective-permute-start(bf16[8,32,2048]{2,1,0:T(8,128)(2,1)} %pad_maximum_fusion.2.refs_4_), channel_id=1, source_target_pairs={{0,4},{1,5},{2,6},{3,7},{4,0},{5,1},{6,2},{7,3},{8,12},{9,13},{10,... | collective-permute-start | bytes 3145736 | tf_op jit(solution)/shard_map/ppermute | solution.py:619
  75.0 19.2 %collective-permute-start.13 = (bf16[8,32,2048]{2,1,0:T(8,128)(2,1)S(1)}, bf16[8,32,2048]{2,1,0:T(8,128)(2,1)}, u32[]{:S(2)}, u32[]{:S(2)}) collective-permute-start(bf16[8,32,2048]{2,1,0:T(8,128)(2,1)S(1)} %pad_maximum_fusion.1.refs_0_), channel_id=1, source_target_pairs={{0,1},{1,0},{2,3},{3,2},{4,5},{5,4},{6,7},{7,6},{8,9},{9,8},{10,11... | collective-permute-start | bytes 3145736 | tf_op jit(solution)/shard_map/ppermute | solution.py:619
  93.7 22.2 %collective-permute-start.17 = (bf16[4,32,2048]{2,1,0:T(8,128)(2,1)S(1)}, bf16[4,32,2048]{2,1,0:T(8,128)(2,1)S(1)}, u32[]{:S(2)}, u32[]{:S(2)}) collective-permute-start(bf16[4,32,2048]{2,1,0:T(8,128)(2,1)S(1)} %get-tuple-element.378), channel_id=1, source_target_pairs={{0,4},{1,5},{2,6},{3,7},{4,0},{5,1},{6,2},{7,3},{8,12},{9,13},{10,... | collective-permute-start | bytes 1572872 | tf_op jit(solution)/shard_map/ppermute | solution.py:619
  94.3 21.6 %collective-permute-start.18 = (bf16[4,32,2048]{2,1,0:T(8,128)(2,1)S(1)}, bf16[4,32,2048]{2,1,0:T(8,128)(2,1)S(1)}, u32[]{:S(2)}, u32[]{:S(2)}) collective-permute-start(bf16[4,32,2048]{2,1,0:T(8,128)(2,1)S(1)} %get-tuple-element.377), channel_id=1, source_target_pairs={{0,2},{1,3},{2,0},{3,1},{4,6},{5,7},{6,4},{7,5},{8,10},{9,11},{10,... | collective-permute-start | bytes 1572872 | tf_op jit(solution)/shard_map/ppermute | solution.py:619
  116.2 27.3 %collective-permute-start.19 = (bf16[8,32,2048]{2,1,0:T(8,128)(2,1)S(1)}, bf16[8,32,2048]{2,1,0:T(8,128)(2,1)}, u32[]{:S(2)}, u32[]{:S(2)}) collective-permute-start(bf16[8,32,2048]{2,1,0:T(8,128)(2,1)S(1)} %pad_maximum_fusion.3.refs_0_), channel_id=1, source_target_pairs={{0,2},{1,3},{2,0},{3,1},{4,6},{5,7},{6,4},{7,5},{8,10},{9,11},{10,... | collective-permute-start | bytes 3145736 | tf_op jit(solution)/shard_map/ppermute | solution.py:619
  116.8 26.9 %collective-permute-start.20 = (bf16[8,32,2048]{2,1,0:T(8,128)(2,1)S(1)}, bf16[8,32,2048]{2,1,0:T(8,128)(2,1)}, u32[]{:S(2)}, u32[]{:S(2)}) collective-permute-start(bf16[8,32,2048]{2,1,0:T(8,128)(2,1)S(1)} %pad_maximum_fusion.4.refs_4_), channel_id=1, source_target_pairs={{0,4},{1,5},{2,6},{3,7},{4,0},{5,1},{6,2},{7,3},{8,12},{9,13},{10,... | collective-permute-start | bytes 3145736 | tf_op jit(solution)/shard_map/ppermute | solution.py:619
  119.2 26.6 %collective-permute-start.21 = (bf16[8,32,2048]{2,1,0:T(8,128)(2,1)S(1)}, bf16[8,32,2048]{2,1,0:T(8,128)(2,1)}, u32[]{:S(2)}, u32[]{:S(2)}) collective-permute-start(bf16[8,32,2048]{2,1,0:T(8,128)(2,1)S(1)} %pad_maximum_fusion.3.refs_0_), channel_id=1, source_target_pairs={{0,1},{1,0},{2,3},{3,2},{4,5},{5,4},{6,7},{7,6},{8,9},{9,8},{10,11... | collective-permute-start | bytes 3145736 | tf_op jit(solution)/shard_map/ppermute | solution.py:619
  119.3 26.5 %collective-permute-start.23 = (bf16[8,32,2048]{2,1,0:T(8,128)(2,1)S(1)}, bf16[8,32,2048]{2,1,0:T(8,128)(2,1)}, u32[]{:S(2)}, u32[]{:S(2)}) collective-permute-start(bf16[8,32,2048]{2,1,0:T(8,128)(2,1)S(1)} %pad_maximum_fusion.4.refs_4_), channel_id=1, source_target_pairs={{0,1},{1,0},{2,3},{3,2},{4,5},{5,4},{6,7},{7,6},{8,9},{9,8},{10,11... | collective-permute-start | bytes 3145736 | tf_op jit(solution)/shard_map/ppermute | solution.py:619
  189.3 33.4 %collective-permute-start.27 = (bf16[8,32,2048]{2,1,0:T(8,128)(2,1)}, bf16[8,32,2048]{2,1,0:T(8,128)(2,1)}, u32[]{:S(2)}, u32[]{:S(2)}) collective-permute-start(bf16[8,32,2048]{2,1,0:T(8,128)(2,1)} %get-tuple-element.223), channel_id=1, source_target_pairs={{0,2},{1,3},{2,0},{3,1},{4,6},{5,7},{6,4},{7,5},{8,10},{9,11},{10,... | collective-permute-start | bytes 3145736 | tf_op jit(solution)/shard_map/ppermute | solution.py:619
  190.7 32.0 %collective-permute-start.28 = (bf16[8,32,2048]{2,1,0:T(8,128)(2,1)}, bf16[8,32,2048]{2,1,0:T(8,128)(2,1)}, u32[]{:S(2)}, u32[]{:S(2)}) collective-permute-start(bf16[8,32,2048]{2,1,0:T(8,128)(2,1)} %get-tuple-element.224), channel_id=1, source_target_pairs={{0,4},{1,5},{2,6},{3,7},{4,0},{5,1},{6,2},{7,3},{8,12},{9,13},{10,... | collective-permute-start | bytes 3145736 | tf_op jit(solution)/shard_map/ppermute | solution.py:619
  226.2 14.4 %collective-permute-start.29 = (bf16[4,32,2048]{2,1,0:T(8,128)(2,1)}, bf16[4,32,2048]{2,1,0:T(8,128)(2,1)S(1)}, u32[]{:S(2)}, u32[]{:S(2)}) collective-permute-start(bf16[4,32,2048]{2,1,0:T(8,128)(2,1)} %get-tuple-element.237), channel_id=1, source_target_pairs={{0,4},{1,5},{2,6},{3,7},{4,0},{5,1},{6,2},{7,3},{8,12},{9,13},{10,... | collective-permute-start | bytes 1572872 | tf_op jit(solution)/shard_map/ppermute | solution.py:619
  227.8 14.0 %collective-permute-start.30 = (bf16[4,32,2048]{2,1,0:T(8,128)(2,1)}, bf16[4,32,2048]{2,1,0:T(8,128)(2,1)S(1)}, u32[]{:S(2)}, u32[]{:S(2)}) collective-permute-start(bf16[4,32,2048]{2,1,0:T(8,128)(2,1)} %get-tuple-element.238), channel_id=1, source_target_pairs={{0,2},{1,3},{2,0},{3,1},{4,6},{5,7},{6,4},{7,5},{8,10},{9,11},{10,... | collective-permute-start | bytes 1572872 | tf_op jit(solution)/shard_map/ppermute | solution.py:619
  252.1 30.4 %collective-permute-start.33 = (bf16[2,32,4096]{2,1,0:T(8,128)(2,1)}, bf16[2,32,4096]{2,1,0:T(8,128)(2,1)}, u32[]{:S(2)}, u32[]{:S(2)}) collective-permute-start(bf16[2,32,4096]{2,1,0:T(8,128)(2,1)} %get-tuple-element.258), channel_id=1, source_target_pairs={{0,8},{1,9},{2,10},{3,11},{4,12},{5,13},{6,14},{7,15},{8,0},{9,1},... | collective-permute-start | bytes 1572872 | tf_op jit(solution)/shard_map/ppermute | solution.py:619
  253.6 28.9 %collective-permute-start.34 = (bf16[8,32,2048]{2,1,0:T(8,128)(2,1)}, bf16[8,32,2048]{2,1,0:T(8,128)(2,1)}, u32[]{:S(2)}, u32[]{:S(2)}) collective-permute-start(bf16[8,32,2048]{2,1,0:T(8,128)(2,1)} %get-tuple-element.259), channel_id=1, source_target_pairs={{0,2},{1,3},{2,0},{3,1},{4,6},{5,7},{6,4},{7,5},{8,10},{9,11},{10,... | collective-permute-start | bytes 3145736 | tf_op jit(solution)/shard_map/ppermute | solution.py:619
  254.2 28.4 %collective-permute-start.35 = (bf16[8,32,2048]{2,1,0:T(8,128)(2,1)}, bf16[8,32,2048]{2,1,0:T(8,128)(2,1)}, u32[]{:S(2)}, u32[]{:S(2)}) collective-permute-start(bf16[8,32,2048]{2,1,0:T(8,128)(2,1)} %get-tuple-element.260), channel_id=1, source_target_pairs={{0,4},{1,5},{2,6},{3,7},{4,0},{5,1},{6,2},{7,3},{8,12},{9,13},{10,... | collective-permute-start | bytes 3145736 | tf_op jit(solution)/shard_map/ppermute | solution.py:619
  288.0 16.4 %collective-permute-start.36 = (bf16[1,32,4096]{2,1,0:T(8,128)(2,1)S(1)}, bf16[1,32,4096]{2,1,0:T(8,128)(2,1)S(1)}, u32[]{:S(2)}, u32[]{:S(2)}) collective-permute-start(bf16[1,32,4096]{2,1,0:T(8,128)(2,1)S(1)} %copy-done.38), channel_id=1, source_target_pairs={{0,16},{1,17},{2,18},{3,19},{4,20},{5,21},{6,22},{7,23},{8,24},{9,... | collective-permute-start | bytes 786440 | tf_op jit(solution)/shard_map/ppermute | solution.py:619
  289.0 15.4 %collective-permute-start.37 = (bf16[4,32,2048]{2,1,0:T(8,128)(2,1)}, bf16[4,32,2048]{2,1,0:T(8,128)(2,1)S(1)}, u32[]{:S(2)}, u32[]{:S(2)}) collective-permute-start(bf16[4,32,2048]{2,1,0:T(8,128)(2,1)} %get-tuple-element.273), channel_id=1, source_target_pairs={{0,4},{1,5},{2,6},{3,7},{4,0},{5,1},{6,2},{7,3},{8,12},{9,13},{10,... | collective-permute-start | bytes 1572872 | tf_op jit(solution)/shard_map/ppermute | solution.py:619
  289.6 14.8 %collective-permute-start.38 = (bf16[4,32,2048]{2,1,0:T(8,128)(2,1)}, bf16[4,32,2048]{2,1,0:T(8,128)(2,1)S(1)}, u32[]{:S(2)}, u32[]{:S(2)}) collective-permute-start(bf16[4,32,2048]{2,1,0:T(8,128)(2,1)} %get-tuple-element.274), channel_id=1, source_target_pairs={{0,2},{1,3},{2,0},{3,1},{4,6},{5,7},{6,4},{7,5},{8,10},{9,11},{10,... | collective-permute-start | bytes 1572872 | tf_op jit(solution)/shard_map/ppermute | solution.py:619
  309.7 30.9 %collective-permute-start.41 = (bf16[2,32,4096]{2,1,0:T(8,128)(2,1)}, bf16[2,32,4096]{2,1,0:T(8,128)(2,1)S(1)}, u32[]{:S(2)}, u32[]{:S(2)}) collective-permute-start(bf16[2,32,4096]{2,1,0:T(8,128)(2,1)} %get-tuple-element.309), channel_id=1, source_target_pairs={{0,8},{1,9},{2,10},{3,11},{4,12},{5,13},{6,14},{7,15},{8,0},{9,1},... | collective-permute-start | bytes 1572872 | tf_op jit(solution)/shard_map/ppermute | solution.py:619
  317.3 25.4 %collective-permute-start.42 = (bf16[8,32,2048]{2,1,0:T(8,128)(2,1)}, bf16[8,32,2048]{2,1,0:T(8,128)(2,1)S(1)}, u32[]{:S(2)}, u32[]{:S(2)}) collective-permute-start(bf16[8,32,2048]{2,1,0:T(8,128)(2,1)} %get-tuple-element.310), channel_id=1, source_target_pairs={{0,2},{1,3},{2,0},{3,1},{4,6},{5,7},{6,4},{7,5},{8,10},{9,11},{10,... | collective-permute-start | bytes 3145736 | tf_op jit(solution)/shard_map/ppermute | solution.py:619
  317.8 25.2 %collective-permute-start.43 = (bf16[8,32,2048]{2,1,0:T(8,128)(2,1)}, bf16[8,32,2048]{2,1,0:T(8,128)(2,1)}, u32[]{:S(2)}, u32[]{:S(2)}) collective-permute-start(bf16[8,32,2048]{2,1,0:T(8,128)(2,1)} %get-tuple-element.311), channel_id=1, source_target_pairs={{0,4},{1,5},{2,6},{3,7},{4,0},{5,1},{6,2},{7,3},{8,12},{9,13},{10,... | collective-permute-start | bytes 3145736 | tf_op jit(solution)/shard_map/ppermute | solution.py:619
  337.1 33.8 %all-to-all-start.1 = ((bf16[32,2,3216]{2,1,0:T(2,128)(2,1)}), bf16[32,2,3216]{2,1,0:T(2,128)(2,1)S(1)}, u32[]{:S(2)}, u32[]{:S(2)}) async-start(bf16[32,2,3216]{2,1,0:T(2,128)(2,1)} %reshape.185), calls=%async_computation.1 | async-start | bytes 851968 | tf_op jit(solution)/shard_map/all_to_all | solution.py:976
  348.5 16.1 %collective-permute-start.45 = (bf16[4,32,2048]{2,1,0:T(8,128)(2,1)}, bf16[4,32,2048]{2,1,0:T(8,128)(2,1)S(1)}, u32[]{:S(2)}, u32[]{:S(2)}) collective-permute-start(bf16[4,32,2048]{2,1,0:T(8,128)(2,1)} %get-tuple-element.324), channel_id=1, source_target_pairs={{0,4},{1,5},{2,6},{3,7},{4,0},{5,1},{6,2},{7,3},{8,12},{9,13},{10,... | collective-permute-start | bytes 1572872 | tf_op jit(solution)/shard_map/ppermute | solution.py:619
  350.3 14.4 %collective-permute-start.46 = (bf16[4,32,2048]{2,1,0:T(8,128)(2,1)}, bf16[4,32,2048]{2,1,0:T(8,128)(2,1)S(1)}, u32[]{:S(2)}, u32[]{:S(2)}) collective-permute-start(bf16[4,32,2048]{2,1,0:T(8,128)(2,1)} %get-tuple-element.325), channel_id=1, source_target_pairs={{0,2},{1,3},{2,0},{3,1},{4,6},{5,7},{6,4},{7,5},{8,10},{9,11},{10,... | collective-permute-start | bytes 1572872 | tf_op jit(solution)/shard_map/ppermute | solution.py:619
  350.6 14.0 %collective-permute-start.44 = (bf16[1,32,4096]{2,1,0:T(8,128)(2,1)S(1)}, bf16[1,32,4096]{2,1,0:T(8,128)(2,1)S(1)}, u32[]{:S(2)}, u32[]{:S(2)}) collective-permute-start(bf16[1,32,4096]{2,1,0:T(8,128)(2,1)S(1)} %copy-done.40), channel_id=1, source_target_pairs={{0,16},{1,17},{2,18},{3,19},{4,20},{5,21},{6,22},{7,23},{8,24},{9,... | collective-permute-start | bytes 786440 | tf_op jit(solution)/shard_map/ppermute | solution.py:619
  385.6 14.7 %collective-permute-start.48 = (bf16[1,32,4096]{2,1,0:T(8,128)(2,1)}, bf16[1,32,4096]{2,1,0:T(8,128)(2,1)S(1)}, u32[]{:S(2)}, u32[]{:S(2)}) collective-permute-start(bf16[1,32,4096]{2,1,0:T(8,128)(2,1)} %get-tuple-element.346), channel_id=1, source_target_pairs={{0,16},{1,17},{2,18},{3,19},{4,20},{5,21},{6,22},{7,23},{8,24},{9,... | collective-permute-start | bytes 786440 | tf_op jit(solution)/shard_map/ppermute | solution.py:619
  (64 other events, 570.4 us)
Sparse Core Ops, SparseCore 0:
  116.3 78.1 all-gather.1

commit v4 on v3

--- a/solution.py
+++ b/solution.py
@@ -30,7 +30,10 @@
 LEVEL_ENDS = np.cumsum(np.square(np.array(scale_sides))).astype(np.int32)
 LAST = (((1,), (1,)), ((), ()))
 FIRST = (((0,), (0,)), ((), ()))
-PARAMS = pltpu.CompilerParams(vmem_limit_bytes=58 << 20)
+
+
+def grant(mebibytes):
+    return pltpu.CompilerParams(vmem_limit_bytes=mebibytes << 20)
 
 
 def dot(left, right, dims=(((1,), (0,)), ((), ()))):
@@ -57,7 +60,7 @@
 
 
 def whole(shape):
-    return pl.BlockSpec(shape, lambda *_: (0,) * len(shape))
+    return pl.BlockSpec(shape, lambda *_: (0,) * len(shape), pipeline_mode=pl.Buffered(1))
 
 
 def fill(dst, code, pairs, block):
@@ -155,7 +158,7 @@
             jax.ShapeDtypeStruct((tokens, 2 * width), F32),
             jax.ShapeDtypeStruct((width, 4 * width), BF),
         ],
-        compiler_params=PARAMS,
+        compiler_params=grant(58),
         cost_estimate=cost(6 * tokens * width * width, 16 * tokens * width + 16 * width * width, 0, 2),
         name="qkv",
     )(code, x, mod, gain, seg, *first, *second)
@@ -204,7 +207,7 @@
             jax.ShapeDtypeStruct((tokens, 2 * HDIM * pairs), BF),
             jax.ShapeDtypeStruct((tokens, 2 * HDIM * pairs), F32),
         ],
-        compiler_params=PARAMS,
+        compiler_params=grant(12),
         cost_estimate=cost(
             16 * pairs * tokens * tokens * HDIM, 20 * tokens * HDIM * pairs, 2 * pairs * tokens * tokens, 0.02
         ),
@@ -231,11 +234,17 @@
     fine = att_ref[...].astype(F32) + low_ref[...].astype(F32)
     inner = head_sums(scaled.astype(F32) * fine)
     acc_q[...] = jnp.zeros_like(acc_q)
+    spans = ((0, 256, 0), (256, 432, 128), (432, tokens, 384))
+    q_turned = q.T
+    k_turned = [k[first:last].T for first, last, _ in spans]
+    upper = lax.broadcasted_iota(jnp.int32, q_turned.shape, 0) < HDIM
+    nothing = jnp.zeros_like(q_turned)
     for h in range(2):
         mine = left if h == 0 else lane >= HDIM
         spare = HDIM * (1 - h)
         q_own = jnp.where(mine, q, zero)
-        k_own = jnp.where(mine, k, zero)
+        queries = jnp.where(upper if h == 0 else ~upper, q_turned, nothing)
+        heads = slice(HDIM * h, HDIM * (h + 1))
         g_own = jnp.where(mine, scaled, zero)
         high, low = split_low(-inner[h])
         wide = q.shape
@@ -245,11 +254,12 @@
             jnp.where(lane == spare + 1, jnp.broadcast_to(low, wide), g_own),
         )
         v_more = jnp.where(mine, v, jnp.where((lane >= spare) & (lane < spare + 2), one, zero))
-        for first, last, row in ((0, 256, 0), (256, 432, 128), (432, tokens, 384)):
-            score = dot(k[first:last], q_own[row:], LAST)
+        g_turned = g_more.T
+        for (first, last, row), k_part in zip(spans, k_turned):
+            score = dot(k[first:last], queries[:, row:])
             key = lax.broadcasted_iota(jnp.int32, score.shape, 0) + first
             weight = jnp.where(key < limit_ref[:, row:], jnp.exp(score), 0.0).astype(BF)
-            slope = dot(v_more[first:last], g_more[row:], LAST)
+            slope = dot(v_more[first:last], g_turned[:, row:])
             slope = (weight.astype(F32) * slope).astype(BF)
             dv = dot(weight, g_own[row:])
             dk = dot(slope, q_own[row:])
@@ -259,9 +269,9 @@
             else:
                 acc_v[first:last, :] += dv
                 acc_k[first:last, :] += dk
-            acc_q[row:, :] += dot(slope, k_own[first:last], FIRST)
+            acc_q[heads, row:] += dot(k_part[heads], slope)
     gain = gain_ref[...]
-    dq, dk = acc_q[...], acc_k[...]
+    dq, dk = acc_q[...].T, acc_k[...]
     q, k = q.astype(F32), k.astype(F32)
     along = dq * q
     first, second = head_sums(along)
@@ -302,8 +312,9 @@
             jax.ShapeDtypeStruct((3, tokens, 2 * HDIM * some), BF),
             jax.ShapeDtypeStruct((8, 2 * HDIM * some), F32),
         ],
-        scratch_shapes=[pltpu.VMEM((tokens, 2 * HDIM), F32)] * 3,
-        compiler_params=PARAMS,
+        scratch_shapes=[pltpu.VMEM((2 * HDIM, tokens), F32)]
+        + [pltpu.VMEM((tokens, 2 * HDIM), F32)] * 2,
+        compiler_params=grant(58),
         cost_estimate=cost(
             40 * some * tokens * tokens * HDIM, 60 * tokens * HDIM * some, 2 * some * tokens * tokens
         ),
@@ -338,7 +349,7 @@
         ],
         out_specs=[full] * 3,
         out_shape=[jax.ShapeDtypeStruct((tokens, width), t) for t in (F32, BF, BF)],
-        compiler_params=PARAMS,
+        compiler_params=grant(22),
         cost_estimate=cost(2 * tokens * width * width, 14 * tokens * width + 2 * width * width, 0, 1),
         name="project",
     )(live, x, attended, w_vo, mod, cot)
@@ -390,7 +401,7 @@
         out_specs=[full, full, full, full, whole((8, width))],
         out_shape=[jax.ShapeDtypeStruct((tokens, width), t) for t in (BF, F32, BF, BF)]
         + [jax.ShapeDtypeStruct((8, width), F32)],
-        compiler_params=PARAMS,
+        compiler_params=grant(58),
         cost_estimate=cost(2 * tokens * width * width, 28 * tokens * width + 4 * width * width),
         name="residual_back",
     )(live, x, proj, mlp_out, gx, cot, mod, weights)
@@ -431,7 +442,7 @@
         ],
         out_specs=[first, first, second, second],
         out_shape=[jax.ShapeDtypeStruct(part[:2] + (2 * width,), BF)] * 4,
-        compiler_params=PARAMS,
+        compiler_params=grant(58),
         cost_estimate=cost(8 * tokens * width * width, 12 * tokens * width + 8 * width * width),
         name="weight_grad",
     )(core, x, g, attended, grad_proj)
@@ -484,7 +495,7 @@
             jax.ShapeDtypeStruct((tokens, width), F32),
             jax.ShapeDtypeStruct((8, width), F32),
         ],
-        compiler_params=PARAMS,
+        compiler_params=grant(58),
         cost_estimate=cost(6 * tokens * width * width, 16 * tokens * width + 6 * width * width),
         name="input_back",
     )(x, resid, mod, g, weights)
@@ -570,7 +581,7 @@
         + [jax.ShapeDtypeStruct((1, total), F32)],
         scratch_shapes=[pltpu.VMEM((width, block), BF), pltpu.VMEM((width, width), BF)],
         input_output_aliases={4 + len(matrices) + i: i for i in range(len(carried))},
-        compiler_params=PARAMS,
+        compiler_params=grant(58),
         cost_estimate=cost(
             12 * tokens * width * total,
             (8 + 8 * len(carried)) * tokens * width + 8 * total * width,
@@ -609,7 +620,7 @@
         in_specs=[pl.BlockSpec(memory_space=pltpu.SMEM)] + [spec(p.shape) for p in parts],
         out_specs=[spec(s) for s, _ in outs],
         out_shape=[jax.ShapeDtypeStruct(s, t) for s, t in outs],
-        compiler_params=PARAMS,
+        compiler_params=grant(58),
         cost_estimate=cost(weight, 8),
         name="fold",
     )(bits, *parts)
@@ -738,7 +749,7 @@
     def add(self):
         parts = [p for pair in zip(self.kept, self.came) for p in pair]
         lead, own, width = self.kept[0].shape
-        split = {1: 4, 2: 2}.get(self.left, 1)
+        split = {1: 2, 2: 2}.get(self.left, 1)
         everything = slice(0, width // split)
         half = lambda cols: ((lead // 2, own, cols), BF)
         if self.left == 5:

time: 416 us -> 414 us (level)
  local copies, waits for them, and re-layouts: 24.4 us -> 33.1 us
  Pallas kernels: 207 us -> 200 us
  waiting for transfers between devices: 89.6 us -> 84.9 us
    unnamed x95 -> x119, local copies, waits for them, and re-layouts: 5.81 us -> 14.5 us
    pallas_call x1, Pallas kernels: 7.1 us -> 2.85 us  [project(): pl.pallas_call(project_body, grid=(1,), in_specs=[pl.BlockSpec(memory_spa...]
  transfers between devices with their start and end apart: 52 -> 52, of which waited for: 26 -> 24; matrix products, arithmetic and copies ran while one was open for 8% -> 8% of each run, Pallas kernels for 45% -> 44%
where the time goes in v4:
time: 414 us; the launch traced here: 408 us
  Pallas kernels  200 us (48%)
  waiting for transfers between devices  84.9 us (21%)
  starting transfers between devices  57.7 us (14%)
  local copies, waits for them, and re-layouts  33.1 us (8%)
  between operations  17.2 us (4%)
  other arithmetic  11.8 us (3%)
    ppermute x49, waiting for transfers between devices, swap(): return lax.ppermute(block, AXES, [(i, i ^ mask) for i in range(count)])  84.3 us
    pallas_call x2, Pallas kernels, mlp(): pl.pallas_call(partial(mlp_body, first=not carried, sources=len(matrices)...  55.6 us
    ppermute x49, starting transfers between devices, swap(): return lax.ppermute(block, AXES, [(i, i ^ mask) for i in range(count)])  46.9 us
    pallas_call x15, Pallas kernels, fold(): pl.pallas_call(partial(fold_body, plan=plan, out_count=len(outs)), grid=(...  46.7 us
    pallas_call x1, Pallas kernels, attend_back(): pl.pallas_call(attend_back_body, grid=(some,), in_specs=[pair(0), pair(pa...  26.5 us
    pallas_call x1, Pallas kernels, qkv_rows(): pl.pallas_call(qkv_body, grid=(4,), in_specs=[pl.BlockSpec(memory_space=p...  17.6 us
    unnamed x119, local copies, waits for them, and re-layouts  14.5 us
    pallas_call x1, Pallas kernels, attend(): pl.pallas_call(attend_body, grid=(pairs,), in_specs=[pair(0), pair(pairs)...  14.2 us
  transfers between devices with their start and end apart: 52, of which 24 were waited for; matrix products, arithmetic and copies ran while one was open for 8% of the time, Pallas kernels for 44%

profile of v4, /device:TPU:0, one launch (start us, length us, event | category | flops | bytes accessed | tf_op | source)
XLA Modules:
  0.0 408.1 jit_solution(934145677957410572)
XLA Ops:
  9.3 7.3 %all-to-all-start = ((bf16[32,1,130]{2,1,0:T(2,128)(2,1)}), bf16[32,1,130]{2,1,0:T(2,128)(2,1)S(1)}, u32[]{:S(2)}, u32[]{:S(2)}) async-start(bf16[32,1,130]{2,1,0:T(2,128)(2,1)} %broadcast_in_dim.17), calls=%async_computation | async-start | bytes 65536 | tf_op jit(solution)/shard_map/all_to_all | solution.py:854
  17.6 2.7 collective-permute-start.1
  26.2 6.7 %collective-permute-done.1 = bf16[1,32,4096]{2,1,0:T(8,128)(2,1)S(1)} collective-permute-done((bf16[1,32,4096]{2,1,0:T(8,128)(2,1)S(1)}, bf16[1,32,4096]{2,1,0:T(8,128)(2,1)S(1)}, u32[]{:S(2)}, u32[]{:S(2)}) %collective-permute-start.1) | collective-permute-done | bytes 262176 | tf_op jit(solution)/shard_map/ppermute | solution.py:630
  36.3 10.3 %collective-permute-done.2 = bf16[2,32,4096]{2,1,0:T(8,128)(2,1)S(1)} collective-permute-done((bf16[2,32,4096]{2,1,0:T(8,128)(2,1)S(1)}, bf16[2,32,4096]{2,1,0:T(8,128)(2,1)S(1)}, u32[]{:S(2)}, u32[]{:S(2)}) %collective-permute-start.2) | collective-permute-done | bytes 524320 | tf_op jit(solution)/shard_map/ppermute | solution.py:630
  57.6 7.0 %collective-permute-done.7 = bf16[1,32,4096]{2,1,0:T(8,128)(2,1)S(1)} collective-permute-done((bf16[1,32,4096]{2,1,0:T(8,128)(2,1)S(1)}, bf16[1,32,4096]{2,1,0:T(8,128)(2,1)S(1)}, u32[]{:S(2)}, u32[]{:S(2)}) %collective-permute-start.7) | collective-permute-done | bytes 262176 | tf_op jit(solution)/shard_map/ppermute | solution.py:630
  71.5 3.5 collective-permute-start.9
  75.1 6.1 %collective-permute-done.9 = f32[1,6144]{1,0:T(1,128)S(1)} collective-permute-done((f32[1,6144]{1,0:T(1,128)S(1)}, f32[1,6144]{1,0:T(1,128)S(1)}, u32[]{:S(2)}, u32[]{:S(2)}) %collective-permute-start.9) | collective-permute-done | bytes 24608 | tf_op jit(solution)/shard_map/ppermute | solution.py:630
  83.3 7.2 %collective-permute-done.10.refs_2_ = bf16[8,32,2048]{2,1,0:T(8,128)(2,1)} collective-permute-done((bf16[8,32,2048]{2,1,0:T(8,128)(2,1)S(1)}, bf16[8,32,2048]{2,1,0:T(8,128)(2,1)}, u32[]{:S(2)}, u32[]{:S(2)}) %collective-permute-start.10) | collective-permute-done | bytes 1048608 | tf_op jit(solution)/shard_map/ppermute | solution.py:630
  98.3 17.6 %qkv.1 = (bf16[680,1024]{1,0:T(8,128)(2,1)}, bf16[680,3072]{1,0:T(8,128)(2,1)}, f32[680,2048]{1,0:T(8,128)}, bf16[1024,4096]{1,0:T(8,128)(2,1)}) custom-call(s32[2,16]{1,0:T(2,128)} %pad_add_fusion.code_ref, bf16[680,1024]{1,0:T(8,128)(2,1)} %bitcast.62, f32[6,1024]{1,0:T(8,128)} %reshape.113.mod_ref, f32[1,1024]{1,0:T(1,128)} %broadcast_in_dim_reshape.3.gain_ref, ...), custom_call_target="tpu_custom_call" | custom-call | flops 8556380160 | bytes 55836672 | tf_op jit(solution)/shard_map/qkv/pallas_call | solution.py:137
  122.0 14.2 %attend.1 = (bf16[680,1024]{1,0:T(8,128)(2,1)S(1)}, bf16[680,1024]{1,0:T(8,128)(2,1)S(1)}, f32[680,1024]{1,0:T(8,128)S(1)}) custom-call(bf16[680,3072]{1,0:T(8,128)(2,1)S(1)} %copy-done.1, bf16[680,3072]{1,0:T(8,128)(2,1)S(1)} %copy-done.1, bf16[680,3072]{1,0:T(8,128)(2,1)S(1)} %copy-done.1, s32[1,680]{1,0:T(1,128)S(1)} %copy-done.7), custom_call_target="tpu_custom_call" | custom-call | flops 75759616 | bytes 139264 | tf_op jit(solution)/shard_map/attend/pallas_call | solution.py:200
  139.0 2.9 project.1
  150.1 27.4 %mlp.2 = (f32[680,1024]{1,0:T(8,128)}, f32[680,1024]{1,0:T(8,128)}, bf16[16,32,2048]{2,1,0:T(8,128)(2,1)}, bf16[16,32,2048]{2,1,0:T(8,128)(2,1)}, bf16[16,32,204...) custom-call(s32[3,16]{1,0:T(4,128)} %add_add_fusion.info_ref, bf16[680,1024]{1,0:T(8,128)(2,1)} %copy-done.11, ...), custom_call_target="tpu_custom_call" | custom-call | flops 5133828096 | bytes 6704332 | tf_op jit(solution)/shard_map/mlp/pallas_call | solution.py:570
  179.3 5.0 %collective-permute-done.25.refs_1_ = bf16[16,32,2048]{2,1,0:T(8,128)(2,1)S(1)} collective-permute-done((bf16[16,32,2048]{2,1,0:T(8,128)(2,1)}, bf16[16,32,2048]{2,1,0:T(8,128)(2,1)S(1)}, u32[]{:S(2)}, u32[]{:S(2)}) %collective-permute-start.25) | collective-permute-done | bytes 2097184 | tf_op jit(solution)/shard_map/ppermute | solution.py:630
  185.7 5.3 %fold.15 = (bf16[8,32,2048]{2,1,0:T(8,128)(2,1)}, bf16[8,32,2048]{2,1,0:T(8,128)(2,1)}, bf16[8,32,2048]{2,1,0:T(8,128)(2,1)}, bf16[8,32,2048]{2,1,0:T(8,128)(2,1)}) custom-call(s32[5]{0:T(128)} %stack.35.bit_ref, bf16[16,32,2048]{2,1,0:T(8,128)(2,1)} %get-tuple-element.214.refs_0_, bf16[16,32,2048]{2,1,0:T(8,128)(2,1)} %copy-done.15, ...), custom_call_target="tpu_custom_call" | custom-call | bytes 160 | tf_op jit(solution)/shard_map/fold/pallas_call | solution.py:617
  194.5 28.2 %mlp.3 = (f32[680,1024]{1,0:T(8,128)}, f32[680,1024]{1,0:T(8,128)}, bf16[16,32,2048]{2,1,0:T(8,128)(2,1)}, bf16[16,32,2048]{2,1,0:T(8,128)(2,1)}, bf16[16,32,204...) custom-call(s32[3,16]{1,0:T(4,128)} %concatenate.85.info_ref, ...), custom_call_target="tpu_custom_call", output_to_operand_aliasing={{0}: (8, {}), {1}: (9, {})} | custom-call | flops 342255206400 | bytes 669777920 | tf_op jit(solution)/shard_map/mlp/pallas_call | solution.py:570
  222.7 3.5 fold.16
  228.9 11.0 %residual_back.1 = (bf16[680,1024]{1,0:T(8,128)(2,1)}, f32[680,1024]{1,0:T(8,128)}, bf16[680,1024]{1,0:T(8,128)(2,1)}, bf16[680,1024]{1,0:T(8,128)(2,1)}, f32[8,1024]{1,0:T(8,128)}) custom-call(s32[1]{0:T(128)S(6)} %select_n.44.live_ref, bf16[680,1024]{1,0:T(8,128)(2,1)} %bitcast.63, f32[680,1024]{1,0:T(8,128)} %copy-done.9, ...), custom_call_target="tpu_custom_call" | custom-call | flops 28521267200 | bytes 473825280 | tf_op jit(solution)/shard_map/residual_back/pallas_call | solution.py:388
  242.6 3.6 fold.17
  246.2 5.2 %fold.18 = (bf16[8,32,2048]{2,1,0:T(8,128)(2,1)}, bf16[8,32,2048]{2,1,0:T(8,128)(2,1)}, bf16[8,32,2048]{2,1,0:T(8,128)(2,1)}, bf16[8,32,2048]{2,1,0:T(8,128)(2,1)}) custom-call(s32[5]{0:T(128)} %stack.35.bit_ref, bf16[16,32,2048]{2,1,0:T(8,128)(2,1)} %get-tuple-element.247.refs_0_, bf16[16,32,2048]{2,1,0:T(8,128)(2,1)} %copy-done.13, ...), custom_call_target="tpu_custom_call" | custom-call | bytes 160 | tf_op jit(solution)/shard_map/fold/pallas_call | solution.py:617
  254.9 26.5 %attend_back.1 = (bf16[3,680,1024]{2,1,0:T(8,128)(2,1)}, f32[8,1024]{1,0:T(8,128)}) custom-call(bf16[680,3072]{1,0:T(8,128)(2,1)} %get-tuple-element.198.q_ref.k_ref.v_ref, bf16[680,3072]{1,0:T(8,128)(2,1)} %get-tuple-element.198.q_ref.k_ref.v_ref, bf16[680,3072]{1,0:T(8,128)(2,1)} %get-tuple-element.198.q_ref.k_ref.v_ref, ...), custom_call_target="tpu_custom_call" | custom-call | flops 189399040000 | bytes 417792000 | tf_op jit(solution)/shard_map/attend_back/pallas_call | solution.py:291
  283.5 3.4 fold.20
  290.0 12.8 %weight_grad.1 = (bf16[16,32,2048]{2,1,0:T(8,128)(2,1)}, bf16[16,32,2048]{2,1,0:T(8,128)(2,1)}, bf16[16,32,2048]{2,1,0:T(8,128)(2,1)}, bf16[16,32,2048]{2,1,0:T(8,128)(2,1)}) custom-call(s32[1]{0:T(128)} %bitcast.32.core_ref, bf16[680,1024]{1,0:T(8,128)(2,1)} %get-tuple-element.286.x_ref, bf16[3,680,1024]{2,1,0:T(8,128)(2,1)} %get-tuple-element.297.g_ref, ...), custom_call_target="tpu_custom_call" | custom-call | flops 114085068800 | bytes 334888960 | tf_op jit(solution)/shard_map/weight_grad/pallas_call | solution.py:433
  310.3 5.2 %fold.23 = (bf16[8,32,2048]{2,1,0:T(8,128)(2,1)}, bf16[8,32,2048]{2,1,0:T(8,128)(2,1)}, bf16[8,32,2048]{2,1,0:T(8,128)(2,1)}, bf16[8,32,2048]{2,1,0:T(8,128)(2,1)}) custom-call(s32[5]{0:T(128)} %stack.35.bit_ref, bf16[16,32,2048]{2,1,0:T(8,128)(2,1)} %get-tuple-element.291.refs_0_, bf16[16,32,2048]{2,1,0:T(8,128)(2,1)} %collective-permute-done.39.refs_1_, ...), custom_call_target="tpu_custom_call" | custom-call | bytes 160 | tf_op jit(solution)/shard_map/fold/pallas_call | solution.py:617
  317.5 12.8 %input_back.1 = (f32[680,1024]{1,0:T(8,128)}, f32[8,1024]{1,0:T(8,128)}) custom-call(bf16[680,1024]{1,0:T(8,128)(2,1)} %bitcast.64, f32[680,1024]{1,0:T(8,128)} %get-tuple-element.235.resid_ref, f32[6,1024]{1,0:T(8,128)} %reshape.113.mod_ref, bf16[3,680,1024]{2,1,0:T(8,128)(2,1)} %get-tuple-element.297.g_ref, bf16[1024,4096]{1,0:T(8,128)(2,1)} %get-tuple-element.200.w_ref), custom_call_target="tpu_custom_call" | custom-call | flops 85563801600 | bytes 348651520 | tf_op jit(solution)/shard_map/input_back/pallas_call | solution.py:483
  335.3 3.5 all-to-all-start.1
  343.4 3.3 fold.25
  350.8 12.1 %collective-permute-done.44.refs_1_ = bf16[1,32,4096]{2,1,0:T(8,128)(2,1)S(1)} collective-permute-done((bf16[1,32,4096]{2,1,0:T(8,128)(2,1)S(1)}, bf16[1,32,4096]{2,1,0:T(8,128)(2,1)S(1)}, u32[]{:S(2)}, u32[]{:S(2)}) %collective-permute-start.44) | collective-permute-done | bytes 262176 | tf_op jit(solution)/shard_map/ppermute | solution.py:630
  365.5 2.7 fold.27
  373.3 2.7 reshape.121
  377.4 4.2 %collective-permute-done.47.refs_1_ = bf16[2,32,4096]{2,1,0:T(8,128)(2,1)} collective-permute-done((bf16[2,32,4096]{2,1,0:T(8,128)(2,1)}, bf16[2,32,4096]{2,1,0:T(8,128)(2,1)}, u32[]{:S(2)}, u32[]{:S(2)}) %collective-permute-start.47) | collective-permute-done | bytes 524320 | tf_op jit(solution)/shard_map/ppermute | solution.py:630
  383.8 2.8 collective-permute-start.48
  390.7 7.8 %collective-permute-done.48.refs_1_ = bf16[1,32,4096]{2,1,0:T(8,128)(2,1)S(1)} collective-permute-done((bf16[1,32,4096]{2,1,0:T(8,128)(2,1)}, bf16[1,32,4096]{2,1,0:T(8,128)(2,1)S(1)}, u32[]{:S(2)}, u32[]{:S(2)}) %collective-permute-start.48) | collective-permute-done | bytes 262176 | tf_op jit(solution)/shard_map/ppermute | solution.py:630
  (302 shorter events, 116.5 us)
Async XLA Ops:
  9.3 15.6 %all-to-all-start = ((bf16[32,1,130]{2,1,0:T(2,128)(2,1)}), bf16[32,1,130]{2,1,0:T(2,128)(2,1)S(1)}, u32[]{:S(2)}, u32[]{:S(2)}) async-start(bf16[32,1,130]{2,1,0:T(2,128)(2,1)} %broadcast_in_dim.17), calls=%async_computation | async-start | bytes 65536 | tf_op jit(solution)/shard_map/all_to_all | solution.py:854
  16.6 177.9 %all-gather.2.cloned.1.call-start = ((), (), s32[]{:S(2)}) async-start(), calls=%async_computation.2 | async-start | bytes 8650752 | tf_op jit(solution)/shard_map/all_gather | solution.py:913
  17.6 15.3 %collective-permute-start.1 = (bf16[1,32,4096]{2,1,0:T(8,128)(2,1)S(1)}, bf16[1,32,4096]{2,1,0:T(8,128)(2,1)S(1)}, u32[]{:S(2)}, u32[]{:S(2)}) collective-permute-start(bf16[1,32,4096]{2,1,0:T(8,128)(2,1)S(1)} %maximum_bitcast_fusion.2), channel_id=1, source_target_pairs={{0,16},{1,17},{2,18},{3,19},{4,20},{5,21},{6,22},{7,23},{8,24},{9,... | collective-permute-start | bytes 786440 | tf_op jit(solution)/shard_map/ppermute | solution.py:630
  49.3 15.3 %collective-permute-start.5 = (bf16[4,32,2048]{2,1,0:T(8,128)(2,1)S(1)}, bf16[4,32,2048]{2,1,0:T(8,128)(2,1)S(1)}, u32[]{:S(2)}, u32[]{:S(2)}) collective-permute-start(bf16[4,32,2048]{2,1,0:T(8,128)(2,1)S(1)} %get-tuple-element.380), channel_id=1, source_target_pairs={{0,4},{1,5},{2,6},{3,7},{4,0},{5,1},{6,2},{7,3},{8,12},{9,13},{10,... | collective-permute-start | bytes 1572872 | tf_op jit(solution)/shard_map/ppermute | solution.py:630
  50.8 13.8 %collective-permute-start.6 = (bf16[4,32,2048]{2,1,0:T(8,128)(2,1)S(1)}, bf16[4,32,2048]{2,1,0:T(8,128)(2,1)S(1)}, u32[]{:S(2)}, u32[]{:S(2)}) collective-permute-start(bf16[4,32,2048]{2,1,0:T(8,128)(2,1)S(1)} %get-tuple-element.379), channel_id=1, source_target_pairs={{0,2},{1,3},{2,0},{3,1},{4,6},{5,7},{6,4},{7,5},{8,10},{9,11},{10,... | collective-permute-start | bytes 1572872 | tf_op jit(solution)/shard_map/ppermute | solution.py:630
  65.9 24.6 %collective-permute-start.10 = (bf16[8,32,2048]{2,1,0:T(8,128)(2,1)S(1)}, bf16[8,32,2048]{2,1,0:T(8,128)(2,1)}, u32[]{:S(2)}, u32[]{:S(2)}) collective-permute-start(bf16[8,32,2048]{2,1,0:T(8,128)(2,1)S(1)} %pad_maximum_fusion.1.refs_0_), channel_id=1, source_target_pairs={{0,2},{1,3},{2,0},{3,1},{4,6},{5,7},{6,4},{7,5},{8,10},{9,11},{10,... | collective-permute-start | bytes 3145736 | tf_op jit(solution)/shard_map/ppermute | solution.py:630
  68.6 24.5 %collective-permute-start.11 = (bf16[8,32,2048]{2,1,0:T(8,128)(2,1)}, bf16[8,32,2048]{2,1,0:T(8,128)(2,1)}, u32[]{:S(2)}, u32[]{:S(2)}) collective-permute-start(bf16[8,32,2048]{2,1,0:T(8,128)(2,1)} %pad_maximum_fusion.2.refs_4_), channel_id=1, source_target_pairs={{0,4},{1,5},{2,6},{3,7},{4,0},{5,1},{6,2},{7,3},{8,12},{9,13},{10,... | collective-permute-start | bytes 3145736 | tf_op jit(solution)/shard_map/ppermute | solution.py:630
  75.1 19.2 %collective-permute-start.13 = (bf16[8,32,2048]{2,1,0:T(8,128)(2,1)S(1)}, bf16[8,32,2048]{2,1,0:T(8,128)(2,1)}, u32[]{:S(2)}, u32[]{:S(2)}) collective-permute-start(bf16[8,32,2048]{2,1,0:T(8,128)(2,1)S(1)} %pad_maximum_fusion.1.refs_0_), channel_id=1, source_target_pairs={{0,1},{1,0},{2,3},{3,2},{4,5},{5,4},{6,7},{7,6},{8,9},{9,8},{10,11... | collective-permute-start | bytes 3145736 | tf_op jit(solution)/shard_map/ppermute | solution.py:630
  93.7 22.2 %collective-permute-start.17 = (bf16[4,32,2048]{2,1,0:T(8,128)(2,1)S(1)}, bf16[4,32,2048]{2,1,0:T(8,128)(2,1)S(1)}, u32[]{:S(2)}, u32[]{:S(2)}) collective-permute-start(bf16[4,32,2048]{2,1,0:T(8,128)(2,1)S(1)} %get-tuple-element.378), channel_id=1, source_target_pairs={{0,4},{1,5},{2,6},{3,7},{4,0},{5,1},{6,2},{7,3},{8,12},{9,13},{10,... | collective-permute-start | bytes 1572872 | tf_op jit(solution)/shard_map/ppermute | solution.py:630
  94.3 21.6 %collective-permute-start.18 = (bf16[4,32,2048]{2,1,0:T(8,128)(2,1)S(1)}, bf16[4,32,2048]{2,1,0:T(8,128)(2,1)S(1)}, u32[]{:S(2)}, u32[]{:S(2)}) collective-permute-start(bf16[4,32,2048]{2,1,0:T(8,128)(2,1)S(1)} %get-tuple-element.377), channel_id=1, source_target_pairs={{0,2},{1,3},{2,0},{3,1},{4,6},{5,7},{6,4},{7,5},{8,10},{9,11},{10,... | collective-permute-start | bytes 1572872 | tf_op jit(solution)/shard_map/ppermute | solution.py:630
  116.2 29.5 %collective-permute-start.19 = (bf16[8,32,2048]{2,1,0:T(8,128)(2,1)S(1)}, bf16[8,32,2048]{2,1,0:T(8,128)(2,1)}, u32[]{:S(2)}, u32[]{:S(2)}) collective-permute-start(bf16[8,32,2048]{2,1,0:T(8,128)(2,1)S(1)} %pad_maximum_fusion.3.refs_0_), channel_id=1, source_target_pairs={{0,2},{1,3},{2,0},{3,1},{4,6},{5,7},{6,4},{7,5},{8,10},{9,11},{10,... | collective-permute-start | bytes 3145736 | tf_op jit(solution)/shard_map/ppermute | solution.py:630
  116.8 28.8 %collective-permute-start.20 = (bf16[8,32,2048]{2,1,0:T(8,128)(2,1)S(1)}, bf16[8,32,2048]{2,1,0:T(8,128)(2,1)}, u32[]{:S(2)}, u32[]{:S(2)}) collective-permute-start(bf16[8,32,2048]{2,1,0:T(8,128)(2,1)S(1)} %pad_maximum_fusion.4.refs_4_), channel_id=1, source_target_pairs={{0,4},{1,5},{2,6},{3,7},{4,0},{5,1},{6,2},{7,3},{8,12},{9,13},{10,... | collective-permute-start | bytes 3145736 | tf_op jit(solution)/shard_map/ppermute | solution.py:630
  119.2 28.5 %collective-permute-start.21 = (bf16[8,32,2048]{2,1,0:T(8,128)(2,1)S(1)}, bf16[8,32,2048]{2,1,0:T(8,128)(2,1)}, u32[]{:S(2)}, u32[]{:S(2)}) collective-permute-start(bf16[8,32,2048]{2,1,0:T(8,128)(2,1)S(1)} %pad_maximum_fusion.3.refs_0_), channel_id=1, source_target_pairs={{0,1},{1,0},{2,3},{3,2},{4,5},{5,4},{6,7},{7,6},{8,9},{9,8},{10,11... | collective-permute-start | bytes 3145736 | tf_op jit(solution)/shard_map/ppermute | solution.py:630
  119.3 28.4 %collective-permute-start.23 = (bf16[8,32,2048]{2,1,0:T(8,128)(2,1)S(1)}, bf16[8,32,2048]{2,1,0:T(8,128)(2,1)}, u32[]{:S(2)}, u32[]{:S(2)}) collective-permute-start(bf16[8,32,2048]{2,1,0:T(8,128)(2,1)S(1)} %pad_maximum_fusion.4.refs_4_), channel_id=1, source_target_pairs={{0,1},{1,0},{2,3},{3,2},{4,5},{5,4},{6,7},{7,6},{8,9},{9,8},{10,11... | collective-permute-start | bytes 3145736 | tf_op jit(solution)/shard_map/ppermute | solution.py:630
  191.0 31.7 %collective-permute-start.27 = (bf16[8,32,2048]{2,1,0:T(8,128)(2,1)}, bf16[8,32,2048]{2,1,0:T(8,128)(2,1)}, u32[]{:S(2)}, u32[]{:S(2)}) collective-permute-start(bf16[8,32,2048]{2,1,0:T(8,128)(2,1)} %get-tuple-element.223), channel_id=1, source_target_pairs={{0,2},{1,3},{2,0},{3,1},{4,6},{5,7},{6,4},{7,5},{8,10},{9,11},{10,... | collective-permute-start | bytes 3145736 | tf_op jit(solution)/shard_map/ppermute | solution.py:630
  192.4 30.3 %collective-permute-start.28 = (bf16[8,32,2048]{2,1,0:T(8,128)(2,1)}, bf16[8,32,2048]{2,1,0:T(8,128)(2,1)}, u32[]{:S(2)}, u32[]{:S(2)}) collective-permute-start(bf16[8,32,2048]{2,1,0:T(8,128)(2,1)} %get-tuple-element.224), channel_id=1, source_target_pairs={{0,4},{1,5},{2,6},{3,7},{4,0},{5,1},{6,2},{7,3},{8,12},{9,13},{10,... | collective-permute-start | bytes 3145736 | tf_op jit(solution)/shard_map/ppermute | solution.py:630
  226.3 14.4 %collective-permute-start.29 = (bf16[4,32,2048]{2,1,0:T(8,128)(2,1)}, bf16[4,32,2048]{2,1,0:T(8,128)(2,1)S(1)}, u32[]{:S(2)}, u32[]{:S(2)}) collective-permute-start(bf16[4,32,2048]{2,1,0:T(8,128)(2,1)} %get-tuple-element.237), channel_id=1, source_target_pairs={{0,4},{1,5},{2,6},{3,7},{4,0},{5,1},{6,2},{7,3},{8,12},{9,13},{10,... | collective-permute-start | bytes 1572872 | tf_op jit(solution)/shard_map/ppermute | solution.py:630
  227.8 14.0 %collective-permute-start.30 = (bf16[4,32,2048]{2,1,0:T(8,128)(2,1)}, bf16[4,32,2048]{2,1,0:T(8,128)(2,1)S(1)}, u32[]{:S(2)}, u32[]{:S(2)}) collective-permute-start(bf16[4,32,2048]{2,1,0:T(8,128)(2,1)} %get-tuple-element.238), channel_id=1, source_target_pairs={{0,2},{1,3},{2,0},{3,1},{4,6},{5,7},{6,4},{7,5},{8,10},{9,11},{10,... | collective-permute-start | bytes 1572872 | tf_op jit(solution)/shard_map/ppermute | solution.py:630
  251.4 30.0 %collective-permute-start.33 = (bf16[2,32,4096]{2,1,0:T(8,128)(2,1)}, bf16[2,32,4096]{2,1,0:T(8,128)(2,1)}, u32[]{:S(2)}, u32[]{:S(2)}) collective-permute-start(bf16[2,32,4096]{2,1,0:T(8,128)(2,1)} %get-tuple-element.258), channel_id=1, source_target_pairs={{0,8},{1,9},{2,10},{3,11},{4,12},{5,13},{6,14},{7,15},{8,0},{9,1},... | collective-permute-start | bytes 1572872 | tf_op jit(solution)/shard_map/ppermute | solution.py:630
  252.9 28.5 %collective-permute-start.34 = (bf16[8,32,2048]{2,1,0:T(8,128)(2,1)}, bf16[8,32,2048]{2,1,0:T(8,128)(2,1)}, u32[]{:S(2)}, u32[]{:S(2)}) collective-permute-start(bf16[8,32,2048]{2,1,0:T(8,128)(2,1)} %get-tuple-element.259), channel_id=1, source_target_pairs={{0,2},{1,3},{2,0},{3,1},{4,6},{5,7},{6,4},{7,5},{8,10},{9,11},{10,... | collective-permute-start | bytes 3145736 | tf_op jit(solution)/shard_map/ppermute | solution.py:630
  253.5 28.0 %collective-permute-start.35 = (bf16[8,32,2048]{2,1,0:T(8,128)(2,1)}, bf16[8,32,2048]{2,1,0:T(8,128)(2,1)}, u32[]{:S(2)}, u32[]{:S(2)}) collective-permute-start(bf16[8,32,2048]{2,1,0:T(8,128)(2,1)} %get-tuple-element.260), channel_id=1, source_target_pairs={{0,4},{1,5},{2,6},{3,7},{4,0},{5,1},{6,2},{7,3},{8,12},{9,13},{10,... | collective-permute-start | bytes 3145736 | tf_op jit(solution)/shard_map/ppermute | solution.py:630
  286.9 16.4 %collective-permute-start.36 = (bf16[1,32,4096]{2,1,0:T(8,128)(2,1)S(1)}, bf16[1,32,4096]{2,1,0:T(8,128)(2,1)S(1)}, u32[]{:S(2)}, u32[]{:S(2)}) collective-permute-start(bf16[1,32,4096]{2,1,0:T(8,128)(2,1)S(1)} %copy-done.50), channel_id=1, source_target_pairs={{0,16},{1,17},{2,18},{3,19},{4,20},{5,21},{6,22},{7,23},{8,24},{9,... | collective-permute-start | bytes 786440 | tf_op jit(solution)/shard_map/ppermute | solution.py:630
  287.9 15.4 %collective-permute-start.37 = (bf16[4,32,2048]{2,1,0:T(8,128)(2,1)}, bf16[4,32,2048]{2,1,0:T(8,128)(2,1)S(1)}, u32[]{:S(2)}, u32[]{:S(2)}) collective-permute-start(bf16[4,32,2048]{2,1,0:T(8,128)(2,1)} %get-tuple-element.273), channel_id=1, source_target_pairs={{0,4},{1,5},{2,6},{3,7},{4,0},{5,1},{6,2},{7,3},{8,12},{9,13},{10,... | collective-permute-start | bytes 1572872 | tf_op jit(solution)/shard_map/ppermute | solution.py:630
  288.5 14.8 %collective-permute-start.38 = (bf16[4,32,2048]{2,1,0:T(8,128)(2,1)}, bf16[4,32,2048]{2,1,0:T(8,128)(2,1)S(1)}, u32[]{:S(2)}, u32[]{:S(2)}) collective-permute-start(bf16[4,32,2048]{2,1,0:T(8,128)(2,1)} %get-tuple-element.274), channel_id=1, source_target_pairs={{0,2},{1,3},{2,0},{3,1},{4,6},{5,7},{6,4},{7,5},{8,10},{9,11},{10,... | collective-permute-start | bytes 1572872 | tf_op jit(solution)/shard_map/ppermute | solution.py:630
  308.6 30.1 %collective-permute-start.41 = (bf16[2,32,4096]{2,1,0:T(8,128)(2,1)}, bf16[2,32,4096]{2,1,0:T(8,128)(2,1)S(1)}, u32[]{:S(2)}, u32[]{:S(2)}) collective-permute-start(bf16[2,32,4096]{2,1,0:T(8,128)(2,1)} %get-tuple-element.309), channel_id=1, source_target_pairs={{0,8},{1,9},{2,10},{3,11},{4,12},{5,13},{6,14},{7,15},{8,0},{9,1},... | collective-permute-start | bytes 1572872 | tf_op jit(solution)/shard_map/ppermute | solution.py:630
  315.5 25.4 %collective-permute-start.42 = (bf16[8,32,2048]{2,1,0:T(8,128)(2,1)}, bf16[8,32,2048]{2,1,0:T(8,128)(2,1)S(1)}, u32[]{:S(2)}, u32[]{:S(2)}) collective-permute-start(bf16[8,32,2048]{2,1,0:T(8,128)(2,1)} %get-tuple-element.310), channel_id=1, source_target_pairs={{0,2},{1,3},{2,0},{3,1},{4,6},{5,7},{6,4},{7,5},{8,10},{9,11},{10,... | collective-permute-start | bytes 3145736 | tf_op jit(solution)/shard_map/ppermute | solution.py:630
  316.1 25.2 %collective-permute-start.43 = (bf16[8,32,2048]{2,1,0:T(8,128)(2,1)}, bf16[8,32,2048]{2,1,0:T(8,128)(2,1)}, u32[]{:S(2)}, u32[]{:S(2)}) collective-permute-start(bf16[8,32,2048]{2,1,0:T(8,128)(2,1)} %get-tuple-element.311), channel_id=1, source_target_pairs={{0,4},{1,5},{2,6},{3,7},{4,0},{5,1},{6,2},{7,3},{8,12},{9,13},{10,... | collective-permute-start | bytes 3145736 | tf_op jit(solution)/shard_map/ppermute | solution.py:630
  335.3 33.8 %all-to-all-start.1 = ((bf16[32,2,3216]{2,1,0:T(2,128)(2,1)}), bf16[32,2,3216]{2,1,0:T(2,128)(2,1)S(1)}, u32[]{:S(2)}, u32[]{:S(2)}) async-start(bf16[32,2,3216]{2,1,0:T(2,128)(2,1)} %reshape.185), calls=%async_computation.1 | async-start | bytes 851968 | tf_op jit(solution)/shard_map/all_to_all | solution.py:987
  346.7 16.2 %collective-permute-start.45 = (bf16[4,32,2048]{2,1,0:T(8,128)(2,1)}, bf16[4,32,2048]{2,1,0:T(8,128)(2,1)S(1)}, u32[]{:S(2)}, u32[]{:S(2)}) collective-permute-start(bf16[4,32,2048]{2,1,0:T(8,128)(2,1)} %get-tuple-element.324), channel_id=1, source_target_pairs={{0,4},{1,5},{2,6},{3,7},{4,0},{5,1},{6,2},{7,3},{8,12},{9,13},{10,... | collective-permute-start | bytes 1572872 | tf_op jit(solution)/shard_map/ppermute | solution.py:630
  348.5 14.4 %collective-permute-start.46 = (bf16[4,32,2048]{2,1,0:T(8,128)(2,1)}, bf16[4,32,2048]{2,1,0:T(8,128)(2,1)S(1)}, u32[]{:S(2)}, u32[]{:S(2)}) collective-permute-start(bf16[4,32,2048]{2,1,0:T(8,128)(2,1)} %get-tuple-element.325), channel_id=1, source_target_pairs={{0,2},{1,3},{2,0},{3,1},{4,6},{5,7},{6,4},{7,5},{8,10},{9,11},{10,... | collective-permute-start | bytes 1572872 | tf_op jit(solution)/shard_map/ppermute | solution.py:630
  348.9 14.0 %collective-permute-start.44 = (bf16[1,32,4096]{2,1,0:T(8,128)(2,1)S(1)}, bf16[1,32,4096]{2,1,0:T(8,128)(2,1)S(1)}, u32[]{:S(2)}, u32[]{:S(2)}) collective-permute-start(bf16[1,32,4096]{2,1,0:T(8,128)(2,1)S(1)} %copy-done.52), channel_id=1, source_target_pairs={{0,16},{1,17},{2,18},{3,19},{4,20},{5,21},{6,22},{7,23},{8,24},{9,... | collective-permute-start | bytes 786440 | tf_op jit(solution)/shard_map/ppermute | solution.py:630
  383.8 14.6 %collective-permute-start.48 = (bf16[1,32,4096]{2,1,0:T(8,128)(2,1)}, bf16[1,32,4096]{2,1,0:T(8,128)(2,1)S(1)}, u32[]{:S(2)}, u32[]{:S(2)}) collective-permute-start(bf16[1,32,4096]{2,1,0:T(8,128)(2,1)} %get-tuple-element.346), channel_id=1, source_target_pairs={{0,16},{1,17},{2,18},{3,19},{4,20},{5,21},{6,22},{7,23},{8,24},{9,... | collective-permute-start | bytes 786440 | tf_op jit(solution)/shard_map/ppermute | solution.py:630
  (76 other events, 653.2 us)
Sparse Core Ops, SparseCore 0:
  116.3 78.1 all-gather.1

commit v5 on v4

--- a/solution.py
+++ b/solution.py
@@ -113,7 +113,7 @@
         spread = dot(high, seg, LAST) + dot(low, seg, LAST)
         gain = jnp.where(step == 0, gain_ref[...], 1.0)
         out_ref[...] = (raw * spread * gain).astype(BF)
-        inv_ref[...] = spread
+        inv_ref[...] = spread.astype(BF)
 
     @pl.when(step >= 2)
     def _():
@@ -155,7 +155,7 @@
         out_shape=[
             jax.ShapeDtypeStruct((tokens, width), BF),
             jax.ShapeDtypeStruct((tokens, 3 * width), BF),
-            jax.ShapeDtypeStruct((tokens, 2 * width), F32),
+            jax.ShapeDtypeStruct((tokens, 2 * width), BF),
             jax.ShapeDtypeStruct((width, 4 * width), BF),
         ],
         compiler_params=grant(58),
@@ -276,11 +276,11 @@
     along = dq * q
     first, second = head_sums(along)
     grad_ref[0] = (
-        rq_ref[...] * (dq * gain - q * (jnp.where(left, first, second) / gain))
+        rq_ref[...].astype(F32) * (dq * gain - q * (jnp.where(left, first, second) / gain))
     ).astype(BF)
     hs_ref[...] = jnp.broadcast_to(jnp.sum(along, axis=0, keepdims=True), hs_ref.shape)
     first, second = head_sums(dk * k)
-    grad_ref[1] = (rk_ref[...] * (dk - k * jnp.where(left, first, second))).astype(BF)
+    grad_ref[1] = (rk_ref[...].astype(F32) * (dk - k * jnp.where(left, first, second))).astype(BF)
     grad_ref[2] = acc_v[...].astype(BF)
 
 
@@ -581,7 +581,7 @@
         + [jax.ShapeDtypeStruct((1, total), F32)],
         scratch_shapes=[pltpu.VMEM((width, block), BF), pltpu.VMEM((width, width), BF)],
         input_output_aliases={4 + len(matrices) + i: i for i in range(len(carried))},
-        compiler_params=grant(58),
+        compiler_params=grant(58 if carried else 50),
         cost_estimate=cost(
             12 * tokens * width * total,
             (8 + 8 * len(carried)) * tokens * width + 8 * total * width,

time: 414 us -> 413 us (level)
    unnamed x119 -> x109, local copies, waits for them, and re-layouts: 14.5 us -> 14.5 us
  transfers between devices with their start and end apart: 52 -> 52, of which waited for: 24 -> 24; matrix products, arithmetic and copies ran while one was open for 8% -> 8% of each run, Pallas kernels for 44% -> 43%
where the time goes in v5:
time: 413 us; the launch traced here: 407 us
  Pallas kernels  198 us (48%)
  waiting for transfers between devices  86.1 us (21%)
  starting transfers between devices  58.4 us (14%)
  local copies, waits for them, and re-layouts  32.5 us (8%)
  between operations  17.2 us (4%)
  other arithmetic  12.2 us (3%)
    ppermute x49, waiting for transfers between devices, swap(): return lax.ppermute(block, AXES, [(i, i ^ mask) for i in range(count)])  83.6 us
    pallas_call x2, Pallas kernels, mlp(): pl.pallas_call(partial(mlp_body, first=not carried, sources=len(matrices)...  54.4 us
    ppermute x49, starting transfers between devices, swap(): return lax.ppermute(block, AXES, [(i, i ^ mask) for i in range(count)])  47.4 us
    pallas_call x15, Pallas kernels, fold(): pl.pallas_call(partial(fold_body, plan=plan, out_count=len(outs)), grid=(...  46.1 us
    pallas_call x1, Pallas kernels, attend_back(): pl.pallas_call(attend_back_body, grid=(some,), in_specs=[pair(0), pair(pa...  26.4 us
    pallas_call x1, Pallas kernels, qkv_rows(): pl.pallas_call(qkv_body, grid=(4,), in_specs=[pl.BlockSpec(memory_space=p...  17.1 us
    unnamed x109, local copies, waits for them, and re-layouts  14.5 us
    pallas_call x1, Pallas kernels, attend(): pl.pallas_call(attend_body, grid=(pairs,), in_specs=[pair(0), pair(pairs)...  14.2 us
  transfers between devices with their start and end apart: 52, of which 24 were waited for; matrix products, arithmetic and copies ran while one was open for 8% of the time, Pallas kernels for 43%

profile of v5, /device:TPU:0, one launch (start us, length us, event | category | flops | bytes accessed | tf_op | source)
XLA Modules:
  0.0 407.3 jit_solution(5382774993304551536)
XLA Ops:
  9.3 7.4 %all-to-all-start = ((bf16[32,1,130]{2,1,0:T(2,128)(2,1)}), bf16[32,1,130]{2,1,0:T(2,128)(2,1)}, u32[]{:S(2)}, u32[]{:S(2)}) async-start(bf16[32,1,130]{2,1,0:T(2,128)(2,1)} %broadcast_in_dim.17), calls=%async_computation | async-start | bytes 65536 | tf_op jit(solution)/shard_map/all_to_all | solution.py:854
  27.0 5.9 %collective-permute-done.1 = bf16[1,32,4096]{2,1,0:T(8,128)(2,1)S(1)} collective-permute-done((bf16[1,32,4096]{2,1,0:T(8,128)(2,1)S(1)}, bf16[1,32,4096]{2,1,0:T(8,128)(2,1)S(1)}, u32[]{:S(2)}, u32[]{:S(2)}) %collective-permute-start.1) | collective-permute-done | bytes 262176 | tf_op jit(solution)/shard_map/ppermute | solution.py:630
  36.3 10.1 %collective-permute-done.2 = bf16[2,32,4096]{2,1,0:T(8,128)(2,1)S(1)} collective-permute-done((bf16[2,32,4096]{2,1,0:T(8,128)(2,1)S(1)}, bf16[2,32,4096]{2,1,0:T(8,128)(2,1)S(1)}, u32[]{:S(2)}, u32[]{:S(2)}) %collective-permute-start.2) | collective-permute-done | bytes 524320 | tf_op jit(solution)/shard_map/ppermute | solution.py:630
  57.7 7.0 %collective-permute-done.7 = bf16[1,32,4096]{2,1,0:T(8,128)(2,1)S(1)} collective-permute-done((bf16[1,32,4096]{2,1,0:T(8,128)(2,1)S(1)}, bf16[1,32,4096]{2,1,0:T(8,128)(2,1)S(1)}, u32[]{:S(2)}, u32[]{:S(2)}) %collective-permute-start.7) | collective-permute-done | bytes 262176 | tf_op jit(solution)/shard_map/ppermute | solution.py:630
  71.5 3.5 collective-permute-start.9
  75.1 6.2 %collective-permute-done.9 = f32[1,6144]{1,0:T(1,128)S(1)} collective-permute-done((f32[1,6144]{1,0:T(1,128)S(1)}, f32[1,6144]{1,0:T(1,128)S(1)}, u32[]{:S(2)}, u32[]{:S(2)}) %collective-permute-start.9) | collective-permute-done | bytes 24608 | tf_op jit(solution)/shard_map/ppermute | solution.py:630
  83.3 7.2 %collective-permute-done.10.refs_2_ = bf16[8,32,2048]{2,1,0:T(8,128)(2,1)} collective-permute-done((bf16[8,32,2048]{2,1,0:T(8,128)(2,1)S(1)}, bf16[8,32,2048]{2,1,0:T(8,128)(2,1)}, u32[]{:S(2)}, u32[]{:S(2)}) %collective-permute-start.10) | collective-permute-done | bytes 1048608 | tf_op jit(solution)/shard_map/ppermute | solution.py:630
  97.5 17.1 %qkv.1 = (bf16[680,1024]{1,0:T(8,128)(2,1)}, bf16[680,3072]{1,0:T(8,128)(2,1)}, bf16[680,2048]{1,0:T(8,128)(2,1)}, bf16[1024,4096]{1,0:T(8,128)(2,1)}) custom-call(s32[2,16]{1,0:T(2,128)} %pad_add_fusion.code_ref, bf16[680,1024]{1,0:T(8,128)(2,1)} %bitcast.62, f32[6,1024]{1,0:T(8,128)} %reshape.113.mod_ref, f32[1,1024]{1,0:T(1,128)} %broadcast_in_dim_reshape.3.gain_ref, ...), custom_call_target="tpu_custom_call" | custom-call | flops 8556380160 | bytes 55836672 | tf_op jit(solution)/shard_map/qkv/pallas_call | solution.py:137
  121.7 14.2 %attend.1 = (bf16[680,1024]{1,0:T(8,128)(2,1)S(1)}, bf16[680,1024]{1,0:T(8,128)(2,1)S(1)}, f32[680,1024]{1,0:T(8,128)S(1)}) custom-call(bf16[680,3072]{1,0:T(8,128)(2,1)S(1)} %copy-done.1, bf16[680,3072]{1,0:T(8,128)(2,1)S(1)} %copy-done.1, bf16[680,3072]{1,0:T(8,128)(2,1)S(1)} %copy-done.1, s32[1,680]{1,0:T(1,128)S(1)} %copy-done.8), custom_call_target="tpu_custom_call" | custom-call | flops 75759616 | bytes 139264 | tf_op jit(solution)/shard_map/attend/pallas_call | solution.py:200
  138.6 2.8 project.1
  149.8 26.1 %mlp.2 = (f32[680,1024]{1,0:T(8,128)}, f32[680,1024]{1,0:T(8,128)}, bf16[16,32,2048]{2,1,0:T(8,128)(2,1)}, bf16[16,32,2048]{2,1,0:T(8,128)(2,1)}, bf16[16,32,204...) custom-call(s32[3,16]{1,0:T(4,128)S(1)} %add_add_fusion.info_ref, ...), custom_call_target="tpu_custom_call" | custom-call | flops 5133828096 | bytes 6704332 | tf_op jit(solution)/shard_map/mlp/pallas_call | solution.py:570
  177.6 2.8 collective-permute-done.25.refs_1_
  180.4 3.1 collective-permute-done.26.refs_3_
  183.5 5.2 %fold.15 = (bf16[8,32,2048]{2,1,0:T(8,128)(2,1)}, bf16[8,32,2048]{2,1,0:T(8,128)(2,1)}, bf16[8,32,2048]{2,1,0:T(8,128)(2,1)}, bf16[8,32,2048]{2,1,0:T(8,128)(2,1)}) custom-call(s32[5]{0:T(128)} %stack.35.bit_ref, bf16[16,32,2048]{2,1,0:T(8,128)(2,1)} %get-tuple-element.214.refs_0_, bf16[16,32,2048]{2,1,0:T(8,128)(2,1)} %collective-permute-done.25.refs_1_, ...), custom_call_target="tpu_custom_call" | custom-call | bytes 160 | tf_op jit(solution)/shard_map/fold/pallas_call | solution.py:617
  194.2 28.3 %mlp.3 = (f32[680,1024]{1,0:T(8,128)}, f32[680,1024]{1,0:T(8,128)}, bf16[16,32,2048]{2,1,0:T(8,128)(2,1)}, bf16[16,32,2048]{2,1,0:T(8,128)(2,1)}, bf16[16,32,204...) custom-call(s32[3,16]{1,0:T(4,128)} %concatenate.85.info_ref, ...), custom_call_target="tpu_custom_call", output_to_operand_aliasing={{0}: (8, {}), {1}: (9, {})} | custom-call | flops 342255206400 | bytes 669777920 | tf_op jit(solution)/shard_map/mlp/pallas_call | solution.py:570
  222.5 3.7 fold.16
  228.8 11.0 %residual_back.1 = (bf16[680,1024]{1,0:T(8,128)(2,1)}, f32[680,1024]{1,0:T(8,128)}, bf16[680,1024]{1,0:T(8,128)(2,1)}, bf16[680,1024]{1,0:T(8,128)(2,1)}, f32[8,1024]{1,0:T(8,128)}) custom-call(s32[1]{0:T(128)S(6)} %select_n.44.live_ref, bf16[680,1024]{1,0:T(8,128)(2,1)} %bitcast.63, f32[680,1024]{1,0:T(8,128)} %copy-done.10, ...), custom_call_target="tpu_custom_call" | custom-call | flops 28521267200 | bytes 473825280 | tf_op jit(solution)/shard_map/residual_back/pallas_call | solution.py:388
  242.6 2.8 fold.17
  245.4 5.2 %fold.18 = (bf16[8,32,2048]{2,1,0:T(8,128)(2,1)}, bf16[8,32,2048]{2,1,0:T(8,128)(2,1)}, bf16[8,32,2048]{2,1,0:T(8,128)(2,1)}, bf16[8,32,2048]{2,1,0:T(8,128)(2,1)}) custom-call(s32[5]{0:T(128)} %stack.35.bit_ref, bf16[16,32,2048]{2,1,0:T(8,128)(2,1)} %get-tuple-element.247.refs_0_, bf16[16,32,2048]{2,1,0:T(8,128)(2,1)} %copy-done.14, ...), custom_call_target="tpu_custom_call" | custom-call | bytes 160 | tf_op jit(solution)/shard_map/fold/pallas_call | solution.py:617
  254.1 26.4 %attend_back.1 = (bf16[3,680,1024]{2,1,0:T(8,128)(2,1)}, f32[8,1024]{1,0:T(8,128)}) custom-call(bf16[680,3072]{1,0:T(8,128)(2,1)} %get-tuple-element.198.q_ref.k_ref.v_ref, bf16[680,3072]{1,0:T(8,128)(2,1)} %get-tuple-element.198.q_ref.k_ref.v_ref, bf16[680,3072]{1,0:T(8,128)(2,1)} %get-tuple-element.198.q_ref.k_ref.v_ref, ...), custom_call_target="tpu_custom_call" | custom-call | flops 189399040000 | bytes 417792000 | tf_op jit(solution)/shard_map/attend_back/pallas_call | solution.py:291
  282.6 3.4 fold.20
  289.1 12.8 %weight_grad.1 = (bf16[16,32,2048]{2,1,0:T(8,128)(2,1)}, bf16[16,32,2048]{2,1,0:T(8,128)(2,1)}, bf16[16,32,2048]{2,1,0:T(8,128)(2,1)}, bf16[16,32,2048]{2,1,0:T(8,128)(2,1)}) custom-call(s32[1]{0:T(128)} %bitcast.32.core_ref, bf16[680,1024]{1,0:T(8,128)(2,1)} %get-tuple-element.286.x_ref, bf16[3,680,1024]{2,1,0:T(8,128)(2,1)} %get-tuple-element.297.g_ref, ...), custom_call_target="tpu_custom_call" | custom-call | flops 114085068800 | bytes 334888960 | tf_op jit(solution)/shard_map/weight_grad/pallas_call | solution.py:433
  305.0 2.7 fold.22
  309.4 5.2 %fold.23 = (bf16[8,32,2048]{2,1,0:T(8,128)(2,1)}, bf16[8,32,2048]{2,1,0:T(8,128)(2,1)}, bf16[8,32,2048]{2,1,0:T(8,128)(2,1)}, bf16[8,32,2048]{2,1,0:T(8,128)(2,1)}) custom-call(s32[5]{0:T(128)} %stack.35.bit_ref, bf16[16,32,2048]{2,1,0:T(8,128)(2,1)} %get-tuple-element.291.refs_0_, bf16[16,32,2048]{2,1,0:T(8,128)(2,1)} %collective-permute-done.39.refs_1_, ...), custom_call_target="tpu_custom_call" | custom-call | bytes 160 | tf_op jit(solution)/shard_map/fold/pallas_call | solution.py:617
  316.6 12.8 %input_back.1 = (f32[680,1024]{1,0:T(8,128)}, f32[8,1024]{1,0:T(8,128)}) custom-call(bf16[680,1024]{1,0:T(8,128)(2,1)} %bitcast.64, f32[680,1024]{1,0:T(8,128)} %get-tuple-element.235.resid_ref, f32[6,1024]{1,0:T(8,128)} %reshape.113.mod_ref, bf16[3,680,1024]{2,1,0:T(8,128)(2,1)} %get-tuple-element.297.g_ref, bf16[1024,4096]{1,0:T(8,128)(2,1)} %get-tuple-element.200.w_ref), custom_call_target="tpu_custom_call" | custom-call | flops 85563801600 | bytes 348651520 | tf_op jit(solution)/shard_map/input_back/pallas_call | solution.py:483
  334.3 3.5 all-to-all-start.1
  342.4 3.4 fold.25
  349.9 12.0 %collective-permute-done.44.refs_1_ = bf16[1,32,4096]{2,1,0:T(8,128)(2,1)S(1)} collective-permute-done((bf16[1,32,4096]{2,1,0:T(8,128)(2,1)S(1)}, bf16[1,32,4096]{2,1,0:T(8,128)(2,1)S(1)}, u32[]{:S(2)}, u32[]{:S(2)}) %collective-permute-start.44) | collective-permute-done | bytes 262176 | tf_op jit(solution)/shard_map/ppermute | solution.py:630
  364.6 2.8 fold.27
  376.5 4.1 %collective-permute-done.47.refs_1_ = bf16[2,32,4096]{2,1,0:T(8,128)(2,1)} collective-permute-done((bf16[2,32,4096]{2,1,0:T(8,128)(2,1)}, bf16[2,32,4096]{2,1,0:T(8,128)(2,1)}, u32[]{:S(2)}, u32[]{:S(2)}) %collective-permute-start.47) | collective-permute-done | bytes 524320 | tf_op jit(solution)/shard_map/ppermute | solution.py:630
  383.0 2.9 collective-permute-start.48
  389.9 7.8 %collective-permute-done.48.refs_1_ = bf16[1,32,4096]{2,1,0:T(8,128)(2,1)S(1)} collective-permute-done((bf16[1,32,4096]{2,1,0:T(8,128)(2,1)}, bf16[1,32,4096]{2,1,0:T(8,128)(2,1)S(1)}, u32[]{:S(2)}, u32[]{:S(2)}) %collective-permute-start.48) | collective-permute-done | bytes 262176 | tf_op jit(solution)/shard_map/ppermute | solution.py:630
  (292 shorter events, 120.7 us)
Async XLA Ops:
  9.3 15.7 %all-to-all-start = ((bf16[32,1,130]{2,1,0:T(2,128)(2,1)}), bf16[32,1,130]{2,1,0:T(2,128)(2,1)}, u32[]{:S(2)}, u32[]{:S(2)}) async-start(bf16[32,1,130]{2,1,0:T(2,128)(2,1)} %broadcast_in_dim.17), calls=%async_computation | async-start | bytes 65536 | tf_op jit(solution)/shard_map/all_to_all | solution.py:854
  16.7 177.5 %all-gather.2.cloned.1.call-start = ((), (), s32[]{:S(2)}) async-start(), calls=%async_computation.2 | async-start | bytes 8650752 | tf_op jit(solution)/shard_map/all_gather | solution.py:913
  17.8 15.2 %collective-permute-start.1 = (bf16[1,32,4096]{2,1,0:T(8,128)(2,1)S(1)}, bf16[1,32,4096]{2,1,0:T(8,128)(2,1)S(1)}, u32[]{:S(2)}, u32[]{:S(2)}) collective-permute-start(bf16[1,32,4096]{2,1,0:T(8,128)(2,1)S(1)} %maximum_bitcast_fusion.2), channel_id=1, source_target_pairs={{0,16},{1,17},{2,18},{3,19},{4,20},{5,21},{6,22},{7,23},{8,24},{9,... | collective-permute-start | bytes 786440 | tf_op jit(solution)/shard_map/ppermute | solution.py:630
  49.4 15.3 %collective-permute-start.5 = (bf16[4,32,2048]{2,1,0:T(8,128)(2,1)S(1)}, bf16[4,32,2048]{2,1,0:T(8,128)(2,1)S(1)}, u32[]{:S(2)}, u32[]{:S(2)}) collective-permute-start(bf16[4,32,2048]{2,1,0:T(8,128)(2,1)S(1)} %get-tuple-element.380), channel_id=1, source_target_pairs={{0,4},{1,5},{2,6},{3,7},{4,0},{5,1},{6,2},{7,3},{8,12},{9,13},{10,... | collective-permute-start | bytes 1572872 | tf_op jit(solution)/shard_map/ppermute | solution.py:630
  50.9 13.8 %collective-permute-start.6 = (bf16[4,32,2048]{2,1,0:T(8,128)(2,1)S(1)}, bf16[4,32,2048]{2,1,0:T(8,128)(2,1)S(1)}, u32[]{:S(2)}, u32[]{:S(2)}) collective-permute-start(bf16[4,32,2048]{2,1,0:T(8,128)(2,1)S(1)} %get-tuple-element.379), channel_id=1, source_target_pairs={{0,2},{1,3},{2,0},{3,1},{4,6},{5,7},{6,4},{7,5},{8,10},{9,11},{10,... | collective-permute-start | bytes 1572872 | tf_op jit(solution)/shard_map/ppermute | solution.py:630
  66.0 24.6 %collective-permute-start.10 = (bf16[8,32,2048]{2,1,0:T(8,128)(2,1)S(1)}, bf16[8,32,2048]{2,1,0:T(8,128)(2,1)}, u32[]{:S(2)}, u32[]{:S(2)}) collective-permute-start(bf16[8,32,2048]{2,1,0:T(8,128)(2,1)S(1)} %pad_maximum_fusion.1.refs_0_), channel_id=1, source_target_pairs={{0,2},{1,3},{2,0},{3,1},{4,6},{5,7},{6,4},{7,5},{8,10},{9,11},{10,... | collective-permute-start | bytes 3145736 | tf_op jit(solution)/shard_map/ppermute | solution.py:630
  68.6 24.5 %collective-permute-start.11 = (bf16[8,32,2048]{2,1,0:T(8,128)(2,1)}, bf16[8,32,2048]{2,1,0:T(8,128)(2,1)}, u32[]{:S(2)}, u32[]{:S(2)}) collective-permute-start(bf16[8,32,2048]{2,1,0:T(8,128)(2,1)} %pad_maximum_fusion.2.refs_4_), channel_id=1, source_target_pairs={{0,4},{1,5},{2,6},{3,7},{4,0},{5,1},{6,2},{7,3},{8,12},{9,13},{10,... | collective-permute-start | bytes 3145736 | tf_op jit(solution)/shard_map/ppermute | solution.py:630
  75.1 19.2 %collective-permute-start.13 = (bf16[8,32,2048]{2,1,0:T(8,128)(2,1)S(1)}, bf16[8,32,2048]{2,1,0:T(8,128)(2,1)}, u32[]{:S(2)}, u32[]{:S(2)}) collective-permute-start(bf16[8,32,2048]{2,1,0:T(8,128)(2,1)S(1)} %pad_maximum_fusion.1.refs_0_), channel_id=1, source_target_pairs={{0,1},{1,0},{2,3},{3,2},{4,5},{5,4},{6,7},{7,6},{8,9},{9,8},{10,11... | collective-permute-start | bytes 3145736 | tf_op jit(solution)/shard_map/ppermute | solution.py:630
  93.7 20.9 %collective-permute-start.17 = (bf16[4,32,2048]{2,1,0:T(8,128)(2,1)S(1)}, bf16[4,32,2048]{2,1,0:T(8,128)(2,1)S(1)}, u32[]{:S(2)}, u32[]{:S(2)}) collective-permute-start(bf16[4,32,2048]{2,1,0:T(8,128)(2,1)S(1)} %get-tuple-element.378), channel_id=1, source_target_pairs={{0,4},{1,5},{2,6},{3,7},{4,0},{5,1},{6,2},{7,3},{8,12},{9,13},{10,... | collective-permute-start | bytes 1572872 | tf_op jit(solution)/shard_map/ppermute | solution.py:630
  94.3 20.3 %collective-permute-start.18 = (bf16[4,32,2048]{2,1,0:T(8,128)(2,1)S(1)}, bf16[4,32,2048]{2,1,0:T(8,128)(2,1)S(1)}, u32[]{:S(2)}, u32[]{:S(2)}) collective-permute-start(bf16[4,32,2048]{2,1,0:T(8,128)(2,1)S(1)} %get-tuple-element.377), channel_id=1, source_target_pairs={{0,2},{1,3},{2,0},{3,1},{4,6},{5,7},{6,4},{7,5},{8,10},{9,11},{10,... | collective-permute-start | bytes 1572872 | tf_op jit(solution)/shard_map/ppermute | solution.py:630
  115.9 29.4 %collective-permute-start.19 = (bf16[8,32,2048]{2,1,0:T(8,128)(2,1)S(1)}, bf16[8,32,2048]{2,1,0:T(8,128)(2,1)S(1)}, u32[]{:S(2)}, u32[]{:S(2)}) collective-permute-start(bf16[8,32,2048]{2,1,0:T(8,128)(2,1)S(1)} %pad_maximum_fusion.3.refs_0_), channel_id=1, source_target_pairs={{0,2},{1,3},{2,0},{3,1},{4,6},{5,7},{6,4},{7,5},{8,10},{9,11},{10,... | collective-permute-start | bytes 3145736 | tf_op jit(solution)/shard_map/ppermute | solution.py:630
  116.5 28.8 %collective-permute-start.20 = (bf16[8,32,2048]{2,1,0:T(8,128)(2,1)}, bf16[8,32,2048]{2,1,0:T(8,128)(2,1)}, u32[]{:S(2)}, u32[]{:S(2)}) collective-permute-start(bf16[8,32,2048]{2,1,0:T(8,128)(2,1)} %pad_maximum_fusion.4.refs_4_), channel_id=1, source_target_pairs={{0,4},{1,5},{2,6},{3,7},{4,0},{5,1},{6,2},{7,3},{8,12},{9,13},{10,... | collective-permute-start | bytes 3145736 | tf_op jit(solution)/shard_map/ppermute | solution.py:630
  119.0 27.3 %collective-permute-start.21 = (bf16[8,32,2048]{2,1,0:T(8,128)(2,1)S(1)}, bf16[8,32,2048]{2,1,0:T(8,128)(2,1)}, u32[]{:S(2)}, u32[]{:S(2)}) collective-permute-start(bf16[8,32,2048]{2,1,0:T(8,128)(2,1)S(1)} %pad_maximum_fusion.3.refs_0_), channel_id=1, source_target_pairs={{0,1},{1,0},{2,3},{3,2},{4,5},{5,4},{6,7},{7,6},{8,9},{9,8},{10,11... | collective-permute-start | bytes 3145736 | tf_op jit(solution)/shard_map/ppermute | solution.py:630
  119.0 27.2 %collective-permute-start.23 = (bf16[8,32,2048]{2,1,0:T(8,128)(2,1)}, bf16[8,32,2048]{2,1,0:T(8,128)(2,1)}, u32[]{:S(2)}, u32[]{:S(2)}) collective-permute-start(bf16[8,32,2048]{2,1,0:T(8,128)(2,1)} %pad_maximum_fusion.4.refs_4_), channel_id=1, source_target_pairs={{0,1},{1,0},{2,3},{3,2},{4,5},{5,4},{6,7},{7,6},{8,9},{9,8},{10,11... | collective-permute-start | bytes 3145736 | tf_op jit(solution)/shard_map/ppermute | solution.py:630
  188.8 33.8 %collective-permute-start.27 = (bf16[8,32,2048]{2,1,0:T(8,128)(2,1)}, bf16[8,32,2048]{2,1,0:T(8,128)(2,1)}, u32[]{:S(2)}, u32[]{:S(2)}) collective-permute-start(bf16[8,32,2048]{2,1,0:T(8,128)(2,1)} %get-tuple-element.223), channel_id=1, source_target_pairs={{0,2},{1,3},{2,0},{3,1},{4,6},{5,7},{6,4},{7,5},{8,10},{9,11},{10,... | collective-permute-start | bytes 3145736 | tf_op jit(solution)/shard_map/ppermute | solution.py:630
  190.2 32.3 %collective-permute-start.28 = (bf16[8,32,2048]{2,1,0:T(8,128)(2,1)}, bf16[8,32,2048]{2,1,0:T(8,128)(2,1)}, u32[]{:S(2)}, u32[]{:S(2)}) collective-permute-start(bf16[8,32,2048]{2,1,0:T(8,128)(2,1)} %get-tuple-element.224), channel_id=1, source_target_pairs={{0,4},{1,5},{2,6},{3,7},{4,0},{5,1},{6,2},{7,3},{8,12},{9,13},{10,... | collective-permute-start | bytes 3145736 | tf_op jit(solution)/shard_map/ppermute | solution.py:630
  226.2 14.4 %collective-permute-start.29 = (bf16[4,32,2048]{2,1,0:T(8,128)(2,1)}, bf16[4,32,2048]{2,1,0:T(8,128)(2,1)S(1)}, u32[]{:S(2)}, u32[]{:S(2)}) collective-permute-start(bf16[4,32,2048]{2,1,0:T(8,128)(2,1)} %get-tuple-element.237), channel_id=1, source_target_pairs={{0,4},{1,5},{2,6},{3,7},{4,0},{5,1},{6,2},{7,3},{8,12},{9,13},{10,... | collective-permute-start | bytes 1572872 | tf_op jit(solution)/shard_map/ppermute | solution.py:630
  227.8 14.0 %collective-permute-start.30 = (bf16[4,32,2048]{2,1,0:T(8,128)(2,1)}, bf16[4,32,2048]{2,1,0:T(8,128)(2,1)S(1)}, u32[]{:S(2)}, u32[]{:S(2)}) collective-permute-start(bf16[4,32,2048]{2,1,0:T(8,128)(2,1)} %get-tuple-element.238), channel_id=1, source_target_pairs={{0,2},{1,3},{2,0},{3,1},{4,6},{5,7},{6,4},{7,5},{8,10},{9,11},{10,... | collective-permute-start | bytes 1572872 | tf_op jit(solution)/shard_map/ppermute | solution.py:630
  250.6 29.9 %collective-permute-start.33 = (bf16[2,32,4096]{2,1,0:T(8,128)(2,1)}, bf16[2,32,4096]{2,1,0:T(8,128)(2,1)}, u32[]{:S(2)}, u32[]{:S(2)}) collective-permute-start(bf16[2,32,4096]{2,1,0:T(8,128)(2,1)} %get-tuple-element.258), channel_id=1, source_target_pairs={{0,8},{1,9},{2,10},{3,11},{4,12},{5,13},{6,14},{7,15},{8,0},{9,1},... | collective-permute-start | bytes 1572872 | tf_op jit(solution)/shard_map/ppermute | solution.py:630
  252.1 28.4 %collective-permute-start.34 = (bf16[8,32,2048]{2,1,0:T(8,128)(2,1)}, bf16[8,32,2048]{2,1,0:T(8,128)(2,1)}, u32[]{:S(2)}, u32[]{:S(2)}) collective-permute-start(bf16[8,32,2048]{2,1,0:T(8,128)(2,1)} %get-tuple-element.259), channel_id=1, source_target_pairs={{0,2},{1,3},{2,0},{3,1},{4,6},{5,7},{6,4},{7,5},{8,10},{9,11},{10,... | collective-permute-start | bytes 3145736 | tf_op jit(solution)/shard_map/ppermute | solution.py:630
  252.7 27.9 %collective-permute-start.35 = (bf16[8,32,2048]{2,1,0:T(8,128)(2,1)}, bf16[8,32,2048]{2,1,0:T(8,128)(2,1)}, u32[]{:S(2)}, u32[]{:S(2)}) collective-permute-start(bf16[8,32,2048]{2,1,0:T(8,128)(2,1)} %get-tuple-element.260), channel_id=1, source_target_pairs={{0,4},{1,5},{2,6},{3,7},{4,0},{5,1},{6,2},{7,3},{8,12},{9,13},{10,... | collective-permute-start | bytes 3145736 | tf_op jit(solution)/shard_map/ppermute | solution.py:630
  286.0 16.5 %collective-permute-start.36 = (bf16[1,32,4096]{2,1,0:T(8,128)(2,1)S(1)}, bf16[1,32,4096]{2,1,0:T(8,128)(2,1)S(1)}, u32[]{:S(2)}, u32[]{:S(2)}) collective-permute-start(bf16[1,32,4096]{2,1,0:T(8,128)(2,1)S(1)} %copy-done.45), channel_id=1, source_target_pairs={{0,16},{1,17},{2,18},{3,19},{4,20},{5,21},{6,22},{7,23},{8,24},{9,... | collective-permute-start | bytes 786440 | tf_op jit(solution)/shard_map/ppermute | solution.py:630
  287.0 15.5 %collective-permute-start.37 = (bf16[4,32,2048]{2,1,0:T(8,128)(2,1)}, bf16[4,32,2048]{2,1,0:T(8,128)(2,1)S(1)}, u32[]{:S(2)}, u32[]{:S(2)}) collective-permute-start(bf16[4,32,2048]{2,1,0:T(8,128)(2,1)} %get-tuple-element.273), channel_id=1, source_target_pairs={{0,4},{1,5},{2,6},{3,7},{4,0},{5,1},{6,2},{7,3},{8,12},{9,13},{10,... | collective-permute-start | bytes 1572872 | tf_op jit(solution)/shard_map/ppermute | solution.py:630
  287.6 14.9 %collective-permute-start.38 = (bf16[4,32,2048]{2,1,0:T(8,128)(2,1)}, bf16[4,32,2048]{2,1,0:T(8,128)(2,1)S(1)}, u32[]{:S(2)}, u32[]{:S(2)}) collective-permute-start(bf16[4,32,2048]{2,1,0:T(8,128)(2,1)} %get-tuple-element.274), channel_id=1, source_target_pairs={{0,2},{1,3},{2,0},{3,1},{4,6},{5,7},{6,4},{7,5},{8,10},{9,11},{10,... | collective-permute-start | bytes 1572872 | tf_op jit(solution)/shard_map/ppermute | solution.py:630
  307.7 30.1 %collective-permute-start.41 = (bf16[2,32,4096]{2,1,0:T(8,128)(2,1)}, bf16[2,32,4096]{2,1,0:T(8,128)(2,1)S(1)}, u32[]{:S(2)}, u32[]{:S(2)}) collective-permute-start(bf16[2,32,4096]{2,1,0:T(8,128)(2,1)} %get-tuple-element.309), channel_id=1, source_target_pairs={{0,8},{1,9},{2,10},{3,11},{4,12},{5,13},{6,14},{7,15},{8,0},{9,1},... | collective-permute-start | bytes 1572872 | tf_op jit(solution)/shard_map/ppermute | solution.py:630
  314.6 25.5 %collective-permute-start.42 = (bf16[8,32,2048]{2,1,0:T(8,128)(2,1)}, bf16[8,32,2048]{2,1,0:T(8,128)(2,1)}, u32[]{:S(2)}, u32[]{:S(2)}) collective-permute-start(bf16[8,32,2048]{2,1,0:T(8,128)(2,1)} %get-tuple-element.310), channel_id=1, source_target_pairs={{0,2},{1,3},{2,0},{3,1},{4,6},{5,7},{6,4},{7,5},{8,10},{9,11},{10,... | collective-permute-start | bytes 3145736 | tf_op jit(solution)/shard_map/ppermute | solution.py:630
  315.2 25.2 %collective-permute-start.43 = (bf16[8,32,2048]{2,1,0:T(8,128)(2,1)}, bf16[8,32,2048]{2,1,0:T(8,128)(2,1)}, u32[]{:S(2)}, u32[]{:S(2)}) collective-permute-start(bf16[8,32,2048]{2,1,0:T(8,128)(2,1)} %get-tuple-element.311), channel_id=1, source_target_pairs={{0,4},{1,5},{2,6},{3,7},{4,0},{5,1},{6,2},{7,3},{8,12},{9,13},{10,... | collective-permute-start | bytes 3145736 | tf_op jit(solution)/shard_map/ppermute | solution.py:630
  334.3 33.9 %all-to-all-start.1 = ((bf16[32,2,3216]{2,1,0:T(2,128)(2,1)}), bf16[32,2,3216]{2,1,0:T(2,128)(2,1)S(1)}, u32[]{:S(2)}, u32[]{:S(2)}) async-start(bf16[32,2,3216]{2,1,0:T(2,128)(2,1)} %reshape.185), calls=%async_computation.1 | async-start | bytes 851968 | tf_op jit(solution)/shard_map/all_to_all | solution.py:987
  345.8 16.1 %collective-permute-start.45 = (bf16[4,32,2048]{2,1,0:T(8,128)(2,1)}, bf16[4,32,2048]{2,1,0:T(8,128)(2,1)S(1)}, u32[]{:S(2)}, u32[]{:S(2)}) collective-permute-start(bf16[4,32,2048]{2,1,0:T(8,128)(2,1)} %get-tuple-element.324), channel_id=1, source_target_pairs={{0,4},{1,5},{2,6},{3,7},{4,0},{5,1},{6,2},{7,3},{8,12},{9,13},{10,... | collective-permute-start | bytes 1572872 | tf_op jit(solution)/shard_map/ppermute | solution.py:630
  347.6 14.4 %collective-permute-start.46 = (bf16[4,32,2048]{2,1,0:T(8,128)(2,1)}, bf16[4,32,2048]{2,1,0:T(8,128)(2,1)S(1)}, u32[]{:S(2)}, u32[]{:S(2)}) collective-permute-start(bf16[4,32,2048]{2,1,0:T(8,128)(2,1)} %get-tuple-element.325), channel_id=1, source_target_pairs={{0,2},{1,3},{2,0},{3,1},{4,6},{5,7},{6,4},{7,5},{8,10},{9,11},{10,... | collective-permute-start | bytes 1572872 | tf_op jit(solution)/shard_map/ppermute | solution.py:630
  348.0 14.0 %collective-permute-start.44 = (bf16[1,32,4096]{2,1,0:T(8,128)(2,1)S(1)}, bf16[1,32,4096]{2,1,0:T(8,128)(2,1)S(1)}, u32[]{:S(2)}, u32[]{:S(2)}) collective-permute-start(bf16[1,32,4096]{2,1,0:T(8,128)(2,1)S(1)} %copy-done.47), channel_id=1, source_target_pairs={{0,16},{1,17},{2,18},{3,19},{4,20},{5,21},{6,22},{7,23},{8,24},{9,... | collective-permute-start | bytes 786440 | tf_op jit(solution)/shard_map/ppermute | solution.py:630
  383.0 14.7 %collective-permute-start.48 = (bf16[1,32,4096]{2,1,0:T(8,128)(2,1)}, bf16[1,32,4096]{2,1,0:T(8,128)(2,1)S(1)}, u32[]{:S(2)}, u32[]{:S(2)}) collective-permute-start(bf16[1,32,4096]{2,1,0:T(8,128)(2,1)} %get-tuple-element.346), channel_id=1, source_target_pairs={{0,16},{1,17},{2,18},{3,19},{4,20},{5,21},{6,22},{7,23},{8,24},{9,... | collective-permute-start | bytes 786440 | tf_op jit(solution)/shard_map/ppermute | solution.py:630
  (71 other events, 621.3 us)
Sparse Core Ops, SparseCore 0:
  116.0 78.1 all-gather.1
